TPU v7x, 32 devices: a whole 2x2x4 slice. The times are simulated.
32 devices in a mesh: rep: 4 (over y, x), fsdp: 8 (over z, core).
Axes of the slice: x: 2, y: 2, z: 4, core: 2. Of those that a mesh axis runs over, the one named last changes fastest.
Arguments:
- tokens: bfloat16 [4, 1024, 2048], P('rep', 'fsdp'), may hold values from -6 to 6
- lengths: int32 [4], P('rep'), may hold values from 1024 to 1024, as said below
- cotangent: bfloat16 [4, 1024, 2048], P('rep', 'fsdp'), may hold values from -6 to 6
- w_qkv: bfloat16 [2048, 6144], P('fsdp'), may hold values from -0.125 to 0.125
- w_out: bfloat16 [2048, 2048], P('fsdp'), may hold values from -2 to 2
- w_in: bfloat16 [2048, 16384], P('fsdp'), may hold values from -0.125 to 0.125
- w_down: bfloat16 [8192, 2048], P('fsdp'), may hold values from -0.0625 to 0.0625
Outputs:
- output: bfloat16 [4, 1024, 2048], P('rep', 'fsdp')
- grad_tokens: bfloat16 [4, 1024, 2048], P('rep', 'fsdp')
- grad_qkv: float32 [2048, 6144], P('fsdp')
- grad_out: float32 [2048, 2048], P('fsdp')
- grad_in: float32 [2048, 16384], P('fsdp')
- grad_down: float32 [8192, 2048], P('fsdp')
Inputs may be any that keep to these rules, and one draw needn't show every extreme that they name: Slot s holds one sequence in its first lengths[s] rows. In every draw one slot is full (1024) and another holds exactly 1024.
All inputs are finite; a program needn't handle non-finite values.
Results may differ from a plain program's by a relative error of at most 0.018.
Values may be sent and summed in bfloat16 or wider, within the bound.
A program may use at most 384 MiB of HBM per device.

v0:
```python
import jax
import jax.numpy as jnp
from jax import lax
from jax.sharding import PartitionSpec as P

HEADS = 16
HEAD_DIM = 128


eps = 1e-05
neg_big = -1e30


def normalize(rows):
    centred = rows - jnp.mean(rows, axis=-1, keepdims=True)
    inv_std = lax.rsqrt(jnp.mean(centred * centred, axis=-1, keepdims=True) + eps)
    return (centred * inv_std, inv_std)


def norm_back(normed, inv_std, grad):
    return inv_std * (
        grad
        - jnp.mean(grad, axis=-1, keepdims=True)
        - normed * jnp.mean(grad * normed, axis=-1, keepdims=True)
    )


def rotary_tables(positions, head_dim):
    half = head_dim // 2
    freqs = 10000.0 ** (-jnp.arange(half, dtype=jnp.float32) * 2.0 / head_dim)
    angles = positions.astype(jnp.float32)[:, None] * freqs[None, :]
    return (jnp.cos(angles), jnp.sin(angles))


def rotate(values, cosine, sine):
    half = values.shape[-1] // 2
    first = values[..., :half]
    second = values[..., half:]
    cosine = cosine[:, None, :]
    sine = sine[:, None, :]
    return jnp.concatenate(
        [first * cosine - second * sine, second * cosine + first * sine], axis=-1
    )


def rotate_back(grads, cosine, sine):
    half = grads.shape[-1] // 2
    first = grads[..., :half]
    second = grads[..., half:]
    cosine = cosine[:, None, :]
    sine = sine[:, None, :]
    return jnp.concatenate(
        [first * cosine + second * sine, second * cosine - first * sine], axis=-1
    )


def times_transpose(left, weight):
    return lax.dot_general(
        left, weight, (((1,), (1,)), ((), ())), preferred_element_type=jnp.float32
    )


def over_rows(left, right):
    return lax.dot_general(
        left, right, (((0,), (0,)), ((), ())), preferred_element_type=jnp.float32
    )


def masked_scores(query, keys, key_pos, query_pos, length, scale):
    raw = jnp.einsum("qhd,khd->hqk", query, keys, preferred_element_type=jnp.float32) * scale
    allowed = (key_pos[None, :] <= query_pos[:, None]) & (key_pos[None, :] < length)
    return jnp.where(allowed[None], raw, neg_big)


def on_device(tokens, lengths, cotangent, w_qkv, w_out, w_in, w_down):
    rows = tokens.shape[1]
    width = tokens.shape[2]
    units = w_in.shape[1] // 2
    heads = HEADS
    head_dim = HEAD_DIM
    slot_len = rows * lax.axis_size("fsdp")
    block = min(512, slot_len)
    count_blocks = slot_len // block
    scale = head_dim ** (-0.5)
    length = lengths[0]
    positions = lax.axis_index("fsdp") * rows + jnp.arange(rows, dtype=jnp.int32)
    valid = (positions < length).astype(jnp.float32)[:, None]
    cosine, sine = rotary_tables(positions, head_dim)
    full_qkv, full_out, full_in, full_down = (
        lax.all_gather(w_qkv, "fsdp", axis=0, tiled=True),
        lax.all_gather(w_out, "fsdp", axis=0, tiled=True),
        lax.all_gather(w_in, "fsdp", axis=0, tiled=True),
        lax.all_gather(w_down, "fsdp", axis=0, tiled=True),
    )
    x_rows = tokens[0].astype(jnp.float32)
    normed1, inv1 = normalize(x_rows)
    n1_low = normed1.astype(jnp.bfloat16)
    qkv = jnp.dot(n1_low, full_qkv, preferred_element_type=jnp.float32)
    query = rotate(qkv[:, :width].reshape(rows, heads, head_dim), cosine, sine).astype(jnp.bfloat16)
    keys_own = rotate(
        qkv[:, width : 2 * width].reshape(rows, heads, head_dim), cosine, sine
    ).astype(jnp.bfloat16)
    values_own = qkv[:, 2 * width :].astype(jnp.bfloat16)
    all_keys, all_values = (
        lax.all_gather(keys_own.reshape(rows, width), "fsdp", axis=0, tiled=True),
        lax.all_gather(values_own, "fsdp", axis=0, tiled=True),
    )

    def key_block(index):
        start = index * block
        keys = lax.dynamic_slice_in_dim(all_keys, start, block, 0).reshape(block, heads, head_dim)
        values = lax.dynamic_slice_in_dim(all_values, start, block, 0).reshape(
            block, heads, head_dim
        )
        key_pos = start + jnp.arange(block, dtype=jnp.int32)
        return (start, key_pos, keys, values)

    def stats_step(index, carry):
        top, total = carry
        start, key_pos, keys, values = key_block(index)
        scores = masked_scores(query, keys, key_pos, positions, length, scale)
        new_top = jnp.maximum(top, jnp.max(scores, axis=-1))
        total = total * jnp.exp(top - new_top) + jnp.sum(
            jnp.exp(scores - new_top[..., None]), axis=-1
        )
        return (new_top, total)

    top0 = jnp.full((heads, rows), neg_big, jnp.float32)
    top, total = lax.fori_loop(
        0, count_blocks, stats_step, (top0, jnp.zeros((heads, rows), jnp.float32))
    )
    log_total = top + jnp.log(total)

    def value_step(index, acc):
        start, key_pos, keys, values = key_block(index)
        scores = masked_scores(query, keys, key_pos, positions, length, scale)
        probs = jnp.exp(scores - log_total[..., None]).astype(jnp.bfloat16)
        return acc + jnp.einsum("hqk,khd->qhd", probs, values, preferred_element_type=jnp.float32)

    attended = lax.fori_loop(
        0, count_blocks, value_step, jnp.zeros((rows, heads, head_dim), jnp.float32)
    )
    attended = attended.reshape(rows, width)
    att_low = attended.astype(jnp.bfloat16)
    hidden_in = x_rows + jnp.dot(att_low, full_out, preferred_element_type=jnp.float32)
    normed2, inv2 = normalize(hidden_in)
    n2_low = normed2.astype(jnp.bfloat16)
    gate_up = jnp.dot(n2_low, full_in, preferred_element_type=jnp.float32)
    gate = gate_up[:, :units]
    upper = gate_up[:, units:]
    sigma = jax.nn.sigmoid(gate)
    silu_gate = gate * sigma
    act_low = (silu_gate * upper).astype(jnp.bfloat16)
    branch = jnp.dot(act_low, full_down, preferred_element_type=jnp.float32)
    output = (valid * (hidden_in + branch)).astype(jnp.bfloat16)
    back_qkv, back_out, back_in, back_down = (full_qkv, full_out, full_in, full_down)
    n1_cols, n2_cols, att_cols, act_cols = (
        lax.all_to_all(n1_low, "fsdp", split_axis=1, concat_axis=0, tiled=True),
        lax.all_to_all(n2_low, "fsdp", split_axis=1, concat_axis=0, tiled=True),
        lax.all_to_all(att_low, "fsdp", split_axis=1, concat_axis=0, tiled=True),
        lax.all_to_all(act_low, "fsdp", split_axis=1, concat_axis=0, tiled=True),
    )
    dy_rows = valid * cotangent[0].astype(jnp.float32)
    dy_low = dy_rows.astype(jnp.bfloat16)
    d_hidden = times_transpose(dy_low, back_down)
    d_gate = d_hidden * upper * sigma * (1.0 + gate * (1.0 - sigma))
    d_up = d_hidden * silu_gate
    dgu_low = jnp.concatenate([d_gate, d_up], axis=1).astype(jnp.bfloat16)
    d_norm2 = times_transpose(dgu_low, back_in)
    d_resid = dy_rows + norm_back(normed2, inv2, d_norm2)
    dres_low = d_resid.astype(jnp.bfloat16)
    dy_piece = lax.all_gather(dy_low, "fsdp", axis=0, tiled=True)
    dgu_piece = lax.all_gather(dgu_low, "fsdp", axis=0, tiled=True)
    dres_piece = lax.all_gather(dres_low, "fsdp", axis=0, tiled=True)
    grad_down = over_rows(act_cols, dy_piece)
    grad_in = over_rows(n2_cols, dgu_piece)
    grad_out = over_rows(att_cols, dres_piece)
    d_att = times_transpose(dres_low, back_out)
    datt_low = d_att.astype(jnp.bfloat16).reshape(rows, heads, head_dim)
    delta = jnp.sum(
        datt_low.astype(jnp.float32) * attended.reshape(rows, heads, head_dim), axis=-1
    ).T

    def grad_step(index, carry):
        dq_acc, dk_buf, dv_buf = carry
        start, key_pos, keys, values = key_block(index)
        scores = masked_scores(query, keys, key_pos, positions, length, scale)
        probs = jnp.exp(scores - log_total[..., None])
        probs_low = probs.astype(jnp.bfloat16)
        d_probs = jnp.einsum("qhd,khd->hqk", datt_low, values, preferred_element_type=jnp.float32)
        d_scores = (probs * (d_probs - delta[..., None])).astype(jnp.bfloat16)
        dq_acc = dq_acc + jnp.einsum(
            "hqk,khd->qhd", d_scores, keys, preferred_element_type=jnp.float32
        )
        dk_block = (
            jnp.einsum("hqk,qhd->khd", d_scores, query, preferred_element_type=jnp.float32) * scale
        )
        dv_block = jnp.einsum(
            "hqk,qhd->khd", probs_low, datt_low, preferred_element_type=jnp.float32
        )
        dk_buf = lax.dynamic_update_slice_in_dim(dk_buf, dk_block.reshape(block, width), start, 0)
        dv_buf = lax.dynamic_update_slice_in_dim(dv_buf, dv_block.reshape(block, width), start, 0)
        return (dq_acc, dk_buf, dv_buf)

    empty_keys = jnp.zeros((slot_len, width), jnp.float32)
    dq_acc, dk_buf, dv_buf = lax.fori_loop(
        0,
        count_blocks,
        grad_step,
        (jnp.zeros((rows, heads, head_dim), jnp.float32), empty_keys, empty_keys),
    )
    dk_own, dv_own = (
        lax.psum_scatter(
            dk_buf.astype(jnp.bfloat16), "fsdp", scatter_dimension=0, tiled=True
        ).astype(jnp.float32),
        lax.psum_scatter(
            dv_buf.astype(jnp.bfloat16), "fsdp", scatter_dimension=0, tiled=True
        ).astype(jnp.float32),
    )
    dq_turned = rotate_back(dq_acc * scale, cosine, sine).reshape(rows, width)
    dk_turned = rotate_back(dk_own.reshape(rows, heads, head_dim), cosine, sine).reshape(
        rows, width
    )
    dqkv_low = jnp.concatenate([dq_turned, dk_turned, dv_own], axis=1).astype(jnp.bfloat16)
    grad_qkv = over_rows(n1_cols, lax.all_gather(dqkv_low, "fsdp", axis=0, tiled=True))
    d_norm1 = times_transpose(dqkv_low, back_qkv)
    grad_tokens = (d_resid + norm_back(normed1, inv1, d_norm1)).astype(jnp.bfloat16)
    grad_qkv, grad_out, grad_in, grad_down = (
        lax.psum(grad_qkv.astype(jnp.bfloat16), "rep").astype(jnp.float32),
        lax.psum(grad_out.astype(jnp.bfloat16), "rep").astype(jnp.float32),
        lax.psum(grad_in.astype(jnp.bfloat16), "rep").astype(jnp.float32),
        lax.psum(grad_down.astype(jnp.bfloat16), "rep").astype(jnp.float32),
    )
    return (output[None], grad_tokens[None], grad_qkv, grad_out, grad_in, grad_down)


def solution(mesh):
    in_specs = (
        P("rep", "fsdp", None),
        P("rep"),
        P("rep", "fsdp", None),
        P("fsdp", None),
        P("fsdp", None),
        P("fsdp", None),
        P("fsdp", None),
    )
    out_specs = (
        P("rep", "fsdp", None),
        P("rep", "fsdp", None),
        P("fsdp", None),
        P("fsdp", None),
        P("fsdp", None),
        P("fsdp", None),
    )
    return jax.shard_map(
        on_device, mesh=mesh, in_specs=in_specs, out_specs=out_specs, check_vma=False
    )
```

profile of v0, /device:TPU:8, one launch (start us, length us, event | category | flops | bytes accessed | tf_op | source)
XLA Modules:
  0.0 2416.1 jit_solution(10049363850367072238)
XLA Ops:
  10.5 217.2 %all-gather.11.cloned.1.call-done = bf16[2048,6144]{1,0:T(8,128)(2,1)} async-done(((bf16[256,6144]{1,0:T(8,128)(2,1)}), bf16[2048,6144]{1,0:T(8,128)(2,1)}) %all-gather.11.cloned.1.call-update) | async-done | bytes 25165840 | tf_op jit(solution)/shard_map/all_gather | solution.py:90
  227.7 10.1 fusion.38
  240.7 2.7 fusion.50
  251.9 35.4 %all-gather.13.cloned.1.call-done = bf16[1024,2048]{1,0:T(8,128)(2,1)} async-done(((bf16[128,2048]{1,0:T(8,128)(2,1)}), bf16[1024,2048]{1,0:T(8,128)(2,1)}) %all-gather.13.cloned.1.call-update) | async-done | bytes 4194320 | tf_op jit(solution)/shard_map/all_gather | solution.py:106
  287.3 6.4 copy.126
  293.7 40.8 %all-gather.15.cloned.1.call-done = bf16[1024,2048]{0,1:T(8,128)(2,1)} async-done(((bf16[128,2048]{0,1:T(8,128)(2,1)}), bf16[1024,2048]{0,1:T(8,128)(2,1)}) %all-gather.15.cloned.1.call-update) | async-done | bytes 4194320 | tf_op jit(solution)/shard_map/all_gather | solution.py:105
  334.5 19.9 while.48
  337.1 4.1 fusion.113
  341.2 3.0 exponential_reduce_fusion.2
  347.1 4.2 fusion.113
  351.3 3.0 exponential_reduce_fusion.2
  354.4 18.9 while.49
  354.4 3.8 constant_dynamic-slice_fusion.10
  359.1 4.5 fusion.118
  363.6 4.0 constant_dynamic-slice_fusion.10
  368.4 4.8 fusion.118
  375.4 41.1 %all-gather.17.cloned.1.call-done = bf16[2048,2048]{1,0:T(8,128)(2,1)} async-done(((bf16[256,2048]{1,0:T(8,128)(2,1)}), bf16[2048,2048]{1,0:T(8,128)(2,1)}) %all-gather.17.cloned.1.call-update) | async-done | bytes 8388624 | tf_op jit(solution)/shard_map/all_gather | solution.py:91
  416.4 4.9 fusion.51
  421.8 558.2 %all-gather.19.cloned.1.call-done = bf16[2048,16384]{1,0:T(8,128)(2,1)} async-done(((bf16[256,16384]{1,0:T(8,128)(2,1)}), bf16[2048,16384]{1,0:T(8,128)(2,1)}) %all-gather.19.cloned.1.call-update) | async-done | bytes 67108880 | tf_op jit(solution)/shard_map/all_gather | solution.py:92
  980.1 31.8 %fusion.53 = f32[128,16384]{1,0:T(8,128)} fusion(bf16[128,2048]{1,0:T(8,128)(2,1)S(1)} %fusion.37, bf16[2048,16384]{1,0:T(8,128)(2,1)} %all-gather.19.cloned.1.call-done), kind=kOutput, calls=%fused_computation.130 | convolution fusion | flops 8589934592 | bytes 76021760 | tf_op jit(solution)/shard_map/dot_general | solution.py:148
  1011.9 256.5 %all-gather.21.cloned.1.call-done = bf16[8192,2048]{1,0:T(8,128)(2,1)} async-done(((bf16[1024,2048]{1,0:T(8,128)(2,1)}), bf16[8192,2048]{1,0:T(8,128)(2,1)}) %all-gather.21.cloned.1.call-update) | async-done | bytes 33554448 | tf_op jit(solution)/shard_map/all_gather | solution.py:93
  1268.4 21.2 multiply_convert_fusion.1
  1289.6 29.9 %fusion.47 = (f32[128]{0:T(128)S(1)}, f32[128]{0:T(128)S(1)}, f32[128,2048]{1,0:T(8,128)}) fusion(f32[128]{0:T(128)S(1)} %add_rsqrt_fusion, f32[128,2048]{1,0:T(8,128)S(1)} %get-tuple-element.801, f32[128]{0:T(128)S(1)} %broadcast_multiply_fusion.5, bf16[2048,16384]{1,0:T(8,128)(2,1)} %all-gather.19.cloned.1.call-done, ...), kind=kOutput, calls=%fused_computation.125 | convolution fusion | flops 8599633920 | bytes 73402368 | tf_op jit(solution)/shard_map/dot_general | solution.py:58
  1319.5 2.7 fusion.48
  1322.2 7.3 convolution_convert_fusion.4
  1331.0 2.5 broadcast_in_dim.149
  1333.5 2.5 broadcast_in_dim.149.clone
  1336.1 53.5 %while.50 = (s32[]{:T(128)}, f32[128,16,128]{0,2,1:T(8,128)}, bf16[1024,2048]{0,1:T(8,128)(2,1)}, bf16[1024,2048]{0,1:T(8,128)(2,1)}, bf16[1024,2048]{0,1:T(8,12...) while((s32[]{:T(128)}, f32[128,16,128]{0,2,1:T(8,128)}, ...), condition=%wide.region_14.15_spmd.clone, body=%wide.region_13.14_spmd.clone.sunk | while | flops 1355417216 | bytes 117668240 | solution.py:206
  1339.6 2.5 copy-done.1
  1343.3 4.2 fusion.130
  1347.4 3.4 fusion.131
  1350.9 4.0 fusion.132
  1355.6 2.6 copy.166
  1358.3 4.6 constant_dynamic-update-slice_fusion.3
  1366.1 2.5 copy-done.1
  1369.8 4.2 fusion.130
  1374.0 3.7 fusion.131
  1377.7 4.0 fusion.132
  1382.4 2.6 copy.166
  1385.0 4.6 constant_dynamic-update-slice_fusion.3
  1389.6 6.5 copy.146
  1396.2 6.4 copy.148
  1404.2 39.7 %reduce-scatter.7.cloned.1.call-done = bf16[128,2048]{1,0:T(8,128)(2,1)} async-done(((bf16[1024,2048]{1,0:T(8,128)(2,1)}), bf16[128,2048]{1,0:T(8,128)(2,1)}) %reduce-scatter.7.cloned.1.call-update) | async-done | bytes 524304
  1445.3 49.9 %reduce-scatter.9.cloned.1.call-done = bf16[128,2048]{1,0:T(8,128)(2,1)} async-done(((bf16[1024,2048]{1,0:T(8,128)(2,1)}), bf16[128,2048]{1,0:T(8,128)(2,1)}) %reduce-scatter.9.cloned.1.call-update) | async-done | bytes 524304
  1499.1 3.9 pad_maximum_fusion
  1503.1 7.5 all-to-all-start.1
  1510.6 3.2 copy.163
  1513.8 21.7 all-to-all-done.1
  1535.5 8.9 all-to-all-start.3
  1546.7 78.9 %all-to-all-done.3 = bf16[128,8,1024]{2,0,1:T(8,128)(2,1)} async-done(((bf16[128,8,1024]{2,0,1:T(8,128)(2,1)}), bf16[128,8,1024]{2,0,1:T(8,128)(2,1)}, u32[]{:S(2)}, u32[]{:S(2)}) %all-to-all-start.3) | async-done | bytes 2097184 | tf_op jit(solution)/shard_map/all_to_all | solution.py:161
  1625.6 8.5 all-to-all-start
  1634.1 9.4 convolution_convert_fusion.2
  1643.6 5.0 convolution_convert_fusion.3
  1648.5 5.1 all-to-all-start.2
  1653.7 112.9 %all-gather.23.cloned.1.call-done = bf16[1024,6144]{0,1:T(8,128)(2,1)} async-done(((bf16[128,6144]{0,1:T(8,128)(2,1)}), bf16[1024,6144]{0,1:T(8,128)(2,1)}) %all-gather.23.cloned.1.call-update) | async-done | bytes 12582928 | tf_op jit(solution)/shard_map/all_gather | solution.py:225
  1766.6 14.4 convolution_convert_fusion.1
  1781.0 274.1 %all-gather.27.cloned.1.call-done = bf16[1024,16384]{1,0:T(8,128)(2,1)} async-done(((bf16[128,16384]{1,0:T(8,128)(2,1)}), bf16[1024,16384]{1,0:T(8,128)(2,1)}) %all-gather.27.cloned.1.call-update) | async-done | bytes 33554448 | tf_op jit(solution)/shard_map/all_gather | solution.py:173
  2055.1 22.4 convolution_convert_fusion
  2078.7 17.7 fusion.30
  2096.5 21.2 fusion.46
  2120.1 266.1 %all-reduce.3.cloned.1.call-done = (bf16[256,6144]{1,0:T(8,128)(2,1)}, bf16[256,2048]{1,0:T(8,128)(2,1)}, bf16[256,16384]{1,0:T(8,128)(2,1)}, bf16[1024,2048]{1,0:T(8,128)(2,1)}) async-done(((bf16[256,6144]{1,0:T(8,128)(2,1)}, bf16[256,2048]{1,0:T(8,128)(2,1)}, bf16[256,16384]{1,0:T(8,128)(2,1)}, bf16[1024,2048]{1,0:T(8,128)(2,1)}), (bf16[256,6144]{1,0:T(8,128)(2,1)}, bf16[256,2048]{1,0:T(8,128)(2,1)}, ...) | async-done | bytes 16777232 | tf_op jit(solution)/shard_map/psum | solution.py:229
  2386.2 5.4 convert_element_type.158
  2393.2 11.7 convert_element_type.163
  2404.9 4.4 convert_element_type.165
  (197 shorter events, 49.6 us)
Async XLA Ops:
  7.2 220.5 %copy-start.7 = (bf16[1,128,2048]{2,1,0:T(8,128)(2,1)S(1)}, bf16[1,128,2048]{2,1,0:T(8,128)(2,1)}, u32[]{:S(2)}) copy-start(bf16[1,128,2048]{2,1,0:T(8,128)(2,1)} %param.13) | copy-start | bytes 1572868
  7.2 220.5 %all-gather.11.cloned.1.call-start = ((), (), s32[]{:S(2)}) async-start(), calls=%async_computation.6 | async-start | bytes 28311552 | tf_op jit(solution)/shard_map/all_gather | solution.py:90
  7.9 279.4 %all-gather.13.cloned.1.call-start = ((), (), s32[]{:S(2)}) async-start(), calls=%async_computation.7 | async-start | bytes 4718592 | tf_op jit(solution)/shard_map/all_gather | solution.py:106
  9.2 228.7 %copy-start.32 = (f32[128]{0:T(128)}, f32[128]{0:T(128)S(1)}, u32[]{:S(2)}) copy-start(f32[128]{0:T(128)S(1)} %broadcast_multiply_fusion.6) | copy-start | bytes 1540
  10.5 227.3 %copy-start.34 = (f32[128]{0:T(128)}, f32[128]{0:T(128)S(1)}, u32[]{:S(2)}) copy-start(f32[128]{0:T(128)S(1)} %add_rsqrt_fusion.1) | copy-start | bytes 1540
  237.9 1.7 copy-start.9
  240.4 94.1 %all-gather.15.cloned.1.call-start = ((), (), s32[]{:S(2)}) async-start(), calls=%async_computation.8 | async-start | bytes 4718592 | tf_op jit(solution)/shard_map/all_gather | solution.py:105
  240.7 4.6 copy-start.28
  240.7 4.6 copy-start.30
  247.2 169.2 %all-gather.17.cloned.1.call-start = ((), (), s32[]{:S(2)}) async-start(), calls=%async_computation.9 | async-start | bytes 9437184 | tf_op jit(solution)/shard_map/all_gather | solution.py:91
  247.8 732.3 %all-gather.19.cloned.1.call-start = ((), (), s32[]{:S(2)}) async-start(), calls=%async_computation.10 | async-start | bytes 75497472 | tf_op jit(solution)/shard_map/all_gather | solution.py:92
  248.4 1.5 copy-start.24
  248.4 2.5 copy-start.27
  248.4 1020.0 %all-gather.21.cloned.1.call-start = ((), (), s32[]{:S(2)}) async-start(), calls=%async_computation.11 | async-start | bytes 37748736 | tf_op jit(solution)/shard_map/all_gather | solution.py:93
  249.0 1194.8 %reduce-scatter.7.cloned.1.call-start = ((), (), s32[]{:S(2)}) async-start(), calls=%async_computation.16 | async-start | bytes 4718592
  421.4 898.1 %copy-start.4 = (f32[128,2048]{1,0:T(8,128)}, f32[128,2048]{1,0:T(8,128)S(1)}, u32[]{:S(2)}) copy-start(f32[128,2048]{1,0:T(8,128)S(1)} %get-tuple-element.801) | copy-start | bytes 3145732
  421.8 846.5 %copy-start.17 = (bf16[128,2048]{1,0:T(8,128)(2,1)S(1)}, bf16[128,2048]{1,0:T(8,128)(2,1)}, u32[]{:S(2)}) copy-start(bf16[128,2048]{1,0:T(8,128)(2,1)} %fusion.32) | copy-start | bytes 1572868
  1289.6 29.9 %copy-start.25 = (bf16[1,128,2048]{2,1,0:T(8,128)(2,1)S(1)}, bf16[1,128,2048]{2,1,0:T(8,128)(2,1)}, u32[]{:S(2)}) copy-start(bf16[1,128,2048]{2,1,0:T(8,128)(2,1)} %param.15) | copy-start | bytes 1572868
  1322.2 7.3 copy-start.11
  1322.2 8.6 copy-start.13
  1336.3 0.8 copy-start.15
  1338.8 3.3 copy-start.1
  1339.6 7.8 copy-start.2
  1347.4 3.4 copy-start.3
  1350.9 4.0 copy-start
  1358.3 4.6 copy-start.16
  1362.8 0.8 copy-start.15
  1365.3 3.3 copy-start.1
  1366.1 7.8 copy-start.2
  1374.0 3.7 copy-start.3
  1377.7 4.0 copy-start
  1385.0 4.6 copy-start.16
  1396.1 99.0 %reduce-scatter.9.cloned.1.call-start = ((), (), s32[]{:S(2)}) async-start(), calls=%async_computation.17 | async-start | bytes 4718592
  1402.6 1.4 copy-start.6
  1402.7 93.8 %copy-start.29 = (f32[128,64]{0,1:T(8,128)S(1)}, f32[128,64]{0,1:T(8,128)}, u32[]{:S(2)}) copy-start(f32[128,64]{0,1:T(8,128)} %copy-done.28) | copy-start | bytes 98308
  1402.7 93.8 %copy-start.31 = (f32[128,64]{0,1:T(8,128)S(1)}, f32[128,64]{0,1:T(8,128)}, u32[]{:S(2)}) copy-start(f32[128,64]{0,1:T(8,128)} %copy-done.30) | copy-start | bytes 98308
  1402.7 231.5 %all-gather.29.cloned.1.call-start = ((), (), s32[]{:S(2)}) async-start(), calls=%async_computation.15 | async-start | bytes 4718592 | tf_op jit(solution)/shard_map/all_gather | solution.py:172
  1403.4 240.1 %all-gather.25.cloned.1.call-start = ((), (), s32[]{:S(2)}) async-start(), calls=%async_computation.13 | async-start | bytes 4718592 | tf_op jit(solution)/shard_map/all_gather | solution.py:174
  1404.0 362.6 %all-gather.23.cloned.1.call-start = ((), (), s32[]{:S(2)}) async-start(), calls=%async_computation.12 | async-start | bytes 14155776 | tf_op jit(solution)/shard_map/all_gather | solution.py:225
  1496.5 2.6 copy-start.18
  1496.8 2.3 copy-start.10
  1496.8 0.8 copy-start.20
  1496.9 0.9 copy-start.22
  1499.1 556.0 %all-gather.27.cloned.1.call-start = ((), (), s32[]{:S(2)}) async-start(), calls=%async_computation.14 | async-start | bytes 37748736 | tf_op jit(solution)/shard_map/all_gather | solution.py:173
  1503.1 32.4 %all-to-all-start.1 = ((bf16[128,8,256]{0,2,1:T(8,128)(2,1)}), bf16[128,8,256]{0,2,1:T(8,128)(2,1)S(1)}, u32[]{:S(2)}, u32[]{:S(2)}) async-start(bf16[128,8,256]{0,2,1:T(8,128)(2,1)} %bitcast.14), calls=%async_computation.1 | async-start | bytes 1048576 | tf_op jit(solution)/shard_map/all_to_all | solution.py:160
  1510.6 33.8 %copy-start.8 = (bf16[1,128,2048]{2,1,0:T(8,128)(2,1)S(1)}, bf16[1,128,2048]{2,1,0:T(8,128)(2,1)}, u32[]{:S(2)}) copy-start(bf16[1,128,2048]{2,1,0:T(8,128)(2,1)} %param.13) | copy-start | bytes 1572868
  1510.6 33.9 %copy-start.33 = (f32[128]{0:T(128)S(1)}, f32[128]{0:T(128)}, u32[]{:S(2)}) copy-start(f32[128]{0:T(128)} %copy-done.32) | copy-start | bytes 1540
  1510.6 33.9 %copy-start.35 = (f32[128]{0:T(128)S(1)}, f32[128]{0:T(128)}, u32[]{:S(2)}) copy-start(f32[128]{0:T(128)} %copy-done.34) | copy-start | bytes 1540
  1535.5 90.1 %all-to-all-start.3 = ((bf16[128,8,1024]{2,0,1:T(8,128)(2,1)}), bf16[128,8,1024]{2,0,1:T(8,128)(2,1)}, u32[]{:S(2)}, u32[]{:S(2)}) async-start(bf16[128,8,1024]{2,0,1:T(8,128)(2,1)} %bitcast.219), calls=%async_computation.3 | async-start | bytes 4194304 | tf_op jit(solution)/shard_map/all_to_all | solution.py:161
  1625.6 22.9 all-to-all-start
  1648.5 132.4 %all-to-all-start.2 = ((bf16[128,8,256]{2,0,1:T(8,128)(2,1)}), bf16[128,8,256]{2,0,1:T(8,128)(2,1)S(1)}, u32[]{:S(2)}, u32[]{:S(2)}) async-start(bf16[128,8,256]{2,0,1:T(8,128)(2,1)} %bitcast.147), calls=%async_computation.2 | async-start | bytes 1048576 | tf_op jit(solution)/shard_map/all_to_all | solution.py:159
  1653.7 732.5 %all-reduce.3.cloned.1.call-start = ((), (), s32[]{:S(2)}) async-start(), calls=%async_computation.18 | async-start | bytes 33554432 | tf_op jit(solution)/shard_map/psum | solution.py:229
  2077.5 1.2 copy-start.5
  2078.7 17.7 copy-start.19
  2078.7 17.7 copy-start.21
  2078.7 17.7 copy-start.23
  2096.5 21.2 copy-start.14
  2386.2 5.4 copy-start.26
  2393.2 11.7 copy-start.12
Sparse Core Ops, SparseCore 0:
  9.6 218.0 all-gather.10
  240.5 46.7 all-gather.12
  289.5 44.9 all-gather.14
  335.9 80.4 all-gather.16
  417.9 562.1 all-gather.18
  981.5 286.7 all-gather.20
  1396.3 47.5 reduce-scatter.6
  1446.7 48.3 reduce-scatter.8
  1496.7 73.6 all-gather.28
  1571.8 59.9 all-gather.24
  1634.0 132.5 all-gather.22
  1768.6 286.4 all-gather.26
  2077.7 308.5 all-reduce.2
where the time goes:
time: 2420 us
  waiting for transfers between devices  2000 us (83%)
  matrix products  239 us (10%)
  local copies, waits for them, and re-layouts  79.4 us (3%)
  other arithmetic  54.8 us (2%)
  starting transfers between devices  30.7 us (1%)
    all_gather x1, waiting for transfers between devices, on_device(): lax.all_gather(w_in, 'fsdp', axis=0, tiled=True)  558 us
    all_gather x1, waiting for transfers between devices, on_device(): dgu_piece = lax.all_gather(dgu_low, 'fsdp', axis=0, tiled=True)  274 us
    psum x1, waiting for transfers between devices, on_device(): lax.psum(grad_qkv.astype(jnp.bfloat16), 'rep').astype(jnp.float32)  266 us
    all_gather x1, waiting for transfers between devices, on_device(): lax.all_gather(w_down, 'fsdp', axis=0, tiled=True)  256 us
    all_gather x1, waiting for transfers between devices, on_device(): lax.all_gather(w_qkv, 'fsdp', axis=0, tiled=True)  217 us
    all_gather x1, waiting for transfers between devices, on_device(): lax.all_gather(dqkv_low, 'fsdp', axis=0, tiled=True)  113 us
    unnamed x15, waiting for transfers between devices  93.1 us
    dot_general x4, matrix products, times_transpose(): lax.dot_general(left, weight, (((1,), (1,)), ((), ())), preferred_element...  79.6 us
  transfers between devices with their start and end apart: 17, of which 13 were waited for; matrix products, arithmetic and copies ran while one was open for 8% of the time, Pallas kernels for 0%

commit v1 on v0

v1 whole, which is shorter than its diff:
```python
import jax
import jax.numpy as jnp
from jax import lax
from jax.sharding import PartitionSpec as P

HEAD_DIM = 128

eps = 1e-05
neg_big = -1e30
F32 = jnp.float32
BF16 = jnp.bfloat16


def normalize(rows):
    centred = rows - jnp.mean(rows, axis=-1, keepdims=True)
    inv_std = lax.rsqrt(jnp.mean(centred * centred, axis=-1, keepdims=True) + eps)
    return (centred * inv_std, inv_std)


def norm_back(normed, inv_std, grad):
    return inv_std * (
        grad
        - jnp.mean(grad, axis=-1, keepdims=True)
        - normed * jnp.mean(grad * normed, axis=-1, keepdims=True)
    )


def rotary_tables(positions, head_dim):
    half = head_dim // 2
    freqs = 10000.0 ** (-jnp.arange(half, dtype=F32) * 2.0 / head_dim)
    angles = positions.astype(F32)[:, None] * freqs[None, :]
    return (jnp.cos(angles), jnp.sin(angles))


def rotate(values, cosine, sine):
    half = values.shape[-1] // 2
    first = values[..., :half]
    second = values[..., half:]
    cosine = cosine[:, None, :]
    sine = sine[:, None, :]
    return jnp.concatenate(
        [first * cosine - second * sine, second * cosine + first * sine], axis=-1
    )


def rotate_back(grads, cosine, sine):
    return rotate(grads, cosine, -sine)


def times_transpose(left, weight):
    return lax.dot_general(
        left, weight, (((1,), (1,)), ((), ())), preferred_element_type=F32
    )


def over_rows(left, right):
    return lax.dot_general(
        left, right, (((0,), (0,)), ((), ())), preferred_element_type=F32
    )


def dot(left, right):
    return jnp.dot(left, right, preferred_element_type=F32)


def gather_rows(block):
    return lax.all_gather(block, "fsdp", axis=0, tiled=True)


def scatter_rows(partial):
    return lax.psum_scatter(
        partial.astype(BF16), "fsdp", scatter_dimension=0, tiled=True
    ).astype(F32)


def to_columns(weight, groups):
    n = lax.axis_size("fsdp")
    reps = lax.axis_size("rep")
    depth, width = weight.shape
    part = depth // reps
    own = lax.dynamic_slice_in_dim(weight, lax.axis_index("rep") * part, part, 0)
    own = own.reshape(part, groups, n, width // (groups * n))
    sent = lax.all_to_all(own, "fsdp", split_axis=2, concat_axis=0, tiled=True)
    sent = sent.reshape(n, part, width // n)
    full = lax.all_gather(sent, "rep", axis=1, tiled=True)
    return full.reshape(n * depth, width // n)


def to_rows(grad, groups):
    n = lax.axis_size("fsdp")
    reps = lax.axis_size("rep")
    depth, width = grad.shape
    part = depth // (n * reps)
    split = grad.astype(BF16).reshape(n, reps, part, width)
    summed = lax.psum_scatter(split, "rep", scatter_dimension=1, tiled=True)
    summed = summed.reshape(n, part, groups, width // groups)
    moved = lax.all_to_all(summed, "fsdp", split_axis=0, concat_axis=0, tiled=True)
    moved = moved.transpose(1, 2, 0, 3).reshape(part, n * width)
    return lax.all_gather(moved, "rep", axis=0, tiled=True).astype(F32)


def on_device(tokens, lengths, cotangent, w_qkv, w_out, w_in, w_down):
    rows = tokens.shape[1]
    width = tokens.shape[2]
    n = lax.axis_size("fsdp")
    slot_len = rows * n
    head_dim = HEAD_DIM
    own_width = width // n
    heads = own_width // head_dim
    scale = head_dim ** (-0.5)
    length = lengths[0]
    own_positions = lax.axis_index("fsdp") * rows + jnp.arange(rows, dtype=jnp.int32)
    valid = (own_positions < length).astype(F32)[:, None]
    positions = jnp.arange(slot_len, dtype=jnp.int32)
    cosine, sine = rotary_tables(positions, head_dim)

    x_rows = tokens[0].astype(F32)
    normed1, inv1 = normalize(x_rows)
    n1_full = gather_rows(normed1.astype(BF16))
    qkv_cols = to_columns(w_qkv, 3)
    in_cols = to_columns(w_in, 2)
    dy_rows = valid * cotangent[0].astype(F32)
    dy_full = gather_rows(dy_rows.astype(BF16))

    qkv = dot(n1_full, qkv_cols)
    query = rotate(
        qkv[:, :own_width].reshape(slot_len, heads, head_dim), cosine, sine
    ).astype(BF16)
    keys = rotate(
        qkv[:, own_width : 2 * own_width].reshape(slot_len, heads, head_dim), cosine, sine
    ).astype(BF16)
    values = qkv[:, 2 * own_width :].reshape(slot_len, heads, head_dim).astype(BF16)
    allowed = (positions[None, :] <= positions[:, None]) & (positions[None, :] < length)

    raw = jnp.einsum("qhd,khd->hqk", query, keys, preferred_element_type=F32) * scale
    scores = jnp.where(allowed[None], raw, neg_big)
    top = jnp.max(scores, axis=-1, keepdims=True)
    log_total = top + jnp.log(jnp.sum(jnp.exp(scores - top), axis=-1, keepdims=True))
    probs = jnp.exp(scores - log_total)
    probs_low = probs.astype(BF16)
    attended = jnp.einsum("hqk,khd->qhd", probs_low, values, preferred_element_type=F32)
    att_low = attended.reshape(slot_len, own_width).astype(BF16)

    hidden_in = x_rows + scatter_rows(dot(att_low, w_out))
    normed2, inv2 = normalize(hidden_in)
    n2_full = gather_rows(normed2.astype(BF16))
    gate_up = dot(n2_full, in_cols)
    units = gate_up.shape[1] // 2
    gate = gate_up[:, :units]
    upper = gate_up[:, units:]
    sigma = jax.nn.sigmoid(gate)
    silu_gate = gate * sigma
    act_low = (silu_gate * upper).astype(BF16)
    d_hidden = times_transpose(dy_full, w_down)
    d_gate = d_hidden * upper * sigma * (1.0 + gate * (1.0 - sigma))
    d_up = d_hidden * silu_gate
    dgu_low = jnp.concatenate([d_gate, d_up], axis=1).astype(BF16)
    d_norm2 = scatter_rows(times_transpose(dgu_low, in_cols))
    branch = scatter_rows(dot(act_low, w_down))
    output = (valid * (hidden_in + branch)).astype(BF16)
    d_resid = dy_rows + norm_back(normed2, inv2, d_norm2)
    dres_full = gather_rows(d_resid.astype(BF16))

    grad_down = over_rows(act_low, dy_full)
    grad_in = over_rows(n2_full, dgu_low)
    grad_out = over_rows(att_low, dres_full)

    datt = times_transpose(dres_full, w_out)
    datt_low = datt.astype(BF16).reshape(slot_len, heads, head_dim)
    delta = jnp.sum(datt_low.astype(F32) * attended, axis=-1).T
    d_probs = jnp.einsum("qhd,khd->hqk", datt_low, values, preferred_element_type=F32)
    d_scores = (probs * (d_probs - delta[..., None])).astype(BF16)
    dq = jnp.einsum("hqk,khd->qhd", d_scores, keys, preferred_element_type=F32) * scale
    dk = jnp.einsum("hqk,qhd->khd", d_scores, query, preferred_element_type=F32) * scale
    dv = jnp.einsum("hqk,qhd->khd", probs_low, datt_low, preferred_element_type=F32)
    dqkv_low = jnp.concatenate(
        [
            rotate_back(dq, cosine, sine).reshape(slot_len, own_width),
            rotate_back(dk, cosine, sine).reshape(slot_len, own_width),
            dv.reshape(slot_len, own_width),
        ],
        axis=1,
    ).astype(BF16)
    d_norm1 = scatter_rows(times_transpose(dqkv_low, qkv_cols))
    grad_tokens = (d_resid + norm_back(normed1, inv1, d_norm1)).astype(BF16)
    grad_qkv = over_rows(n1_full, dqkv_low)

    return (
        output[None],
        grad_tokens[None],
        to_rows(grad_qkv, 3),
        lax.psum(grad_out.astype(BF16), "rep").astype(F32),
        to_rows(grad_in, 2),
        lax.psum(grad_down.astype(BF16), "rep").astype(F32),
    )


def solution(mesh):
    in_specs = (
        P("rep", "fsdp", None),
        P("rep"),
        P("rep", "fsdp", None),
        P("fsdp", None),
        P("fsdp", None),
        P("fsdp", None),
        P("fsdp", None),
    )
    out_specs = (
        P("rep", "fsdp", None),
        P("rep", "fsdp", None),
        P("fsdp", None),
        P("fsdp", None),
        P("fsdp", None),
        P("fsdp", None),
    )
    return jax.shard_map(
        on_device, mesh=mesh, in_specs=in_specs, out_specs=out_specs, check_vma=False
    )
```

time: 2420 us -> 1210 us (0.50)
  waiting for transfers between devices: 2000 us -> 758 us
  blocking collectives: 0 us -> 209 us
  matrix products: 239 us -> 119 us
  local copies, waits for them, and re-layouts: 79.4 us -> 47.8 us
  starting transfers between devices: 30.7 us -> 1.88 us
    all_gather x10 -> x8, waiting for transfers between devices: 1540 us -> 421 us  [the longest x4 177 us: gather_rows(): return lax.all_gather(block, 'fsdp', axis=0, tiled=True)]
    all_to_all x0 -> x4, blocking collectives: none -> 209 us  [the longest x2 105 us: to_rows(): lax.all_to_all(summed, 'fsdp', split_axis=0, concat_axis=0, tiled=True)]
    all_to_all x4 -> x0, waiting for transfers between devices: 101 us -> none  [the longest x1 78.9 us: on_device(): lax.all_to_all(act_low, 'fsdp', split_axis=1, concat_axis=0, tiled=True)]
    reduce_scatter x0 -> x4, waiting for transfers between devices: none -> 91.4 us  [scatter_rows(): lax.psum_scatter(partial.astype(BF16), 'fsdp', scatter_dimension=0, tiled...]
    unnamed x15, waiting for transfers between devices: 93.1 us -> 13.2 us
    dot_general x18 -> x10, matrix products: 109 us -> 53 us  [the longest x4 33.3 us: dot(): return jnp.dot(left, right, preferred_element_type=F32)]
    dot_general x4, matrix products: 79.6 us -> 36.6 us  [times_transpose(): lax.dot_general(left, weight, (((1,), (1,)), ((), ())), preferred_element...]
    psum x1, waiting for transfers between devices: 266 us -> 232 us  [on_device(): lax.psum(grad_out.astype(BF16), 'rep').astype(F32)]
  transfers between devices with their start and end apart: 17 -> 14, of which waited for: 13 -> 14; matrix products, arithmetic and copies ran while one was open for 8% -> 9% of each run, Pallas kernels for 0% -> 0%
where the time goes in v1:
time: 1210 us; the launch traced here: 1200 us
  waiting for transfers between devices  758 us (63%)
  blocking collectives  209 us (17%)
  matrix products  119 us (10%)
  other arithmetic  51.3 us (4%)
  local copies, waits for them, and re-layouts  47.8 us (4%)
  between operations  15.4 us (1%)
    psum x1, waiting for transfers between devices, on_device(): lax.psum(grad_out.astype(BF16), 'rep').astype(F32)  232 us
    all_gather x4, waiting for transfers between devices, gather_rows(): return lax.all_gather(block, 'fsdp', axis=0, tiled=True)  177 us
    all_gather x2, waiting for transfers between devices, to_columns(): full = lax.all_gather(sent, 'rep', axis=1, tiled=True)  124 us
    all_gather x2, waiting for transfers between devices, to_rows(): return lax.all_gather(moved, 'rep', axis=0, tiled=True).astype(F32)  121 us
    all_to_all x2, blocking collectives, to_rows(): lax.all_to_all(summed, 'fsdp', split_axis=0, concat_axis=0, tiled=True)  105 us
    all_to_all x2, blocking collectives, to_columns(): sent = lax.all_to_all(own, 'fsdp', split_axis=2, concat_axis=0, tiled=True)  104 us
    reduce_scatter x4, waiting for transfers between devices, scatter_rows(): lax.psum_scatter(partial.astype(BF16), 'fsdp', scatter_dimension=0, tiled...  91.4 us
    dot_general x4, matrix products, times_transpose(): lax.dot_general(left, weight, (((1,), (1,)), ((), ())), preferred_element...  36.6 us
  transfers between devices with their start and end apart: 14, of which 14 were waited for; matrix products, arithmetic and copies ran while one was open for 9% of the time, Pallas kernels for 0%

profile of v1, /device:TPU:8, one launch (start us, length us, event | category | flops | bytes accessed | tf_op | source)
XLA Modules:
  0.0 1202.9 jit_solution(6206446378640740312)
XLA Ops:
  7.2 1.8 copy-done
  9.5 23.8 %all_to_all.40 = bf16[64,3,8,256]{3,0,1,2:T(8,128)(2,1)S(1)} all-to-all(bf16[64,3,8,256]{3,0,1,2:T(8,128)(2,1)S(1)} %copy.126), channel_id=1, replica_groups=mesh['rep'=4,'fsdp'=8] {'fsdp'}, dimensions={2} | all-to-all | bytes 1572864 | tf_op jit(solution)/shard_map/all_to_all | solution.py:83
  33.9 1.7 reshape.247
  38.6 3.1 fusion.27
  42.0 38.3 %all-gather.11.cloned.1.call-done = bf16[8,256,768]{2,1,0:T(8,128)(2,1)} async-done(((bf16[8,64,768]{2,1,0:T(8,128)(2,1)}), bf16[8,256,768]{2,1,0:T(8,128)(2,1)}) %all-gather.11.cloned.1.call-update) | async-done | bytes 3145744 | tf_op jit(solution)/shard_map/all_gather | solution.py:85
  80.3 47.8 %all-gather.9.cloned.1.call-done = bf16[1024,2048]{1,0:T(8,128)(2,1)} async-done(((bf16[128,2048]{1,0:T(8,128)(2,1)}), bf16[1024,2048]{1,0:T(8,128)(2,1)}) %all-gather.9.cloned.1.call-update) | async-done | bytes 4194320 | tf_op jit(solution)/shard_map/all_gather | solution.py:67
  128.2 6.2 fusion.44
  138.8 2.4 copy.166
  141.2 2.3 fusion.42
  143.4 2.4 copy.168
  145.8 2.4 copy.169
  148.1 2.6 subtract_convert_fusion.3
  150.8 2.3 fusion.1
  153.1 2.0 exponential_reduce_fusion
  156.5 3.6 fusion.43
  160.1 3.3 convolution_convert_fusion.2
  163.6 1.7 constant_dynamic-slice_fusion.1
  166.6 2.2 copy.133
  168.8 80.3 %all_to_all.41 = bf16[64,2,8,1024]{3,1,0,2:T(2,128)(2,1)} all-to-all(bf16[64,2,8,1024]{3,1,0,2:T(2,128)(2,1)S(1)} %copy.133), channel_id=1, replica_groups=mesh['rep'=4,'fsdp'=8] {'fsdp'}, dimensions={2} | all-to-all | bytes 4194304 | tf_op jit(solution)/shard_map/all_to_all | solution.py:83
  249.0 4.5 reshape.252
  253.6 1.9 reduce-scatter.11.cloned.1.call-done
  258.1 2.1 fusion.24
  261.2 85.6 %all-gather.15.cloned.1.call-done = bf16[8,256,2048]{2,1,0:T(8,128)(2,1)} async-done(((bf16[8,64,2048]{2,1,0:T(8,128)(2,1)}), bf16[8,256,2048]{2,1,0:T(8,128)(2,1)}) %all-gather.15.cloned.1.call-update) | async-done | bytes 8388624 | tf_op jit(solution)/shard_map/all_gather | solution.py:85
  346.8 47.7 %all-gather.13.cloned.1.call-done = bf16[1024,2048]{1,0:T(8,128)(2,1)} async-done(((bf16[128,2048]{1,0:T(8,128)(2,1)}), bf16[1024,2048]{1,0:T(8,128)(2,1)}) %all-gather.13.cloned.1.call-update) | async-done | bytes 4194320 | tf_op jit(solution)/shard_map/all_gather | solution.py:67
  394.5 14.5 %fusion.45 = f32[1024,2048]{1,0:T(8,128)} fusion(bf16[1024,2048]{1,0:T(8,128)(2,1)} %all-gather.13.cloned.1.call-done, bf16[2048,2048]{1,0:T(8,128)(2,1)} %bitcast.170), kind=kOutput, calls=%fused_computation.110 | convolution fusion | flops 8589934592 | bytes 20971520 | tf_op jit(solution)/shard_map/dot_general | solution.py:63
  409.0 33.3 %all-gather.17.cloned.1.call-done = bf16[1024,2048]{1,0:T(8,128)(2,1)} async-done(((bf16[128,2048]{1,0:T(8,128)(2,1)}), bf16[1024,2048]{1,0:T(8,128)(2,1)}) %all-gather.17.cloned.1.call-update) | async-done | bytes 4194320 | tf_op jit(solution)/shard_map/all_gather | solution.py:67
  442.2 14.0 %multiply_convert_fusion.2 = (bf16[1024,1024]{1,0:T(8,128)(2,1)S(1)}, bf16[1024,1024]{1,0:T(8,128)(2,1)}, bf16[1024,1024]{1,0:T(8,128)(2,1)}) fusion(f32[1024,2048]{1,0:T(8,128)} %fusion.45, bf16[1024,2048]{1,0:T(8,128)(2,1)} %all-gather.17.cloned.1.call-done, bf16[1024,2048]{1,0:T(8,128)(2,1)} %param.13), kind=kOutput, calls=%fused_computation.9 | convolution fusion | flops 4310695936 | bytes 23068672 | tf_op jit(solution)/shard_map/dot_general | solution.py:51
  457.6 11.6 convolution_convert_fusion.1
  469.5 9.3 convolution_convert_fusion.5
  478.9 36.9 %reduce-scatter.15.cloned.1.call-done = bf16[128,2048]{1,0:T(8,128)(2,1)} async-done(((bf16[1024,2048]{1,0:T(8,128)(2,1)}), bf16[128,2048]{1,0:T(8,128)(2,1)}) %reduce-scatter.15.cloned.1.call-update) | async-done | bytes 524304 | tf_op jit(solution)/shard_map/reduce_scatter | solution.py:71
  515.8 1.5 convert_reduce_fusion.1
  517.3 49.8 %reduce-scatter.13.cloned.1.call-done = bf16[128,2048]{1,0:T(8,128)(2,1)} async-done(((bf16[1024,2048]{1,0:T(8,128)(2,1)}), bf16[128,2048]{1,0:T(8,128)(2,1)}) %reduce-scatter.13.cloned.1.call-update) | async-done | bytes 524304 | tf_op jit(solution)/shard_map/reduce_scatter | solution.py:71
  567.1 3.3 fusion.38
  570.5 47.7 %all-gather.19.cloned.1.call-done = bf16[1024,2048]{1,0:T(8,128)(2,1)} async-done(((bf16[128,2048]{1,0:T(8,128)(2,1)}), bf16[1024,2048]{1,0:T(8,128)(2,1)}) %all-gather.19.cloned.1.call-update) | async-done | bytes 4194320 | tf_op jit(solution)/shard_map/all_gather | solution.py:67
  618.2 3.9 multiply_reduce_fusion
  622.2 6.9 convolution_convert_fusion.8
  629.1 3.7 multiply_convert_fusion
  632.8 2.0 fusion.5
  636.2 1.7 subtract_convert_fusion.1
  638.4 1.5 pad_maximum_fusion.8
  640.1 5.8 convolution_convert_fusion.6
  645.9 1.8 copy.148
  648.0 9.6 convolution_convert_fusion.4
  657.6 11.6 convolution_convert_fusion
  669.2 2.3 convolution_convert_fusion.7
  671.8 7.0 convolution_convert_fusion.3
  678.9 13.0 %reduce-scatter.19.cloned.1.call-done = bf16[8,1,64,768]{3,2,0,1:T(8,128)(2,1)} async-done(((bf16[8,4,64,768]{3,2,0,1:T(8,128)(2,1)}), bf16[8,1,64,768]{3,2,0,1:T(8,128)(2,1)}) %reduce-scatter.19.cloned.1.call-update) | async-done | bytes 786448
  691.9 2.5 reshape.259
  694.6 23.6 %all_to_all.42 = bf16[8,64,3,256]{3,1,2,0:T(8,128)(2,1)S(1)} all-to-all(bf16[8,64,3,256]{3,1,2,0:T(8,128)(2,1)S(1)} %copy.149), channel_id=1, replica_groups=mesh['rep'=4,'fsdp'=8] {'fsdp'}, dimensions={0} | all-to-all | bytes 1572864 | tf_op jit(solution)/shard_map/all_to_all | solution.py:97
  720.3 232.4 %all-reduce.5.cloned.1.call-done = (bf16[256,2048]{1,0:T(8,128)(2,1)}, bf16[8,4,64,2048]{3,2,1,0:T(8,128)(2,1)}, bf16[1024,2048]{1,0:T(8,128)(2,1)}) async-done(((bf16[256,2048]{1,0:T(8,128)(2,1)}, bf16[8,4,64,2048]{3,2,1,0:T(8,128)(2,1)}, bf16[1024,2048]{1,0:T(8,128)(2,1)}), (bf16[256,2048]{1,0:T(8,128)(2,1)}, bf16[8,4,64,2048]{3,2,1,0:T(8,128)(2,1)}, ...) | async-done | bytes 13631504 | tf_op jit(solution)/shard_map/psum | solution.py:192
  952.8 2.5 constant_dynamic-slice_fusion
  955.3 2.8 reshape.262
  958.0 81.7 %all_to_all.43 = bf16[8,64,2,1024]{3,2,1,0:T(2,128)(2,1)S(1)} all-to-all(bf16[8,64,2,1024]{3,2,1,0:T(2,128)(2,1)} %reshape.262), channel_id=1, replica_groups=mesh['rep'=4,'fsdp'=8] {'fsdp'}, dimensions={0} | all-to-all | bytes 4194304 | tf_op jit(solution)/shard_map/all_to_all | solution.py:97
  1039.7 2.2 copy.151
  1041.9 2.5 copy.173
  1044.5 2.9 reduce-scatter.17.cloned.1.call-done
  1047.3 1.4 convert_reduce_fusion
  1048.8 2.3 fusion.26
  1051.1 43.6 %all-gather.21.cloned.1.call-done = bf16[256,6144]{1,0:T(8,128)(2,1)} async-done(((bf16[64,6144]{1,0:T(8,128)(2,1)}), bf16[256,6144]{1,0:T(8,128)(2,1)}) %all-gather.21.cloned.1.call-update) | async-done | bytes 3145744 | tf_op jit(solution)/shard_map/all_gather | solution.py:99
  1094.7 5.5 convert_element_type.180
  1100.2 1.6 convert_element_type.182
  1101.8 5.3 convert_element_type.186
  1107.1 77.4 %all-gather.23.cloned.1.call-done = bf16[256,16384]{1,0:T(8,128)(2,1)} async-done(((bf16[64,16384]{1,0:T(8,128)(2,1)}), bf16[256,16384]{1,0:T(8,128)(2,1)}) %all-gather.23.cloned.1.call-update) | async-done | bytes 8388624 | tf_op jit(solution)/shard_map/all_gather | solution.py:99
  1184.5 11.7 convert_element_type.184
  (144 shorter events, 21.5 us)
Async XLA Ops:
  7.2 1.9 copy-start
  7.2 73.1 %all-gather.11.cloned.1.call-start = ((), (), s32[]{:S(2)}) async-start(), calls=%async_computation.10 | async-start | bytes 3932160 | tf_op jit(solution)/shard_map/all_gather | solution.py:85
  9.3 26.4 %copy-start.2 = (bf16[1,128,2048]{2,1,0:T(8,128)(2,1)S(1)}, bf16[1,128,2048]{2,1,0:T(8,128)(2,1)}, u32[]{:S(2)}) copy-start(bf16[1,128,2048]{2,1,0:T(8,128)(2,1)} %param.7) | copy-start | bytes 1572868
  35.6 92.5 %all-gather.9.cloned.1.call-start = ((), (), s32[]{:S(2)}) async-start(), calls=%async_computation.9 | async-start | bytes 4718592 | tf_op jit(solution)/shard_map/all_gather | solution.py:67
  35.9 2.7 copy-start.26
  36.2 2.4 copy-start.28
  37.3 218.1 %reduce-scatter.11.cloned.1.call-start = ((), (), s32[]{:S(2)}) async-start(), calls=%async_computation.11 | async-start | bytes 4718592 | tf_op jit(solution)/shard_map/reduce_scatter | solution.py:71
  42.0 113.1 %copy-start.6 = (pred[1024,1024]{0,1:T(8,128)(4,1)}, pred[1024,1024]{0,1:T(8,128)(4,1)S(1)}, u32[]{:S(2)}) copy-start(pred[1024,1024]{0,1:T(8,128)(4,1)S(1)} %fusion.3) | copy-start | bytes 3145732
  150.7 2.3 copy-start.9
  150.7 2.3 copy-start.11
  150.7 2.3 copy-start.13
  150.7 2.3 copy-start.15
  153.1 3.4 copy-start.4
  153.1 3.4 copy-start.24
  156.5 3.6 copy-start.22
  160.1 3.4 copy-start.19
  163.4 183.4 %all-gather.15.cloned.1.call-start = ((), (), s32[]{:S(2)}) async-start(), calls=%async_computation.13 | async-start | bytes 10485760 | tf_op jit(solution)/shard_map/all_gather | solution.py:85
  253.5 6.7 copy-start.18
  253.5 141.0 %all-gather.13.cloned.1.call-start = ((), (), s32[]{:S(2)}) async-start(), calls=%async_computation.12 | async-start | bytes 4718592 | tf_op jit(solution)/shard_map/all_gather | solution.py:67
  260.1 182.1 %all-gather.17.cloned.1.call-start = ((), (), s32[]{:S(2)}) async-start(), calls=%async_computation.15 | async-start | bytes 4718592 | tf_op jit(solution)/shard_map/all_gather | solution.py:67
  261.2 254.6 %reduce-scatter.15.cloned.1.call-start = ((), (), s32[]{:S(2)}) async-start(), calls=%async_computation.16 | async-start | bytes 4718592 | tf_op jit(solution)/shard_map/reduce_scatter | solution.py:71
  442.2 15.4 %copy-start.30 = (bf16[8,256,2048]{2,1,0:T(8,128)(2,1)S(1)}, bf16[8,256,2048]{2,1,0:T(8,128)(2,1)}, u32[]{:S(2)}) copy-start(bf16[8,256,2048]{2,1,0:T(8,128)(2,1)} %all-gather.15.cloned.1.call-done) | copy-start | bytes 25165828
  456.2 1.3 copy-start.35
  469.2 97.9 %reduce-scatter.13.cloned.1.call-start = ((), (), s32[]{:S(2)}) async-start(), calls=%async_computation.14 | async-start | bytes 4718592 | tf_op jit(solution)/shard_map/reduce_scatter | solution.py:71
  478.8 37.0 %copy-start.3 = (bf16[128,2048]{1,0:T(8,128)(2,1)S(1)}, bf16[128,2048]{1,0:T(8,128)(2,1)}, u32[]{:S(2)}) copy-start(bf16[128,2048]{1,0:T(8,128)(2,1)} %reduce-scatter.11.cloned.1.call-done) | copy-start | bytes 1572868
  478.8 139.4 %copy-start.23 = (bf16[256,2048]{1,0:T(8,128)(2,1)S(1)}, bf16[256,2048]{1,0:T(8,128)(2,1)}, u32[]{:S(2)}) copy-start(bf16[256,2048]{1,0:T(8,128)(2,1)} %param.11) | copy-start | bytes 3145732
  478.9 139.4 %all-gather.19.cloned.1.call-start = ((), (), s32[]{:S(2)}) async-start(), calls=%async_computation.17 | async-start | bytes 4718592 | tf_op jit(solution)/shard_map/all_gather | solution.py:67
  570.4 51.8 %copy-start.7 = (pred[1024,1024]{0,1:T(8,128)(4,1)S(1)}, pred[1024,1024]{0,1:T(8,128)(4,1)}, u32[]{:S(2)}) copy-start(pred[1024,1024]{0,1:T(8,128)(4,1)} %copy-done.6) | copy-start | bytes 3145732
  570.4 121.5 %reduce-scatter.19.cloned.1.call-start = ((), (), s32[]{:S(2)}) async-start(), calls=%async_computation.21 | async-start | bytes 3932160
  618.2 10.9 slice-start
  622.2 6.9 slice-start.1
  622.2 6.9 copy-start.25
  629.1 3.7 copy-start.14
  629.1 3.7 copy-start.16
  632.8 2.0 copy-start.10
  632.8 2.0 copy-start.12
  634.8 1.3 copy-start.17
  637.9 2.2 copy-start.33
  647.8 305.0 %all-reduce.5.cloned.1.call-start = ((), (), s32[]{:S(2)}) async-start(), calls=%async_computation.22 | async-start | bytes 27262976 | tf_op jit(solution)/shard_map/psum | solution.py:192
  648.0 9.6 copy-start.31
  648.0 9.6 copy-start.36
  648.0 9.6 copy-start.37
  657.6 11.6 copy-start.20
  657.6 11.6 copy-start.32
  671.5 375.8 %reduce-scatter.17.cloned.1.call-start = ((), (), s32[]{:S(2)}) async-start(), calls=%async_computation.18 | async-start | bytes 4718592 | tf_op jit(solution)/shard_map/reduce_scatter | solution.py:71
  678.8 40.9 %copy-start.34 = (u32[32]{0:T(128)S(1)}, u32[32]{0:T(128)}, u32[]{:S(2)}) copy-start(u32[32]{0:T(128)} %constant.51) | copy-start | bytes 388
  678.9 415.8 %all-gather.21.cloned.1.call-start = ((), (), s32[]{:S(2)}) async-start(), calls=%async_computation.19 | async-start | bytes 3932160 | tf_op jit(solution)/shard_map/all_gather | solution.py:99
  719.7 464.8 %all-gather.23.cloned.1.call-start = ((), (), s32[]{:S(2)}) async-start(), calls=%async_computation.20 | async-start | bytes 10485760 | tf_op jit(solution)/shard_map/all_gather | solution.py:99
  1041.9 5.5 copy-start.27
  1041.9 5.4 copy-start.29
  1041.9 6.9 copy-start.8
  1051.1 49.1 %copy-start.21 = (bf16[256,2048]{1,0:T(8,128)(2,1)S(1)}, bf16[256,2048]{1,0:T(8,128)(2,1)}, u32[]{:S(2)}) copy-start(bf16[256,2048]{1,0:T(8,128)(2,1)} %get-tuple-element.10) | copy-start | bytes 3145732
  1094.7 7.1 copy-start.5
  1184.5 11.7 copy-start.1
Sparse Core Ops, SparseCore 0:
  35.8 44.5 all-gather.10
  82.5 45.6 all-gather.8
  163.5 91.8 reduce-scatter.10
  257.7 89.0 all-gather.14
  348.8 45.6 all-gather.12
  396.5 45.6 all-gather.16
  469.3 46.4 reduce-scatter.14
  518.7 48.3 reduce-scatter.12
  570.6 47.6 all-gather.18
  647.9 43.9 reduce-scatter.18
  696.4 256.3 all-reduce.4
  955.5 91.8 reduce-scatter.16
  1049.2 45.4 all-gather.20
  1097.0 87.4 all-gather.22

commit v2 on v1

--- a/solution.py
+++ b/solution.py
@@ -1,6 +1,10 @@
+import functools
+
 import jax
 import jax.numpy as jnp
 from jax import lax
+from jax.experimental import pallas as pl
+from jax.experimental.pallas import tpu as pltpu
 from jax.sharding import PartitionSpec as P
 
 HEAD_DIM = 128
@@ -63,6 +67,686 @@
     return jnp.dot(left, right, preferred_element_type=F32)
 
 
+MESH = pl.DeviceIdType.MESH
+LIMIT = 60 * 1024 * 1024
+
+
+class Kit:
+    def __init__(self, sems, sizes):
+        self.sems = sems
+        self.used = 0
+        self.n, self.reps = sizes
+        self.chips = self.n // 2
+        self.me = lax.axis_index("fsdp")
+        self.rep = lax.axis_index("rep")
+        self.chip = self.me // 2
+        self.core = self.me % 2
+        self.bits = self.reps.bit_length() - 1
+
+    def sem(self):
+        self.used += 1
+        return self.sems.at[self.used - 1]
+
+    def barrier(self, fsdp=True, rep=True):
+        wall = pltpu.get_barrier_semaphore()
+        count = 0
+        if fsdp:
+            for k in range(1, self.n):
+                pl.semaphore_signal(wall, inc=1, device_id={"fsdp": self.me ^ k}, device_id_type=MESH)
+                count += 1
+        if rep:
+            for b in range(self.bits):
+                pl.semaphore_signal(wall, inc=1, device_id={"rep": self.rep ^ (1 << b)}, device_id_type=MESH)
+                count += 1
+        pl.semaphore_wait(wall, count)
+
+    def copy(self, src, dst, sems, fsdp=None, rep=None):
+        where = {"fsdp": fsdp} if rep is None else {"rep": rep}
+        return pltpu.make_async_remote_copy(
+            src_ref=src, dst_ref=dst, send_sem=sems[0], recv_sem=sems[1],
+            device_id=where, device_id_type=MESH,
+        )
+
+    def pair(self):
+        return (self.sem(), self.sem())
+
+    def bit(self, index):
+        return (self.rep >> index) & 1
+
+    def gather_line(self, src, dst, rows):
+        C, z, c = self.chips, self.chip, self.core
+
+        def blk(chip, core):
+            return dst.at[pl.ds(pl.multiple_of((2 * chip + core) * rows, rows), rows)]
+
+        local = pltpu.make_async_copy(src, blk(z, c), self.sem())
+        local.start()
+        partner = self.me ^ 1
+        own_sems = self.pair()
+        own_pair = self.copy(src, blk(z, c), own_sems, fsdp=partner)
+        other_own = blk(z, 1 - c)
+        ways = []
+        for sign in (1, -1):
+            sends = [self.pair() for _ in range(C - 1)]
+            forwards = [self.pair() for _ in range(C - 1)]
+            ways.append((sign, sends, forwards))
+
+        def inside(chip):
+            return (chip >= 0) & (chip < C)
+
+        def hop(sign, sends, k):
+            shard = z - sign * k
+            ref = src if k == 0 else blk(shard, c)
+            return self.copy(ref, blk(shard, c), sends[k], fsdp=2 * (z + sign) + c)
+
+        def across(sign, forwards, k):
+            shard = z - sign * k
+            return self.copy(blk(shard, c), blk(shard, c), forwards[k - 1], fsdp=partner)
+
+        for sign, sends, forwards in ways:
+            @pl.when(inside(z + sign))
+            def _():
+                hop(sign, sends, 0).start()
+        own_pair.start()
+        for k in range(1, C):
+            yield
+            for sign, sends, forwards in ways:
+                @pl.when(inside(z - sign * k))
+                def _():
+                    shard = z - sign * k
+                    self.copy(blk(shard, c), blk(shard, c), sends[k - 1], fsdp=partner).wait_recv()
+                    if k < C - 1:
+                        @pl.when(inside(z + sign))
+                        def _():
+                            hop(sign, sends, k).start()
+                    across(sign, forwards, k).start()
+        yield
+        local.wait()
+        own_pair.wait_send()
+        self.copy(src, other_own, own_sems, fsdp=partner).wait_recv()
+        for k in range(0, C - 1):
+            for sign, sends, forwards in ways:
+                @pl.when(inside(z + sign) & inside(z - sign * k))
+                def _():
+                    hop(sign, sends, k).wait_send()
+        for k in range(1, C):
+            for sign, sends, forwards in ways:
+                @pl.when(inside(z - sign * k))
+                def _():
+                    across(sign, forwards, k).wait_send()
+                    shard = z - sign * k
+                    self.copy(blk(shard, c), blk(shard, 1 - c), forwards[k - 1], fsdp=partner).wait_recv()
+
+    def scatter_line(self, partial, total, rows, near, mine, left, right):
+        C, z, c = self.chips, self.chip, self.core
+        partner = self.me ^ 1
+
+        def blk(chip, core):
+            return partial.at[pl.ds(pl.multiple_of((2 * chip + core) * rows, rows), rows)]
+
+        order = []
+        for j in range(C):
+            for d in (C - 1 - j, j):
+                if d not in order:
+                    order.append(d)
+        near_sems = [self.pair() for _ in range(C)]
+        right_sems = [self.pair() for _ in range(C)]
+        left_sems = [self.pair() for _ in range(C)]
+
+        def swap(d):
+            return self.copy(blk(d, 1 - c), near.at[d], near_sems[d], fsdp=partner)
+
+        def to_right(d):
+            return self.copy(mine.at[d], right.at[d], right_sems[d], fsdp=2 * (z + 1) + c)
+
+        def to_left(d):
+            return self.copy(mine.at[d], left.at[d], left_sems[d], fsdp=2 * (z - 1) + c)
+
+        for d in order:
+            swap(d).start()
+        yield
+        for d in order:
+            swap(d).wait_recv()
+            add_into(mine.at[d], blk(d, c), near.at[d])
+            @pl.when((z == 0) & (d > 0))
+            def _():
+                to_right(d).start()
+            @pl.when((z == C - 1) & (d < C - 1))
+            def _():
+                to_left(d).start()
+        for j in range(C - 1):
+            yield
+            d = C - 1 - j
+            @pl.when((z > 0) & (z < d))
+            def _():
+                to_right(d).wait_recv()
+                add_into(mine.at[d], mine.at[d], right.at[d])
+                to_right(d).start()
+            e = j
+            @pl.when((z < C - 1) & (z > e))
+            def _():
+                to_left(e).wait_recv()
+                add_into(mine.at[e], mine.at[e], left.at[e])
+                to_left(e).start()
+        yield
+        keep(total, mine.at[z])
+        for d in range(C):
+            if d > 0:
+                @pl.when(z == d)
+                def _():
+                    to_right(d).wait_recv()
+                    accumulate(total, right.at[d])
+            if d < C - 1:
+                @pl.when(z == d)
+                def _():
+                    to_left(d).wait_recv()
+                    accumulate(total, left.at[d])
+        yield
+        for d in range(C):
+            swap(d).wait_send()
+            @pl.when(z < d)
+            def _():
+                to_right(d).wait_send()
+            @pl.when(z > d)
+            def _():
+                to_left(d).wait_send()
+
+    def exchange(self, pieces, arrivals):
+        sems = {}
+        for k in range(1, self.n):
+            for i, (src, dst) in enumerate(pieces(self.me ^ k)):
+                sems[k, i] = self.pair()
+                self.copy(src, dst, sems[k, i], fsdp=self.me ^ k).start()
+        yield
+        for k in range(1, self.n):
+            for i, (src, dst) in enumerate(arrivals(self.me ^ k)):
+                self.copy(src, dst, sems[k, i], fsdp=self.me ^ k).wait_recv()
+        yield
+        for k in range(1, self.n):
+            for i, (src, dst) in enumerate(pieces(self.me ^ k)):
+                self.copy(src, dst, sems[k, i], fsdp=self.me ^ k).wait_send()
+
+    def gather_rep(self, blk):
+        sent = []
+        waits = {0: [], 1: []}
+        for i in range(self.bits):
+            for half in (0, 1):
+                b = i if half == 0 else self.bits - 1 - i
+                before = [j if half == 0 else self.bits - 1 - j for j in range(i)]
+                for cp in waits[half]:
+                    cp.wait_recv()
+                waits[half] = []
+                peer = self.rep ^ (1 << b)
+                for mask in range(1 << i):
+                    flip = sum(((mask >> j) & 1) << before[j] for j in range(i))
+                    r = self.rep ^ flip
+                    sems = self.pair()
+                    cp = self.copy(blk(half, r), blk(half, r), sems, rep=peer)
+                    cp.start()
+                    sent.append(cp)
+                    waits[half].append(self.copy(blk(half, r), blk(half, r ^ (1 << b)), sems, rep=peer))
+            yield
+        for half in (0, 1):
+            for cp in waits[half]:
+                cp.wait_recv()
+        yield
+        for cp in sent:
+            cp.wait_send()
+
+    def scatter_rep(self, blk, land, done):
+        sent = []
+        waits = {0: [], 1: []}
+        nb = self.bits
+
+        def start(half, i):
+            order = list(range(nb)) if half == 0 else list(range(nb))[::-1]
+            peer = self.rep ^ (1 << order[i])
+            rest = order[i + 1:]
+            todo = []
+            for combo in range(1 << len(rest)):
+                def source(own, combo=combo):
+                    value = self.bit(order[i]) if own else 1 - self.bit(order[i])
+                    if i == 0:
+                        r = value << order[0]
+                        r = r + sum(((combo >> j) & 1) << rest[j] for j in range(len(rest)))
+                        return blk(half, r)
+                    return land(half, i - 1, value + 2 * combo)
+                sems = self.pair()
+                cp = self.copy(source(False), land(half, i, combo), sems, rep=peer)
+                cp.start()
+                sent.append(cp)
+                todo.append((cp, land(half, i, combo), source(True)))
+            return todo
+
+        for i in range(nb):
+            for half in (0, 1):
+                if i == 0:
+                    waits[half] = start(half, 0)
+            if i == 0:
+                yield
+            for half in (0, 1):
+                for cp, ref, own in waits[half]:
+                    cp.wait_recv()
+                    if i < nb - 1:
+                        add_into(ref, ref, own)
+                    else:
+                        done(half, ref, own)
+                if i < nb - 1:
+                    waits[half] = start(half, i + 1)
+            yield
+        for cp in sent:
+            cp.wait_send()
+
+
+def each(ref, body):
+    lead = ref.shape[:-2]
+    count = ref.shape[-2] // 16
+    total = count
+    for size in lead:
+        total *= size
+
+    def step(t, carry):
+        rows = pl.ds(pl.multiple_of((t % count) * 16, 16), 16)
+        rest = t // count
+        index = []
+        for size in reversed(lead):
+            index.append(rest % size)
+            rest = rest // size
+        body(tuple(reversed(index)) + (rows,))
+        return carry
+
+    lax.fori_loop(0, total, step, 0)
+
+
+def add_into(dst, a, b):
+    def body(at):
+        dst[at] = (a[at].astype(F32) + b[at].astype(F32)).astype(dst.dtype)
+
+    each(dst, body)
+
+
+def keep(dst, a):
+    def body(at):
+        dst[at] = a[at].astype(dst.dtype)
+
+    each(dst, body)
+
+
+def accumulate(dst, a):
+    def body(at):
+        dst[at] = dst[at] + a[at].astype(F32)
+
+    each(dst, body)
+
+
+def finish(*tasks):
+    for task in tasks:
+        for _ in task:
+            pass
+
+
+def turns(order):
+    for task in order:
+        next(task, None)
+
+
+def cut(width):
+    low = width // 256 * 128
+    return ((0, low), (low, width - low))
+
+
+def column_blocks(ref):
+    parts = cut(ref.shape[-1])
+    lead = len(ref.shape) - 3
+
+    def blk(half, r):
+        start, size = parts[half]
+        return ref.at[(slice(None),) * lead + (r, slice(None), pl.ds(start, size))]
+
+    return blk
+
+
+def own_piece(kit, src_of, dst_of, stage, groups, width):
+    first, second = kit.sem(), kit.sem()
+    loads = [
+        pltpu.make_async_copy(src_of(g), stage.at[:, pl.ds(g * width, width)], kit.sem())
+        for g in range(groups)
+    ]
+    for cp in loads:
+        cp.start()
+    yield
+    for cp in loads:
+        cp.wait()
+    store = pltpu.make_async_copy(stage, dst_of, first)
+    store.start()
+    yield
+    store.wait()
+
+
+def column_slice(start, size):
+    return pl.ds(pl.multiple_of(start, 128), size)
+
+
+def reshard(kit, weight, cols, stage, groups):
+    n, reps, part, total = cols.shape
+    width = total // groups
+    rows = pl.ds(pl.multiple_of(kit.rep * part, part), part)
+
+    def source(g, d):
+        return weight.at[rows, column_slice(g * (width * n) + d * width, width)]
+
+    def pieces(d):
+        return [
+            (source(g, d), cols.at[kit.me, kit.rep, :, pl.ds(g * width, width)])
+            for g in range(groups)
+        ]
+
+    def arrivals(d):
+        return [
+            (source(g, d), cols.at[d, kit.rep, :, pl.ds(g * width, width)])
+            for g in range(groups)
+        ]
+
+    own = own_piece(
+        kit, lambda g: source(g, kit.me), cols.at[kit.me, kit.rep], stage, groups, width
+    )
+    move = kit.exchange(pieces, arrivals)
+    next(move)
+    next(own)
+    yield
+    next(own)
+    next(own, None)
+    next(move)
+    yield
+    finish(move)
+
+
+def unshard(kit, sums, out, groups):
+    n, part, total = sums.shape
+    width = total // groups
+
+    def target(g, d):
+        return out.at[kit.rep, :, column_slice(g * (width * n) + d * width, width)]
+
+    def pieces(d):
+        return [(sums.at[d, :, pl.ds(g * width, width)], target(g, kit.me)) for g in range(groups)]
+
+    def arrivals(d):
+        return [(sums.at[d, :, pl.ds(g * width, width)], target(g, d)) for g in range(groups)]
+
+    own = [
+        pltpu.make_async_copy(src, dst, kit.sem()) for src, dst in pieces(kit.me)
+    ]
+    for cp in own:
+        cp.start()
+    move = kit.exchange(pieces, arrivals)
+    next(move)
+    yield
+    for cp in own:
+        cp.wait()
+    next(move)
+    yield
+    finish(move)
+
+
+def call(body, ins, outs, scratch, count, ident, name):
+    def spec(space):
+        return pl.BlockSpec(memory_space=space)
+
+    return pl.pallas_call(
+        body,
+        out_shape=[jax.ShapeDtypeStruct(s, d) for s, d, _ in outs],
+        in_specs=[spec(space) for _, space in ins],
+        out_specs=[spec(space) for _, _, space in outs],
+        scratch_shapes=list(scratch) + [pltpu.SemaphoreType.DMA((count,))],
+        compiler_params=pltpu.CompilerParams(
+            collective_id=ident, has_side_effects=True, vmem_limit_bytes=LIMIT
+        ),
+        name=name,
+    )(*[a for a, _ in ins])
+
+
+ANY = pl.ANY
+VMEM = pltpu.VMEM
+SEMS = 200
+
+
+def begin_kernel(sizes, n1, w_qkv, n1_full, cols, stage, sems):
+    kit = Kit(sems, sizes)
+    kit.barrier()
+    move = reshard(kit, w_qkv, cols, stage, 3)
+    next(move)
+    rows = kit.gather_line(n1, n1_full, n1.shape[0])
+    next(rows)
+    next(move)
+    spread = kit.gather_rep(column_blocks(cols))
+    next(spread)
+    finish_in_turn([rows, spread, move])
+
+
+def finish_in_turn(tasks):
+    tasks = list(tasks)
+    done = object()
+    while tasks:
+        tasks = [t for t in tasks if next(t, done) is not done]
+
+
+def begin(sizes, n1, w_qkv):
+    n, reps = sizes
+    rows, width = n1.shape
+    depth = w_qkv.shape[0]
+    part, own = depth // reps, w_qkv.shape[1] // n
+    full, cols = call(
+        functools.partial(begin_kernel, sizes),
+        [(n1, VMEM), (w_qkv, ANY)],
+        [((n * rows, width), BF16, ANY), ((n, reps, part, own), BF16, ANY)],
+        [VMEM((part, own), BF16)],
+        SEMS, 1, "begin",
+    )
+    return full, cols.reshape(n * depth, own)
+
+
+def norm_rows(dst, src):
+    def body(at):
+        h = src[at]
+        centred = h - jnp.mean(h, axis=-1, keepdims=True)
+        inv = lax.rsqrt(jnp.mean(centred * centred, axis=-1, keepdims=True) + eps)
+        dst[at] = (centred * inv).astype(BF16)
+
+    each(dst, body)
+
+
+def middle_kernel(sizes, partial, x, w_in, hidden, n2_full, cols, near, mine, left, right, n2, stage, sems):
+    kit = Kit(sems, sizes)
+    kit.barrier()
+    total = kit.scatter_line(partial, hidden, x.shape[0], near, mine, left, right)
+    next(total)
+    move = reshard(kit, w_in, cols, stage, 2)
+    next(total)
+    next(move)
+    for _ in range(kit.chips - 1):
+        next(total)
+    accumulated = next(total)
+
+    def body(at):
+        hidden[at] = hidden[at] + x[at].astype(F32)
+
+    each(hidden, body)
+    norm_rows(n2, hidden)
+    rows = kit.gather_line(n2, n2_full, n2.shape[0])
+    next(rows)
+    next(move)
+    spread = kit.gather_rep(column_blocks(cols))
+    next(spread)
+    finish_in_turn([rows, spread, move, total])
+
+
+def middle(sizes, partial, x, w_in):
+    n, reps = sizes
+    rows, width = x.shape
+    depth = w_in.shape[0]
+    part, own = depth // reps, w_in.shape[1] // n
+    lands = [VMEM((n // 2, rows, width), BF16) for _ in range(4)]
+    hidden, full, cols = call(
+        functools.partial(middle_kernel, sizes),
+        [(partial, VMEM), (x, VMEM), (w_in, ANY)],
+        [
+            ((rows, width), F32, VMEM),
+            ((n * rows, width), BF16, ANY),
+            ((n, reps, part, own), BF16, ANY),
+        ],
+        lands + [VMEM((rows, width), BF16), VMEM((part, own), BF16)],
+        SEMS, 2, "middle",
+    )
+    return hidden, full, cols.reshape(n * depth, own)
+
+
+def lands_of(shape, reps):
+    lead, (part, width) = shape[:-3], shape[-2:]
+    bits = reps.bit_length() - 1
+    places = []
+    for start, size in cut(width):
+        for i in range(bits):
+            places.append(VMEM((1 << (bits - 1 - i),) + lead + (part, size), BF16))
+    return places
+
+
+def land_in(places):
+    bits = len(places) // 2
+
+    def land(half, i, j):
+        return places[half * bits + i].at[j]
+
+    return land
+
+
+def put_half(out):
+    parts = cut(out.shape[-1])
+
+    def done(half, a, b):
+        start, size = parts[half]
+        add_into(out.at[(slice(None),) * (len(out.shape) - 1) + (pl.ds(start, size),)], a, b)
+
+    return done
+
+
+def back_kernel(sizes, partial, hidden, dy, g_in, g_down, resid, full, s_in, s_down, near, mine, left, right, low, *rest):
+    sems = rest[-1]
+    bits = sizes[1].bit_length() - 1
+    kit = Kit(sems, sizes)
+    kit.barrier()
+    total = kit.scatter_line(partial, resid, dy.shape[0], near, mine, left, right)
+    next(total)
+    t_in = kit.scatter_rep(column_blocks(g_in), land_in(rest[: 2 * bits]), put_half(s_in))
+    next(t_in)
+    t_down = kit.scatter_rep(column_blocks(g_down), land_in(rest[2 * bits : 4 * bits]), put_half(s_down))
+    next(t_down)
+    next(total)
+    for _ in range(kit.chips - 1):
+        next(total)
+    next(total)
+
+    def body(at):
+        h = hidden[at]
+        centred = h - jnp.mean(h, axis=-1, keepdims=True)
+        inv = lax.rsqrt(jnp.mean(centred * centred, axis=-1, keepdims=True) + eps)
+        d = dy[at].astype(F32) + norm_back(centred * inv, inv, resid[at])
+        resid[at] = d
+        low[at] = d.astype(BF16)
+
+    each(resid, body)
+    rows = kit.gather_line(low, full, low.shape[0])
+    next(rows)
+    finish_in_turn([t_in, rows, t_down, total])
+
+
+def back(sizes, partial, hidden, dy, g_in, g_down):
+    n, reps = sizes
+    rows, width = dy.shape
+    g_in = g_in.reshape(n, reps, g_in.shape[0] // (n * reps), g_in.shape[1])
+    g_down = g_down.reshape(reps, g_down.shape[0] // reps, g_down.shape[1])
+    lands = [VMEM((n // 2, rows, width), BF16) for _ in range(4)]
+    return call(
+        functools.partial(back_kernel, sizes),
+        [(partial, VMEM), (hidden, VMEM), (dy, VMEM), (g_in, VMEM), (g_down, VMEM)],
+        [
+            ((rows, width), F32, VMEM),
+            ((n * rows, width), BF16, ANY),
+            ((n,) + g_in.shape[2:], BF16, VMEM),
+            (g_down.shape[1:], BF16, VMEM),
+        ],
+        lands + [VMEM((rows, width), BF16)] + lands_of(g_in.shape, reps) + lands_of(g_down.shape, reps),
+        SEMS, 3, "back",
+    )
+
+
+def end_kernel(sizes, partial, s_in, s_down, g_qkv, g_out, total_out, o_in, o_down, o_qkv, o_out, near, mine, left, right, s_qkv, s_out, *rest):
+    sems = rest[-1]
+    bits = sizes[1].bit_length() - 1
+    kit = Kit(sems, sizes)
+    kit.barrier()
+    total = kit.scatter_line(partial, total_out, total_out.shape[0], near, mine, left, right)
+    next(total)
+    move_in = unshard(kit, s_in, o_in, 2)
+    next(move_in)
+    t_qkv = kit.scatter_rep(column_blocks(g_qkv), land_in(rest[: 2 * bits]), put_half(s_qkv))
+    next(t_qkv)
+    own_down = pltpu.make_async_copy(s_down, o_down.at[kit.rep], kit.sem())
+    own_down.start()
+    own_down.wait()
+    spread_down = kit.gather_rep(column_blocks(o_down))
+    next(spread_down)
+    next(total)
+    for _ in range(bits):
+        next(t_qkv)
+    move_qkv = unshard(kit, s_qkv, o_qkv, 3)
+    next(move_qkv)
+    next(total)
+    t_out = kit.scatter_rep(column_blocks(g_out), land_in(rest[2 * bits : 4 * bits]), put_half(s_out))
+    next(t_out)
+    next(spread_down)
+    next(total)
+    next(move_in)
+    spread_in = kit.gather_rep(column_blocks(o_in))
+    next(spread_in)
+    next(move_qkv)
+    spread_qkv = kit.gather_rep(column_blocks(o_qkv))
+    next(spread_qkv)
+    for _ in range(bits):
+        next(t_out)
+    own_out = pltpu.make_async_copy(s_out, o_out.at[kit.rep], kit.sem())
+    own_out.start()
+    own_out.wait()
+    spread_out = kit.gather_rep(column_blocks(o_out))
+    next(spread_out)
+    finish_in_turn([total, spread_in, spread_qkv, spread_out, spread_down, move_in, move_qkv, t_qkv, t_out])
+
+
+def end(sizes, partial, s_in, s_down, g_qkv, g_out):
+    n, reps = sizes
+    rows, width = partial.shape[0] // n, partial.shape[1]
+    g_qkv = g_qkv.reshape(n, reps, g_qkv.shape[0] // (n * reps), g_qkv.shape[1])
+    g_out = g_out.reshape(reps, g_out.shape[0] // reps, g_out.shape[1])
+    lands = [VMEM((n // 2, rows, width), BF16) for _ in range(4)]
+    total, o_in, o_down, o_qkv, o_out = call(
+        functools.partial(end_kernel, sizes),
+        [(partial, VMEM), (s_in, VMEM), (s_down, VMEM), (g_qkv, VMEM), (g_out, VMEM)],
+        [
+            ((rows, width), F32, VMEM),
+            ((reps, s_in.shape[1], n * s_in.shape[2]), BF16, ANY),
+            ((reps,) + s_down.shape, BF16, ANY),
+            ((reps, g_qkv.shape[2], n * g_qkv.shape[3]), BF16, ANY),
+            (g_out.shape, BF16, ANY),
+        ],
+        lands
+        + [VMEM((n,) + g_qkv.shape[2:], BF16), VMEM(g_out.shape[1:], BF16)]
+        + lands_of(g_qkv.shape, reps)
+        + lands_of(g_out.shape, reps),
+        SEMS, 4, "end",
+    )
+    return [total] + [o.reshape(-1, o.shape[-1]).astype(F32) for o in (o_in, o_down, o_qkv, o_out)]
+
+
 def gather_rows(block):
     return lax.all_gather(block, "fsdp", axis=0, tiled=True)
 
@@ -71,32 +755,6 @@
     return lax.psum_scatter(
         partial.astype(BF16), "fsdp", scatter_dimension=0, tiled=True
     ).astype(F32)
-
-
-def to_columns(weight, groups):
-    n = lax.axis_size("fsdp")
-    reps = lax.axis_size("rep")
-    depth, width = weight.shape
-    part = depth // reps
-    own = lax.dynamic_slice_in_dim(weight, lax.axis_index("rep") * part, part, 0)
-    own = own.reshape(part, groups, n, width // (groups * n))
-    sent = lax.all_to_all(own, "fsdp", split_axis=2, concat_axis=0, tiled=True)
-    sent = sent.reshape(n, part, width // n)
-    full = lax.all_gather(sent, "rep", axis=1, tiled=True)
-    return full.reshape(n * depth, width // n)
-
-
-def to_rows(grad, groups):
-    n = lax.axis_size("fsdp")
-    reps = lax.axis_size("rep")
-    depth, width = grad.shape
-    part = depth // (n * reps)
-    split = grad.astype(BF16).reshape(n, reps, part, width)
-    summed = lax.psum_scatter(split, "rep", scatter_dimension=1, tiled=True)
-    summed = summed.reshape(n, part, groups, width // groups)
-    moved = lax.all_to_all(summed, "fsdp", split_axis=0, concat_axis=0, tiled=True)
-    moved = moved.transpose(1, 2, 0, 3).reshape(part, n * width)
-    return lax.all_gather(moved, "rep", axis=0, tiled=True).astype(F32)
 
 
 def on_device(tokens, lengths, cotangent, w_qkv, w_out, w_in, w_down):
@@ -114,13 +772,13 @@
     positions = jnp.arange(slot_len, dtype=jnp.int32)
     cosine, sine = rotary_tables(positions, head_dim)
 
+    sizes = (n, lax.axis_size("rep"))
     x_rows = tokens[0].astype(F32)
     normed1, inv1 = normalize(x_rows)
-    n1_full = gather_rows(normed1.astype(BF16))
-    qkv_cols = to_columns(w_qkv, 3)
-    in_cols = to_columns(w_in, 2)
+    n1_full, qkv_cols = begin(sizes, normed1.astype(BF16), w_qkv)
     dy_rows = valid * cotangent[0].astype(F32)
-    dy_full = gather_rows(dy_rows.astype(BF16))
+    dy_low = dy_rows.astype(BF16)
+    dy_full = gather_rows(dy_low)
 
     qkv = dot(n1_full, qkv_cols)
     query = rotate(
@@ -141,9 +799,8 @@
     attended = jnp.einsum("hqk,khd->qhd", probs_low, values, preferred_element_type=F32)
     att_low = attended.reshape(slot_len, own_width).astype(BF16)
 
-    hidden_in = x_rows + scatter_rows(dot(att_low, w_out))
-    normed2, inv2 = normalize(hidden_in)
-    n2_full = gather_rows(normed2.astype(BF16))
+    out_partial = dot(att_low, w_out).astype(BF16)
+    hidden_in, n2_full, in_cols = middle(sizes, out_partial, tokens[0], w_in)
     gate_up = dot(n2_full, in_cols)
     units = gate_up.shape[1] // 2
     gate = gate_up[:, :units]
@@ -155,15 +812,16 @@
     d_gate = d_hidden * upper * sigma * (1.0 + gate * (1.0 - sigma))
     d_up = d_hidden * silu_gate
     dgu_low = jnp.concatenate([d_gate, d_up], axis=1).astype(BF16)
-    d_norm2 = scatter_rows(times_transpose(dgu_low, in_cols))
-    branch = scatter_rows(dot(act_low, w_down))
+    dn2_partial = times_transpose(dgu_low, in_cols).astype(BF16)
+    branch_partial = dot(act_low, w_down)
+    grad_down = over_rows(act_low, dy_full).astype(BF16)
+    grad_in = over_rows(n2_full, dgu_low).astype(BF16)
+    d_resid, dres_full, sum_in, sum_down = back(
+        sizes, dn2_partial, hidden_in, dy_low, grad_in, grad_down
+    )
+    branch = scatter_rows(branch_partial)
     output = (valid * (hidden_in + branch)).astype(BF16)
-    d_resid = dy_rows + norm_back(normed2, inv2, d_norm2)
-    dres_full = gather_rows(d_resid.astype(BF16))
-
-    grad_down = over_rows(act_low, dy_full)
-    grad_in = over_rows(n2_full, dgu_low)
-    grad_out = over_rows(att_low, dres_full)
+    grad_out = over_rows(att_low, dres_full).astype(BF16)
 
     datt = times_transpose(dres_full, w_out)
     datt_low = datt.astype(BF16).reshape(slot_len, heads, head_dim)
@@ -181,18 +839,13 @@
         ],
         axis=1,
     ).astype(BF16)
-    d_norm1 = scatter_rows(times_transpose(dqkv_low, qkv_cols))
+    dn1_partial = times_transpose(dqkv_low, qkv_cols).astype(BF16)
+    grad_qkv = over_rows(n1_full, dqkv_low).astype(BF16)
+    d_norm1, all_in, all_down, all_qkv, all_out = end(
+        sizes, dn1_partial, sum_in, sum_down, grad_qkv, grad_out
+    )
     grad_tokens = (d_resid + norm_back(normed1, inv1, d_norm1)).astype(BF16)
-    grad_qkv = over_rows(n1_full, dqkv_low)
-
-    return (
-        output[None],
-        grad_tokens[None],
-        to_rows(grad_qkv, 3),
-        lax.psum(grad_out.astype(BF16), "rep").astype(F32),
-        to_rows(grad_in, 2),
-        lax.psum(grad_down.astype(BF16), "rep").astype(F32),
-    )
+    return (output[None], grad_tokens[None], all_qkv, all_out, all_in, all_down)
 
 
 def solution(mesh):

time: 1210 us -> 852 us (0.70)
  waiting for transfers between devices: 758 us -> 0.04 us
  Pallas kernels: 0 us -> 651 us
  blocking collectives: 209 us -> 0 us
  local copies, waits for them, and re-layouts: 47.8 us -> 13 us
    pallas_call x0 -> x4, Pallas kernels: none -> 651 us  [call(): pl.pallas_call(body, out_shape=[jax.ShapeDtypeStruct(s, d) for s, d, _ in...]
    all_gather x4 -> x0, waiting for transfers between devices: 245 us -> none  [the longest x2 124 us: to_columns(): full = lax.all_gather(sent, 'rep', axis=1, tiled=True)]
    psum x1 -> x0, waiting for transfers between devices: 232 us -> none  [on_device(): lax.psum(grad_out.astype(BF16), 'rep').astype(F32)]
    all_to_all x4 -> x0, blocking collectives: 209 us -> none  [the longest x2 105 us: to_rows(): lax.all_to_all(summed, 'fsdp', split_axis=0, concat_axis=0, tiled=True)]
    all_gather x4 -> x1, waiting for transfers between devices: 177 us -> 0.01 us  [gather_rows(): return lax.all_gather(block, 'fsdp', axis=0, tiled=True)]
    reduce_scatter x4 -> x1, waiting for transfers between devices: 91.4 us -> 0.01 us  [scatter_rows(): lax.psum_scatter(partial.astype(BF16), 'fsdp', scatter_dimension=0, tiled...]
    reshape x8 -> x0, local copies, waits for them, and re-layouts: 15.8 us -> none  [the longest x2 6.16 us: to_columns(): sent = sent.reshape(n, part, width // n)]
    unnamed x15 -> x2, waiting for transfers between devices: 13.2 us -> 0.03 us
  transfers between devices with their start and end apart: 14 -> 2, of which waited for: 14 -> 0; matrix products, arithmetic and copies ran while one was open for 9% -> 10% of each run, Pallas kernels for 0% -> 63%
where the time goes in v2:
time: 852 us; the launch traced here: 842 us
  Pallas kernels  651 us (76%)
  matrix products  118 us (14%)
  other arithmetic  45.1 us (5%)
  between operations  15.6 us (2%)
  local copies, waits for them, and re-layouts  13 us (2%)
    pallas_call x4, Pallas kernels, call(): pl.pallas_call(body, out_shape=[jax.ShapeDtypeStruct(s, d) for s, d, _ in...  651 us
    dot_general x4, matrix products, times_transpose(): lax.dot_general(left, weight, (((1,), (1,)), ((), ())), preferred_element...  35.6 us
    dot_general x4, matrix products, over_rows(): lax.dot_general(left, right, (((0,), (0,)), ((), ())), preferred_element_...  32.5 us
    dot_general x4, matrix products, dot(): return jnp.dot(left, right, preferred_element_type=F32)  30.3 us
    convert_element_type x4, other arithmetic, end(): o.reshape(-1, o.shape[-1]).astype(F32)  22.8 us
  transfers between devices with their start and end apart: 2, of which 0 were waited for; matrix products, arithmetic and copies ran while one was open for 10% of the time, Pallas kernels for 63%

profile of v2, /device:TPU:8, one launch (start us, length us, event | category | flops | bytes accessed | tf_op | source)
XLA Modules:
  0.0 842.5 jit_solution(17699181786574677887)
XLA Ops:
  7.2 0.0 copy-start
  7.2 0.0 all-gather.2.cloned.1.call-start
  8.0 0.5 copy-done.22
  8.5 2.0 fusion.17.dy
  10.5 0.0 all-gather.2.cloned.1.call-update
  10.5 0.0 reduce-scatter.2.cloned.1.call-start
  10.6 1.2 convert_reduce_fusion
  11.8 1.3 fusion.16
  13.2 0.5 copy-done.20
  13.7 2.1 fusion.10.n1
  15.8 94.3 %begin.1 = (bf16[1024,2048]{1,0:T(8,128)(2,1)}, bf16[8,4,64,768]{3,2,1,0:T(8,128)(2,1)}) custom-call(bf16[128,2048]{1,0:T(8,128)(2,1)} %fusion.10.n1, bf16[256,6144]{1,0:T(8,128)(2,1)} %w_qkv.1), custom_call_target="tpu_custom_call" | custom-call | tf_op jit(solution)/shard_map/begin/pallas_call | solution.py:496
  110.1 6.2 fusion.36
  116.4 0.9 slice.83
  117.2 0.1 fusion.32
  117.4 0.1 fusion.33
  117.5 1.3 copy.62
  118.8 0.9 fusion.34
  119.7 2.4 copy.64
  122.0 1.3 copy.61
  123.3 1.3 copy.63
  124.7 3.0 fusion.20
  127.7 0.4 fusion.3
  128.0 2.7 subtract_convert_fusion.3
  130.8 2.3 fusion.1
  133.1 0.0 copy-start.16
  133.1 2.0 exponential_reduce_fusion
  135.1 1.4 copy-done.2
  136.5 3.5 fusion.35
  140.0 0.8 copy-done.13
  140.8 3.3 convolution_convert_fusion.2.partial
  144.1 170.4 %middle.1 = (f32[128,2048]{1,0:T(8,128)}, bf16[1024,2048]{1,0:T(8,128)(2,1)}, bf16[8,4,64,2048]{3,2,1,0:T(8,128)(2,1)}) custom-call(bf16[1024,2048]{1,0:T(8,128)(2,1)} %convolution_convert_fusion.2.partial, bf16[128,2048]{1,0:T(8,128)(2,1)} %bitcast.78, bf16[256,16384]{1,0:T(8,128)(2,1)} %w_in.1), custom_call_target="tpu_custom_call" | custom-call | tf_op jit(solution)/shard_map/middle/pallas_call | solution.py:496
  314.5 14.5 %fusion.37 = f32[1024,2048]{1,0:T(8,128)} fusion(bf16[1024,2048]{1,0:T(8,128)(2,1)} %get-tuple-element.23, bf16[2048,2048]{1,0:T(8,128)(2,1)} %bitcast.95), kind=kOutput, calls=%fused_computation.92 | convolution fusion | flops 8589934592 | bytes 20971520 | tf_op jit(solution)/shard_map/dot_general | solution.py:67
  329.0 14.0 %multiply_convert_fusion.2 = (bf16[1024,1024]{1,0:T(8,128)(2,1)}, bf16[1024,1024]{1,0:T(8,128)(2,1)}, bf16[1024,1024]{1,0:T(8,128)(2,1)S(1)}) fusion(f32[1024,2048]{1,0:T(8,128)} %fusion.37, bf16[1024,2048]{1,0:T(8,128)(2,1)} %all-gather.2.cloned.1.call-done, bf16[1024,2048]{1,0:T(8,128)(2,1)} %param.13), kind=kOutput, calls=%fused_computation.11 | convolution fusion | flops 4310695936 | bytes 23068672 | tf_op jit(solution)/shard_map/dot_general | solution.py:55
  343.0 12.7 %convolution_convert_fusion.1.partial = bf16[1024,2048]{1,0:T(8,128)(2,1)} fusion(bf16[2048,2048]{1,0:T(8,128)(2,1)S(1)} %bitcast.96, bf16[1024,1024]{1,0:T(8,128)(2,1)} %get-tuple-element.37, bf16[1024,1024]{1,0:T(8,128)(2,1)} %get-tuple-element.36), kind=kOutput, calls=%fused_computation.17 | convolution fusion | flops 8600420352 | bytes 16777216 | tf_op jit(solution)/shard_map/dot_general | solution.py:55
  355.6 14.2 %convolution_convert_fusion = bf16[2048,2048]{1,0:T(8,128)(2,1)} fusion(bf16[1024,2048]{1,0:T(8,128)(2,1)} %get-tuple-element.23, bf16[1024,1024]{1,0:T(8,128)(2,1)} %get-tuple-element.37, bf16[1024,1024]{1,0:T(8,128)(2,1)} %get-tuple-element.36), kind=kOutput, calls=%fused_computation.5 | convolution fusion | flops 8602517504 | bytes 16777216 | tf_op jit(solution)/shard_map/dot_general | solution.py:61
  369.9 6.3 convolution_convert_fusion.4
  376.1 116.8 %back.1 = (f32[128,2048]{1,0:T(8,128)}, bf16[1024,2048]{1,0:T(8,128)(2,1)}, bf16[8,64,2048]{2,1,0:T(8,128)(2,1)}, bf16[256,2048]{1,0:T(8,128)(2,1)}) custom-call(bf16[1024,2048]{1,0:T(8,128)(2,1)} %convolution_convert_fusion.1.partial, f32[128,2048]{1,0:T(8,128)} %get-tuple-element.22.hidden, bf16[128,2048]{1,0:T(8,128)(2,1)} %fusion.17.dy, ...), custom_call_target="tpu_custom_call" | custom-call | tf_op jit(solution)/shard_map/back/pallas_call | solution.py:496
  492.9 0.0 slice-start
  493.0 3.9 multiply_reduce_fusion
  496.9 0.0 slice-start.1
  496.9 6.9 convolution_convert_fusion.8
  503.8 3.4 multiply_convert_fusion
  507.3 1.3 fusion.4
  508.7 0.0 copy-start.12
  508.7 2.0 fusion.5
  510.6 0.7 subtract_convert_fusion.1
  511.4 0.6 pad_maximum_fusion.8
  512.0 0.2 copy.43
  512.2 0.2 copy.47
  512.4 0.0 copy-done.28
  512.4 7.6 convolution_convert_fusion.6
  520.0 5.0 convolution_convert_fusion.3.partial
  525.1 6.3 convolution_convert_fusion.5
  531.4 0.0 reduce-scatter.2.cloned.1.call-update
  531.4 1.0 copy-done.14
  532.4 4.4 convolution_convert_fusion.7
  536.8 269.3 %end.1 = (f32[128,2048]{1,0:T(8,128)}, bf16[4,64,16384]{2,1,0:T(8,128)(2,1)}, bf16[4,256,2048]{2,1,0:T(8,128)(2,1)}, bf16[4,64,6144]{2,1,0:T(8,128)(2,1)}, bf16[4,64,2048]{2,1,0:T(8,128)(2,1)}) custom-call(bf16[1024,2048]{1,0:T(8,128)(2,1)} %convolution_convert_fusion.3.partial, bf16[8,64,2048]{2,1,0:T(8,128)(2,1)} %get-tuple-element.27.s_in, ...), custom_call_target="tpu_custom_call" | custom-call | tf_op jit(solution)/shard_map/end/pallas_call | solution.py:496
  806.2 1.7 fusion.31
  807.9 2.8 bitcast_convert_fusion.3
  810.7 2.5 fusion.19
  813.2 4.7 bitcast_convert_fusion.1
  817.9 3.7 bitcast_convert_fusion.2
  821.6 11.6 %bitcast_convert_fusion = f32[256,16384]{1,0:T(8,128)} fusion(bf16[4,64,16384]{2,1,0:T(8,128)(2,1)} %get-tuple-element.32), kind=kLoop, calls=%fused_computation | loop fusion | flops 4194304 | bytes 25165824 | tf_op jit(solution)/shard_map/convert_element_type | solution.py:747
  833.2 2.0 fusion.18
  (67 shorter events, 0.2 us)
Async XLA Ops:
  7.2 133.7 %copy-start = (bf16[256,2048]{1,0:T(8,128)(2,1)S(1)}, bf16[256,2048]{1,0:T(8,128)(2,1)}, u32[]{:S(2)}) copy-start(bf16[256,2048]{1,0:T(8,128)(2,1)} %param.11) | copy-start | bytes 3145732
  7.2 321.8 %all-gather.2.cloned.1.call-start = ((), (), s32[]{:S(2)}) async-start(), calls=%async_computation.2 | async-start | bytes 4718592 | tf_op jit(solution)/shard_map/all_gather | solution.py:751
  8.0 0.5 copy-start.22
  10.5 822.7 %reduce-scatter.2.cloned.1.call-start = ((), (), s32[]{:S(2)}) async-start(), calls=%async_computation.1 | async-start | bytes 4718592 | tf_op jit(solution)/shard_map/reduce_scatter | solution.py:755
  11.8 1.3 copy-start.18
  13.1 0.5 copy-start.20
  130.7 2.3 copy-start.6
  130.7 2.3 copy-start.8
  130.8 2.3 copy-start.10
  133.1 3.4 copy-start.2
  133.1 3.4 copy-start.16
  140.0 0.8 copy-start.13
  329.0 14.0 %copy-start.24 = (bf16[8,4,64,2048]{3,2,1,0:T(8,128)(2,1)S(1)}, bf16[8,4,64,2048]{3,2,1,0:T(8,128)(2,1)}, u32[]{:S(2)}) copy-start(bf16[8,4,64,2048]{3,2,1,0:T(8,128)(2,1)} %get-tuple-element.24) | copy-start | bytes 25165828
  343.0 26.9 %copy-start.29 = (bf16[1024,1024]{1,0:T(8,128)(2,1)}, bf16[1024,1024]{1,0:T(8,128)(2,1)S(1)}, u32[]{:S(2)}) copy-start(bf16[1024,1024]{1,0:T(8,128)(2,1)S(1)} %get-tuple-element.38) | copy-start | bytes 6291460
  355.6 14.2 %copy-start.26 = (bf16[1024,2048]{1,0:T(8,128)(2,1)S(1)}, bf16[1024,2048]{1,0:T(8,128)(2,1)}, u32[]{:S(2)}) copy-start(bf16[1024,2048]{1,0:T(8,128)(2,1)} %all-gather.2.cloned.1.call-done) | copy-start | bytes 12582916
  492.9 10.9 %slice-start = ((s8[8388608]{0:T(1024)(128)(4,1)}), s8[4194304]{0:T(1024)(128)(4,1)S(1)}, s32[]{:S(2)}) async-start(s8[8388608]{0:T(1024)(128)(4,1)} %bitcast.79), calls=%async_computation.3 | async-start | bytes 8388608
  496.9 6.9 slice-start.1
  496.9 6.9 copy-start.17
  503.8 3.5 copy-start.9
  503.8 3.5 copy-start.11
  507.3 1.3 copy-start.7
  508.7 2.0 copy-start.12
  511.4 1.0 copy-start.28
  512.4 7.6 copy-start.27
  520.0 5.0 copy-start.25
  520.0 5.0 copy-start.30
  531.4 1.0 copy-start.14
  536.8 269.3 %copy-start.1 = (bf16[1,128,2048]{2,1,0:T(8,128)(2,1)S(1)}, bf16[1,128,2048]{2,1,0:T(8,128)(2,1)}, u32[]{:S(2)}) copy-start(bf16[1,128,2048]{2,1,0:T(8,128)(2,1)} %param.7) | copy-start | bytes 1572868
  536.8 269.3 %copy-start.19 = (f32[128]{0:T(128)S(1)}, f32[128]{0:T(128)}, u32[]{:S(2)}) copy-start(f32[128]{0:T(128)} %copy-done.18) | copy-start | bytes 1540
  536.8 269.3 %copy-start.21 = (f32[128]{0:T(128)S(1)}, f32[128]{0:T(128)}, u32[]{:S(2)}) copy-start(f32[128]{0:T(128)} %copy-done.20) | copy-start | bytes 1540
  536.8 273.9 %copy-start.15 = (f32[128,2048]{1,0:T(8,128)S(1)}, f32[128,2048]{1,0:T(8,128)}, u32[]{:S(2)}) copy-start(f32[128,2048]{1,0:T(8,128)} %get-tuple-element.25) | copy-start | bytes 3145732
  806.1 7.0 copy-start.3
  813.2 4.8 copy-start.5
  821.6 11.6 %copy-start.4 = (f32[128,2048]{1,0:T(8,128)S(1)}, f32[128,2048]{1,0:T(8,128)}, u32[]{:S(2)}) copy-start(f32[128,2048]{1,0:T(8,128)} %get-tuple-element.22.hidden) | copy-start | bytes 3145732
  821.6 11.6 %copy-start.23 = (f32[128]{0:T(128)S(1)}, f32[128]{0:T(128)}, u32[]{:S(2)}) copy-start(f32[128]{0:T(128)} %copy-done.22) | copy-start | bytes 1540
Sparse Core Ops, SparseCore 0:
  10.7 69.6 all-gather.1
  531.5 100.1 reduce-scatter.1

commit v3 on v2

--- a/solution.py
+++ b/solution.py
@@ -68,7 +68,7 @@
 
 
 MESH = pl.DeviceIdType.MESH
-LIMIT = 60 * 1024 * 1024
+LIMIT = 67043328
 
 
 class Kit:
@@ -85,6 +85,7 @@
 
     def sem(self):
         self.used += 1
+        assert self.used <= self.sems.shape[0], "semaphores"
         return self.sems.at[self.used - 1]
 
     def barrier(self, fsdp=True, rep=True):
@@ -177,7 +178,7 @@
                     shard = z - sign * k
                     self.copy(blk(shard, c), blk(shard, 1 - c), forwards[k - 1], fsdp=partner).wait_recv()
 
-    def scatter_line(self, partial, total, rows, near, mine, left, right):
+    def scatter_line(self, partial, total, rows, near, land, compute=None, stage=None):
         C, z, c = self.chips, self.chip, self.core
         partner = self.me ^ 1
 
@@ -197,50 +198,71 @@
             return self.copy(blk(d, 1 - c), near.at[d], near_sems[d], fsdp=partner)
 
         def to_right(d):
-            return self.copy(mine.at[d], right.at[d], right_sems[d], fsdp=2 * (z + 1) + c)
+            return self.copy(near.at[d], land.at[d], right_sems[d], fsdp=2 * (z + 1) + c)
 
         def to_left(d):
-            return self.copy(mine.at[d], left.at[d], left_sems[d], fsdp=2 * (z - 1) + c)
-
-        for d in order:
+            place = jnp.where(z - 1 == d, C, d)
+            return self.copy(near.at[d], land.at[place], left_sems[d], fsdp=2 * (z - 1) + c)
+
+        def arrived_left(d, last):
+            return self.copy(near.at[d], land.at[C if last else d], left_sems[d], fsdp=partner)
+
+        def settle(d):
+            own = blk(d, c)
+            if stage is not None:
+                load = pltpu.make_async_copy(own, stage, self.sem())
+                load.start()
+                load.wait()
+                own = stage
+            swap(d).wait_recv()
+            add_into(near.at[d], near.at[d], own)
+            if d > 0:
+                @pl.when(z == 0)
+                def _():
+                    to_right(d).start()
+            if d < C - 1:
+                @pl.when(z == C - 1)
+                def _():
+                    to_left(d).start()
+
+        for i, d in enumerate(order):
+            if compute is not None:
+                compute(d)
             swap(d).start()
+            if i > 0 and compute is not None:
+                settle(order[i - 1])
         yield
-        for d in order:
-            swap(d).wait_recv()
-            add_into(mine.at[d], blk(d, c), near.at[d])
-            @pl.when((z == 0) & (d > 0))
-            def _():
-                to_right(d).start()
-            @pl.when((z == C - 1) & (d < C - 1))
-            def _():
-                to_left(d).start()
+        for d in order if compute is None else order[-1:]:
+            settle(d)
         for j in range(C - 1):
             yield
             d = C - 1 - j
-            @pl.when((z > 0) & (z < d))
-            def _():
-                to_right(d).wait_recv()
-                add_into(mine.at[d], mine.at[d], right.at[d])
-                to_right(d).start()
+            if d > 1:
+                @pl.when((z > 0) & (z < d))
+                def _():
+                    to_right(d).wait_recv()
+                    add_into(near.at[d], near.at[d], land.at[d])
+                    to_right(d).start()
             e = j
-            @pl.when((z < C - 1) & (z > e))
-            def _():
-                to_left(e).wait_recv()
-                add_into(mine.at[e], mine.at[e], left.at[e])
-                to_left(e).start()
+            if e < C - 2:
+                @pl.when((z < C - 1) & (z > e))
+                def _():
+                    arrived_left(e, False).wait_recv()
+                    add_into(near.at[e], near.at[e], land.at[e])
+                    to_left(e).start()
         yield
-        keep(total, mine.at[z])
+        keep(total, near.at[z])
         for d in range(C):
             if d > 0:
                 @pl.when(z == d)
                 def _():
                     to_right(d).wait_recv()
-                    accumulate(total, right.at[d])
+                    accumulate(total, land.at[d])
             if d < C - 1:
                 @pl.when(z == d)
                 def _():
-                    to_left(d).wait_recv()
-                    accumulate(total, left.at[d])
+                    arrived_left(d, True).wait_recv()
+                    accumulate(total, land.at[C])
         yield
         for d in range(C):
             swap(d).wait_send()
@@ -293,7 +315,7 @@
         for cp in sent:
             cp.wait_send()
 
-    def scatter_rep(self, blk, land, done):
+    def scatter_rep(self, blk, land, done, stage=None):
         sent = []
         waits = {0: [], 1: []}
         nb = self.bits
@@ -326,6 +348,11 @@
                 yield
             for half in (0, 1):
                 for cp, ref, own in waits[half]:
+                    if stage is not None and i == 0:
+                        load = pltpu.make_async_copy(own, stage[half], self.sem())
+                        load.start()
+                        load.wait()
+                        own = stage[half]
                     cp.wait_recv()
                     if i < nb - 1:
                         add_into(ref, ref, own)
@@ -508,7 +535,6 @@
 
 ANY = pl.ANY
 VMEM = pltpu.VMEM
-SEMS = 200
 
 
 def begin_kernel(sizes, n1, w_qkv, n1_full, cols, stage, sems):
@@ -541,7 +567,7 @@
         [(n1, VMEM), (w_qkv, ANY)],
         [((n * rows, width), BF16, ANY), ((n, reps, part, own), BF16, ANY)],
         [VMEM((part, own), BF16)],
-        SEMS, 1, "begin",
+        20 * n, 1, "begin",
     )
     return full, cols.reshape(n * depth, own)
 
@@ -556,17 +582,20 @@
     each(dst, body)
 
 
-def middle_kernel(sizes, partial, x, w_in, hidden, n2_full, cols, near, mine, left, right, n2, stage, sems):
+def middle_kernel(sizes, partial, x, w_in, hidden, n2_full, cols, near, land, n2, stage, sems):
     kit = Kit(sems, sizes)
     kit.barrier()
-    total = kit.scatter_line(partial, hidden, x.shape[0], near, mine, left, right)
+    move = reshard(kit, w_in, cols, stage, 2)
+    next(move)
+    total = kit.scatter_line(partial, hidden, x.shape[0], near, land)
     next(total)
-    move = reshard(kit, w_in, cols, stage, 2)
     next(total)
     next(move)
+    spread = kit.gather_rep(column_blocks(cols))
+    next(spread)
     for _ in range(kit.chips - 1):
         next(total)
-    accumulated = next(total)
+    next(total)
 
     def body(at):
         hidden[at] = hidden[at] + x[at].astype(F32)
@@ -575,10 +604,11 @@
     norm_rows(n2, hidden)
     rows = kit.gather_line(n2, n2_full, n2.shape[0])
     next(rows)
-    next(move)
-    spread = kit.gather_rep(column_blocks(cols))
-    next(spread)
-    finish_in_turn([rows, spread, move, total])
+    finish_in_turn([spread, rows, move, total])
+
+
+def line_lands(n, rows, width):
+    return [VMEM((n // 2, rows, width), BF16), VMEM((n // 2 + 1, rows, width), BF16)]
 
 
 def middle(sizes, partial, x, w_in):
@@ -586,7 +616,7 @@
     rows, width = x.shape
     depth = w_in.shape[0]
     part, own = depth // reps, w_in.shape[1] // n
-    lands = [VMEM((n // 2, rows, width), BF16) for _ in range(4)]
+    lands = line_lands(n, rows, width)
     hidden, full, cols = call(
         functools.partial(middle_kernel, sizes),
         [(partial, VMEM), (x, VMEM), (w_in, ANY)],
@@ -596,7 +626,7 @@
             ((n, reps, part, own), BF16, ANY),
         ],
         lands + [VMEM((rows, width), BF16), VMEM((part, own), BF16)],
-        SEMS, 2, "middle",
+        24 * n, 2, "middle",
     )
     return hidden, full, cols.reshape(n * depth, own)
 
@@ -630,20 +660,64 @@
     return done
 
 
-def back_kernel(sizes, partial, hidden, dy, g_in, g_down, resid, full, s_in, s_down, near, mine, left, right, low, *rest):
+def times_tiles(left, at_rows, right, out, transposed, tile):
+    count = out.shape[1] // tile
+
+    def step(t, carry):
+        cols = pl.ds(pl.multiple_of(t * tile, tile), tile)
+        if transposed:
+            value = times_transpose(left[at_rows, :], right[cols, :])
+        else:
+            value = dot(left[at_rows, :], right[:, cols])
+        out[at_rows, cols] = value.astype(BF16)
+        return carry
+
+    lax.fori_loop(0, count, step, 0)
+
+
+def own_stages(shape):
+    return [VMEM(shape[:-3] + (shape[-2], size), BF16) for _, size in cut(shape[-1])]
+
+
+def load_all(kit, pairs):
+    copies = [pltpu.make_async_copy(src, dst, kit.sem()) for src, dst in pairs]
+    for cp in copies:
+        cp.start()
+    return copies
+
+
+def wait_all(copies):
+    for cp in copies:
+        cp.wait()
+
+
+def back_kernel(sizes, dgu_h, cols_h, act_h, down_h, hidden, dy, g_in, g_down, resid, out, full, s_in, s_down, dgu, cols, act, down, dn2, near, land, low, *rest):
     sems = rest[-1]
+    rows = dy.shape[0]
     bits = sizes[1].bit_length() - 1
     kit = Kit(sems, sizes)
+    loads = load_all(kit, [(dgu_h, dgu), (cols_h, cols)])
+    later = load_all(kit, [(act_h, act), (down_h, down)])
     kit.barrier()
-    total = kit.scatter_line(partial, resid, dy.shape[0], near, mine, left, right)
+    t_in = kit.scatter_rep(
+        column_blocks(g_in), land_in(rest[: 2 * bits]), put_half(s_in), rest[4 * bits : 4 * bits + 2]
+    )
+    next(t_in)
+    t_down = kit.scatter_rep(
+        column_blocks(g_down), land_in(rest[2 * bits : 4 * bits]), put_half(s_down), rest[4 * bits + 2 : 4 * bits + 4]
+    )
+    next(t_down)
+
+    def first(d):
+        times_tiles(dgu, pl.ds(d * 2 * rows, 2 * rows), cols, dn2, True, 256)
+
+    wait_all(loads)
+    total = kit.scatter_line(dn2, resid, rows, near, land, first)
     next(total)
-    t_in = kit.scatter_rep(column_blocks(g_in), land_in(rest[: 2 * bits]), put_half(s_in))
-    next(t_in)
-    t_down = kit.scatter_rep(column_blocks(g_down), land_in(rest[2 * bits : 4 * bits]), put_half(s_down))
-    next(t_down)
-    next(total)
-    for _ in range(kit.chips - 1):
+    wait_all(later)
+    for d in range(kit.chips):
         next(total)
+        times_tiles(act, pl.ds(d * 2 * rows, 2 * rows), down, out, False, 256)
     next(total)
 
     def body(at):
@@ -655,106 +729,235 @@
         low[at] = d.astype(BF16)
 
     each(resid, body)
-    rows = kit.gather_line(low, full, low.shape[0])
-    next(rows)
-    finish_in_turn([t_in, rows, t_down, total])
-
-
-def back(sizes, partial, hidden, dy, g_in, g_down):
+    line = kit.gather_line(low, full, rows)
+    next(line)
+    finish_in_turn([line, t_in, t_down, total])
+
+
+def back(sizes, dgu, in_cols, act, w_down, hidden, dy, g_in, g_down):
     n, reps = sizes
     rows, width = dy.shape
     g_in = g_in.reshape(n, reps, g_in.shape[0] // (n * reps), g_in.shape[1])
     g_down = g_down.reshape(reps, g_down.shape[0] // reps, g_down.shape[1])
-    lands = [VMEM((n // 2, rows, width), BF16) for _ in range(4)]
+    own = [(a, ANY) for a in (dgu, in_cols, act, w_down)]
     return call(
         functools.partial(back_kernel, sizes),
-        [(partial, VMEM), (hidden, VMEM), (dy, VMEM), (g_in, VMEM), (g_down, VMEM)],
+        own + [(hidden, VMEM), (dy, VMEM), (g_in, ANY), (g_down, ANY)],
         [
             ((rows, width), F32, VMEM),
+            ((n * rows, width), BF16, VMEM),
             ((n * rows, width), BF16, ANY),
             ((n,) + g_in.shape[2:], BF16, VMEM),
             (g_down.shape[1:], BF16, VMEM),
         ],
-        lands + [VMEM((rows, width), BF16)] + lands_of(g_in.shape, reps) + lands_of(g_down.shape, reps),
-        SEMS, 3, "back",
-    )
-
-
-def end_kernel(sizes, partial, s_in, s_down, g_qkv, g_out, total_out, o_in, o_down, o_qkv, o_out, near, mine, left, right, s_qkv, s_out, *rest):
-    sems = rest[-1]
-    bits = sizes[1].bit_length() - 1
-    kit = Kit(sems, sizes)
+        [VMEM(a.shape, a.dtype) for a, _ in own]
+        + [VMEM((n * rows, width), BF16)]
+        + line_lands(n, rows, width)
+        + [VMEM((rows, width), BF16)]
+        + lands_of(g_in.shape, reps)
+        + lands_of(g_down.shape, reps)
+        + own_stages(g_in.shape)
+        + own_stages(g_down.shape),
+        20 * n, 3, "back",
+    )
+
+
+def attend_back(q, k, v, datt, att, lse, length, acc_q, acc_k, acc_v):
+    slot, own = q.shape
+    heads = own // HEAD_DIM
+    size = min(256, slot)
+    scale = HEAD_DIM ** (-0.5)
+
+    def zero(at):
+        for acc in (acc_q, acc_k, acc_v):
+            acc[at] = jnp.zeros((16, own), F32)
+
+    each(acc_q, zero)
+    for head in range(heads):
+        cols = slice(head * HEAD_DIM, (head + 1) * HEAD_DIM)
+
+        def query_block(i, carry):
+            at = pl.ds(pl.multiple_of(i * size, size), size)
+            qb, db = q[at, cols], datt[at, cols]
+            delta = jnp.sum(db.astype(F32) * att[at, cols], axis=-1, keepdims=True)
+            level = lse[at, head : head + 1]
+            rows = i * size + lax.broadcasted_iota(jnp.int32, (size, size), 0)
+
+            def key_block(j, carry):
+                there = pl.ds(pl.multiple_of(j * size, size), size)
+                kb, vb = k[there, cols], v[there, cols]
+                keys = j * size + lax.broadcasted_iota(jnp.int32, (size, size), 1)
+                scores = times_transpose(qb, kb) * scale
+                scores = jnp.where((keys <= rows) & (keys < length), scores, neg_big)
+                probs = jnp.exp(scores - level)
+                grads = (probs * (times_transpose(db, vb) - delta)).astype(BF16)
+                acc_v[there, cols] = acc_v[there, cols] + over_rows(probs.astype(BF16), db)
+                acc_k[there, cols] = acc_k[there, cols] + over_rows(grads, qb)
+                acc_q[at, cols] = acc_q[at, cols] + dot(grads, kb)
+                return carry
+
+            return lax.fori_loop(0, i + 1, key_block, carry)
+
+        lax.fori_loop(0, slot // size, query_block, 0)
+
+
+def turn_back(acc, cosine, sine, out, start):
+    slot, own = acc.shape
+    scale = HEAD_DIM ** (-0.5)
+    size = 128
+
+    def step(i, carry):
+        at = pl.ds(pl.multiple_of(i * size, size), size)
+        for head in range(own // HEAD_DIM):
+            low = head * HEAD_DIM
+            value = acc[at, low : low + HEAD_DIM] * scale
+            turned = value * cosine[at, :] + pltpu.roll(value, HEAD_DIM // 2, 1) * sine[at, :]
+            out[at, start + low : start + low + HEAD_DIM] = turned.astype(BF16)
+        return carry
+
+    lax.fori_loop(0, slot // size, step, 0)
+
+
+def rows_tiles(left, right, out, tile):
+    def step(t, carry):
+        cols = pl.ds(pl.multiple_of(t * tile, tile), tile)
+        out[cols, :] = over_rows(left[:, cols], right[...]).astype(BF16)
+        return carry
+
+    lax.fori_loop(0, left.shape[1] // tile, step, 0)
+
+
+def end_kernel(sizes, *refs):
+    n, reps = sizes
+    bits = reps.bit_length() - 1
+    (length, dres_h, w_out_h, q_h, att_h, low_h, lse_h, cos_h, sin_h, cols_h, n1_h, part_h, s_in, s_down) = refs[:14]
+    total_out, branch, o_in, o_down, o_qkv, o_out = refs[14:20]
+    (dres, w_out, q, k, v, att, att_low, lse, cosine, sine, cols, n1, datt, acc_q, acc_k, acc_v, dqkv, g_qkv, g_out, dn1, near, land, near_b, land_b, stage, s_qkv, s_out) = refs[20:47]
+    rest = refs[47:]
+    rows = total_out.shape[0]
+    own = q.shape[1]
+    kit = Kit(rest[-1], sizes)
+    loads = load_all(
+        kit,
+        [(dres_h, dres), (w_out_h, w_out)]
+        + [(q_h.at[:, pl.ds(i * own, own)], ref) for i, ref in enumerate((q, k, v))]
+        + [(att_h, att), (lse_h, lse)],
+    )
+    later = load_all(
+        kit, [(low_h, att_low), (cos_h, cosine), (sin_h, sine), (cols_h, cols), (n1_h, n1)]
+    )
+    own_down = pltpu.make_async_copy(s_down, o_down.at[kit.rep], kit.sem())
+    own_down.start()
     kit.barrier()
-    total = kit.scatter_line(partial, total_out, total_out.shape[0], near, mine, left, right)
-    next(total)
     move_in = unshard(kit, s_in, o_in, 2)
     next(move_in)
-    t_qkv = kit.scatter_rep(column_blocks(g_qkv), land_in(rest[: 2 * bits]), put_half(s_qkv))
-    next(t_qkv)
-    own_down = pltpu.make_async_copy(s_down, o_down.at[kit.rep], kit.sem())
-    own_down.start()
     own_down.wait()
     spread_down = kit.gather_rep(column_blocks(o_down))
     next(spread_down)
+    wait_all(loads)
+
+    def project(i, carry):
+        at = pl.ds(pl.multiple_of(i * 2 * rows, 2 * rows), 2 * rows)
+        datt[at, :] = times_transpose(dres[at, :], w_out[...]).astype(BF16)
+        return carry
+
+    lax.fori_loop(0, kit.chips, project, 0)
+    attend_back(q, k, v, datt, att, lse, length[0], acc_q, acc_k, acc_v)
+    next(spread_down)
+    wait_all(later)
+    turn_back(acc_q, cosine, sine, dqkv, 0)
+    turn_back(acc_k, cosine, sine, dqkv, own)
+
+    def place(at):
+        dqkv[at + (pl.ds(2 * own, own),)] = acc_v[at].astype(BF16)
+
+    each(acc_v, place)
+    rows_tiles(n1, dqkv, g_qkv, 256)
+    parts = g_qkv.shape[0] // (n * reps)
+    t_qkv = kit.scatter_rep(
+        column_blocks(g_qkv.reshape(n, reps, parts, 3 * own)), land_in(rest[: 2 * bits]), put_half(s_qkv)
+    )
+    next(t_qkv)
+
+    def first(d):
+        times_tiles(dqkv, pl.ds(d * 2 * rows, 2 * rows), cols, dn1, True, 256)
+
+    total = kit.scatter_line(dn1, total_out, rows, near, land, first)
+    next(total)
+    rows_tiles(att_low, dres, g_out, 128)
+    t_out = kit.scatter_rep(
+        column_blocks(g_out.reshape(reps, g_out.shape[0] // reps, g_out.shape[1])),
+        land_in(rest[2 * bits : 4 * bits]),
+        put_half(s_out),
+    )
+    next(t_out)
+    next(total)
+    next(move_in)
+    spread_in = kit.gather_rep(column_blocks(o_in))
+    next(spread_in)
     next(total)
     for _ in range(bits):
         next(t_qkv)
     move_qkv = unshard(kit, s_qkv, o_qkv, 3)
     next(move_qkv)
-    next(total)
-    t_out = kit.scatter_rep(column_blocks(g_out), land_in(rest[2 * bits : 4 * bits]), put_half(s_out))
-    next(t_out)
-    next(spread_down)
-    next(total)
-    next(move_in)
-    spread_in = kit.gather_rep(column_blocks(o_in))
-    next(spread_in)
-    next(move_qkv)
-    spread_qkv = kit.gather_rep(column_blocks(o_qkv))
-    next(spread_qkv)
     for _ in range(bits):
         next(t_out)
     own_out = pltpu.make_async_copy(s_out, o_out.at[kit.rep], kit.sem())
     own_out.start()
+    for _ in range(kit.chips - 1):
+        next(total)
+    other = kit.scatter_line(part_h, branch, rows, near_b, land_b, stage=stage)
+    next(other)
     own_out.wait()
     spread_out = kit.gather_rep(column_blocks(o_out))
     next(spread_out)
-    finish_in_turn([total, spread_in, spread_qkv, spread_out, spread_down, move_in, move_qkv, t_qkv, t_out])
-
-
-def end(sizes, partial, s_in, s_down, g_qkv, g_out):
+    next(other)
+    next(move_qkv)
+    spread_qkv = kit.gather_rep(column_blocks(o_qkv))
+    next(spread_qkv)
+    finish_in_turn([other, spread_in, spread_qkv, spread_out, total, spread_down, move_in, move_qkv, t_qkv, t_out])
+
+
+def end(sizes, length, dres, w_out, qkv, att, att_low, lse, cosine, sine, cols, n1, part, s_in, s_down):
     n, reps = sizes
-    rows, width = partial.shape[0] // n, partial.shape[1]
-    g_qkv = g_qkv.reshape(n, reps, g_qkv.shape[0] // (n * reps), g_qkv.shape[1])
-    g_out = g_out.reshape(reps, g_out.shape[0] // reps, g_out.shape[1])
-    lands = [VMEM((n // 2, rows, width), BF16) for _ in range(4)]
-    total, o_in, o_down, o_qkv, o_out = call(
+    slot, width = dres.shape
+    rows, own = slot // n, w_out.shape[0]
+    g_qkv = (n, reps, width // (n * reps), 3 * own)
+    g_out = (reps, own // reps, width)
+    big = lambda *shape: VMEM(shape, BF16)
+    wide = lambda *shape: VMEM(shape, F32)
+    any_of = [(a, ANY) for a in (dres, w_out, qkv, att, att_low, lse, cosine, sine, cols, n1, part)]
+    total, branch, o_in, o_down, o_qkv, o_out = call(
         functools.partial(end_kernel, sizes),
-        [(partial, VMEM), (s_in, VMEM), (s_down, VMEM), (g_qkv, VMEM), (g_out, VMEM)],
+        [(length, pltpu.SMEM)] + any_of + [(s_in, VMEM), (s_down, VMEM)],
         [
+            ((rows, width), F32, VMEM),
             ((rows, width), F32, VMEM),
             ((reps, s_in.shape[1], n * s_in.shape[2]), BF16, ANY),
             ((reps,) + s_down.shape, BF16, ANY),
-            ((reps, g_qkv.shape[2], n * g_qkv.shape[3]), BF16, ANY),
-            (g_out.shape, BF16, ANY),
+            ((reps, g_qkv[2], n * g_qkv[3]), BF16, ANY),
+            (g_out, BF16, ANY),
         ],
-        lands
-        + [VMEM((n,) + g_qkv.shape[2:], BF16), VMEM(g_out.shape[1:], BF16)]
-        + lands_of(g_qkv.shape, reps)
-        + lands_of(g_out.shape, reps),
-        SEMS, 4, "end",
-    )
-    return [total] + [o.reshape(-1, o.shape[-1]).astype(F32) for o in (o_in, o_down, o_qkv, o_out)]
+        [big(slot, width), big(own, width), big(slot, own), big(slot, own), big(slot, own)]
+        + [wide(slot, own), big(slot, own), wide(slot, 128), wide(slot, 128), wide(slot, 128)]
+        + [big(width, 3 * own), big(slot, width), big(slot, own)]
+        + [wide(slot, own)] * 3
+        + [big(slot, 3 * own), big(width, 3 * own), big(own, width), big(slot, width)]
+        + line_lands(n, rows, width) * 2
+        + [big(rows, width), big(n, g_qkv[2], 3 * own), big(*g_out[1:])]
+        + lands_of(g_qkv, reps)
+        + lands_of(g_out, reps),
+        32 * n, 4, "end",
+    )
+    return [total, branch] + [o.reshape(-1, o.shape[-1]).astype(F32) for o in (o_in, o_down, o_qkv, o_out)]
+
+
+def after(value, *tokens):
+    return lax.optimization_barrier((value,) + tokens)[0]
 
 
 def gather_rows(block):
     return lax.all_gather(block, "fsdp", axis=0, tiled=True)
-
-
-def scatter_rows(partial):
-    return lax.psum_scatter(
-        partial.astype(BF16), "fsdp", scatter_dimension=0, tiled=True
-    ).astype(F32)
 
 
 def on_device(tokens, lengths, cotangent, w_qkv, w_out, w_in, w_down):
@@ -778,7 +981,7 @@
     n1_full, qkv_cols = begin(sizes, normed1.astype(BF16), w_qkv)
     dy_rows = valid * cotangent[0].astype(F32)
     dy_low = dy_rows.astype(BF16)
-    dy_full = gather_rows(dy_low)
+    dy_full = gather_rows(after(dy_low, n1_full))
 
     qkv = dot(n1_full, qkv_cols)
     query = rotate(
@@ -812,38 +1015,34 @@
     d_gate = d_hidden * upper * sigma * (1.0 + gate * (1.0 - sigma))
     d_up = d_hidden * silu_gate
     dgu_low = jnp.concatenate([d_gate, d_up], axis=1).astype(BF16)
-    dn2_partial = times_transpose(dgu_low, in_cols).astype(BF16)
-    branch_partial = dot(act_low, w_down)
     grad_down = over_rows(act_low, dy_full).astype(BF16)
     grad_in = over_rows(n2_full, dgu_low).astype(BF16)
-    d_resid, dres_full, sum_in, sum_down = back(
-        sizes, dn2_partial, hidden_in, dy_low, grad_in, grad_down
-    )
-    branch = scatter_rows(branch_partial)
+    d_resid, branch_partial, dres_full, sum_in, sum_down = back(
+        sizes, dgu_low, in_cols, act_low, w_down, hidden_in, dy_low, grad_in, grad_down
+    )
+
+    qkv_low = jnp.concatenate(
+        [m.reshape(slot_len, own_width) for m in (query, keys, values)], axis=1
+    )
+    level = jnp.pad(log_total[..., 0].T, ((0, 0), (0, 128 - heads)))
+    d_norm1, branch, all_in, all_down, all_qkv, all_out = end(
+        sizes,
+        lengths,
+        dres_full,
+        w_out,
+        qkv_low,
+        attended.reshape(slot_len, own_width),
+        att_low,
+        level,
+        jnp.concatenate([cosine, cosine], axis=1),
+        jnp.concatenate([sine, -sine], axis=1),
+        qkv_cols,
+        n1_full,
+        branch_partial,
+        sum_in,
+        sum_down,
+    )
     output = (valid * (hidden_in + branch)).astype(BF16)
-    grad_out = over_rows(att_low, dres_full).astype(BF16)
-
-    datt = times_transpose(dres_full, w_out)
-    datt_low = datt.astype(BF16).reshape(slot_len, heads, head_dim)
-    delta = jnp.sum(datt_low.astype(F32) * attended, axis=-1).T
-    d_probs = jnp.einsum("qhd,khd->hqk", datt_low, values, preferred_element_type=F32)
-    d_scores = (probs * (d_probs - delta[..., None])).astype(BF16)
-    dq = jnp.einsum("hqk,khd->qhd", d_scores, keys, preferred_element_type=F32) * scale
-    dk = jnp.einsum("hqk,qhd->khd", d_scores, query, preferred_element_type=F32) * scale
-    dv = jnp.einsum("hqk,qhd->khd", probs_low, datt_low, preferred_element_type=F32)
-    dqkv_low = jnp.concatenate(
-        [
-            rotate_back(dq, cosine, sine).reshape(slot_len, own_width),
-            rotate_back(dk, cosine, sine).reshape(slot_len, own_width),
-            dv.reshape(slot_len, own_width),
-        ],
-        axis=1,
-    ).astype(BF16)
-    dn1_partial = times_transpose(dqkv_low, qkv_cols).astype(BF16)
-    grad_qkv = over_rows(n1_full, dqkv_low).astype(BF16)
-    d_norm1, all_in, all_down, all_qkv, all_out = end(
-        sizes, dn1_partial, sum_in, sum_down, grad_qkv, grad_out
-    )
     grad_tokens = (d_resid + norm_back(normed1, inv1, d_norm1)).astype(BF16)
     return (output[None], grad_tokens[None], all_qkv, all_out, all_in, all_down)
 

time: 852 us -> 733 us (0.86)
  Pallas kernels: 651 us -> 576 us
  matrix products: 118 us -> 61.5 us
  local copies, waits for them, and re-layouts: 13 us -> 21.9 us
    pallas_call x4, Pallas kernels: 651 us -> 576 us  [call(): pl.pallas_call(body, out_shape=[jax.ShapeDtypeStruct(s, d) for s, d, _ in...]
    dot_general x4 -> x1, matrix products: 35.6 us -> 11.9 us  [times_transpose(): lax.dot_general(left, weight, (((1,), (1,)), ((), ())), preferred_element...]
    dot_general x4 -> x2, matrix products: 32.5 us -> 18 us  [over_rows(): lax.dot_general(left, right, (((0,), (0,)), ((), ())), preferred_element_...]
    dot_general x4 -> x0, matrix products: 13.6 us -> none  [the longest x1 6.87 us: on_device(): jnp.einsum('hqk,qhd->khd', probs_low, datt_low, preferred_element_type=F32)]
    dot_general x4 -> x3, matrix products: 30.3 us -> 22.8 us  [dot(): return jnp.dot(left, right, preferred_element_type=F32)]
  transfers between devices with their start and end apart: 2 -> 1, of which waited for: 0 -> 0; matrix products, arithmetic and copies ran while one was open for 10% -> 8% of each run, Pallas kernels for 63% -> 21%
where the time goes in v3:
time: 733 us; the launch traced here: 725 us
  Pallas kernels  576 us (79%)
  matrix products  61.5 us (8%)
  other arithmetic  49.3 us (7%)
  local copies, waits for them, and re-layouts  21.9 us (3%)
  between operations  15.5 us (2%)
    pallas_call x4, Pallas kernels, call(): pl.pallas_call(body, out_shape=[jax.ShapeDtypeStruct(s, d) for s, d, _ in...  576 us
    dot_general x3, matrix products, dot(): return jnp.dot(left, right, preferred_element_type=F32)  22.8 us
    convert_element_type x4, other arithmetic, end(): o.reshape(-1, o.shape[-1]).astype(F32)  21.7 us
    dot_general x2, matrix products, over_rows(): lax.dot_general(left, right, (((0,), (0,)), ((), ())), preferred_element_...  18 us
  transfers between devices with their start and end apart: 1, of which 0 were waited for; matrix products, arithmetic and copies ran while one was open for 8% of the time, Pallas kernels for 21%

profile of v3, /device:TPU:8, one launch (start us, length us, event | category | flops | bytes accessed | tf_op | source)
XLA Modules:
  0.0 724.7 jit_solution(3866191702867058325)
XLA Ops:
  7.2 0.0 all-gather.2.cloned.1.call-start
  7.9 1.2 convert_reduce_fusion
  9.1 1.3 fusion.15
  10.4 0.0 copy-start.21
  10.4 0.5 copy-done.21
  10.9 2.1 fusion.9.n1
  13.1 0.6 copy-done.23
  13.7 2.0 fusion.16.dy
  15.7 58.8 %begin.1 = (bf16[1024,2048]{1,0:T(8,128)(2,1)}, bf16[8,4,64,768]{3,2,1,0:T(8,128)(2,1)}) custom-call(bf16[128,2048]{1,0:T(8,128)(2,1)} %fusion.9.n1, bf16[256,6144]{1,0:T(8,128)(2,1)} %w_qkv.1), custom_call_target="tpu_custom_call" | custom-call | tf_op jit(solution)/shard_map/begin/pallas_call | solution.py:523
  74.5 0.0 all-gather.2.cloned.1.call-update
  74.5 6.3 fusion.26
  80.8 0.0 copy-start.12
  80.8 1.7 copy-done.12
  82.4 0.1 slice.36
  82.5 0.2 copy.59
  82.7 0.0 copy-start.6
  82.7 1.9 fusion.23
  84.7 0.9 fusion.24
  85.5 1.4 copy.63
  87.0 1.0 fusion.25
  88.0 1.4 copy.61
  89.4 1.0 copy.57
  90.4 1.3 copy.62
  91.7 2.4 copy.60
  94.1 3.0 fusion.19
  97.1 2.5 multiply_subtract_fusion
  99.5 0.6 maximum_convert_fusion
  100.2 0.4 fusion.3
  100.5 1.8 fusion
  102.4 0.0 copy-start.2
  102.4 0.0 copy-start.18
  102.4 2.2 exponential_reduce_fusion
  104.6 1.2 copy-done.2
  105.8 0.2 copy.54
  106.0 7.0 fusion.2
  113.0 1.6 copy.58.refs_4_
  114.6 0.0 copy-start.1
  114.6 0.1 convert_element_type.132.refs_5_
  114.7 0.0 copy-start.3
  114.7 1.0 pad.4.refs_6_
  115.7 3.3 convolution_convert_fusion.1.partial
  119.0 0.0 copy-done.1
  119.0 152.6 %middle.1 = (f32[128,2048]{1,0:T(8,128)}, bf16[1024,2048]{1,0:T(8,128)(2,1)}, bf16[8,4,64,2048]{3,2,1,0:T(8,128)(2,1)}) custom-call(bf16[1024,2048]{1,0:T(8,128)(2,1)} %convolution_convert_fusion.1.partial, bf16[128,2048]{1,0:T(8,128)(2,1)} %bitcast.63, bf16[256,16384]{1,0:T(8,128)(2,1)} %w_in.1), custom_call_target="tpu_custom_call" | custom-call | tf_op jit(solution)/shard_map/middle/pallas_call | solution.py:523
  271.6 0.0 copy-start.7
  271.6 3.0 pad_maximum_fusion.2
  274.7 1.1 copy_bitcast_fusion.1
  275.8 1.1 copy_bitcast_fusion
  276.9 1.3 pad_maximum_fusion.1.refs_3_
  278.1 13.2 %fusion.27 = f32[1024,2048]{1,0:T(8,128)} fusion(bf16[1024,2048]{1,0:T(8,128)(2,1)S(1)} %copy-done.25, bf16[2048,2048]{1,0:T(8,128)(2,1)} %bitcast.64), kind=kOutput, calls=%fused_computation.69 | convolution fusion | flops 8589934592 | bytes 20971520 | tf_op jit(solution)/shard_map/dot_general | solution.py:67
  291.4 11.9 %multiply_convert_fusion.2 = (bf16[1024,1024]{1,0:T(8,128)(2,1)S(1)}, bf16[1024,1024]{1,0:T(8,128)(2,1)S(1)}, bf16[1024,1024]{1,0:T(8,128)(2,1)S(1)}) fusion(f32[1024,2048]{1,0:T(8,128)} %fusion.27, bf16[1024,2048]{1,0:T(8,128)(2,1)} %all-gather.2.cloned.1.call-done, bf16[1024,2048]{1,0:T(8,128)(2,1)} %down_h.1), kind=kOutput, calls=%fused_computation.10 | convolution fusion | flops 4310695936 | bytes 23068672 | tf_op jit(solution)/shard_map/dot_general | solution.py:55
  303.3 0.0 copy-start.13
  303.3 11.8 %convolution_convert_fusion = bf16[2048,2048]{1,0:T(8,128)(2,1)} fusion(bf16[1024,2048]{1,0:T(8,128)(2,1)S(1)} %copy-done.26, bf16[1024,1024]{1,0:T(8,128)(2,1)S(1)} %get-tuple-element.43, bf16[1024,1024]{1,0:T(8,128)(2,1)S(1)} %get-tuple-element.42), kind=kOutput, calls=%fused_computation.4 | convolution fusion | flops 8602517504 | bytes 16777216 | tf_op jit(solution)/shard_map/dot_general | solution.py:61
  315.1 2.4 pad_maximum_fusion.dgu_h
  317.6 1.3 copy-done.24
  318.8 6.2 convolution_convert_fusion.2
  325.0 130.0 %back.1 = (f32[128,2048]{1,0:T(8,128)}, bf16[1024,2048]{1,0:T(8,128)(2,1)}, bf16[1024,2048]{1,0:T(8,128)(2,1)}, bf16[8,64,2048]{2,1,0:T(8,128)(2,1)}, bf16[256,2048]{1,0:T(8,128)(2,1)}) custom-call(bf16[1024,2048]{1,0:T(8,128)(2,1)} %pad_maximum_fusion.dgu_h, bf16[2048,2048]{1,0:T(8,128)(2,1)} %bitcast.65, bf16[1024,1024]{1,0:T(8,128)(2,1)} %copy-done.13, ...), custom_call_target="tpu_custom_call" | custom-call | tf_op jit(solution)/shard_map/back/pallas_call | solution.py:523
  455.0 235.0 %end.1 = (f32[128,2048]{1,0:T(8,128)}, f32[128,2048]{1,0:T(8,128)}, bf16[4,64,16384]{2,1,0:T(8,128)(2,1)}, bf16[4,256,2048]{2,1,0:T(8,128)(2,1)}, bf16[4,64,6144...) custom-call(s32[1]{0:T(128)} %copy.68.refs_0_, bf16[1024,2048]{1,0:T(8,128)(2,1)} %get-tuple-element.29.refs_1_, ...), custom_call_target="tpu_custom_call" | custom-call | tf_op jit(solution)/shard_map/end/pallas_call | solution.py:523
  690.0 2.6 fusion.17
  692.6 1.7 fusion.22
  694.4 1.6 bitcast_convert_fusion.3
  696.0 3.7 bitcast_convert_fusion.2
  699.6 4.7 bitcast_convert_fusion.1
  704.4 11.7 %bitcast_convert_fusion = f32[256,16384]{1,0:T(8,128)} fusion(bf16[4,64,16384]{2,1,0:T(8,128)(2,1)} %get-tuple-element.38), kind=kLoop, calls=%fused_computation | loop fusion | flops 4194304 | bytes 25165824 | tf_op jit(solution)/shard_map/convert_element_type | solution.py:952
  716.1 1.3 fusion.18
  (49 shorter events, 0.1 us)
Async XLA Ops:
  7.2 284.2 %all-gather.2.cloned.1.call-start = ((), (), s32[]{:S(2)}) async-start(), calls=%async_computation | async-start | bytes 4718592 | tf_op jit(solution)/shard_map/all_gather | solution.py:960
  9.1 1.3 copy-start.19
  10.4 0.5 copy-start.21
  13.1 0.6 copy-start.23
  80.8 1.7 copy-start.12
  82.7 6.7 copy-start.6
  97.1 3.1 copy-start.4
  97.1 3.1 copy-start.5
  100.1 2.2 copy-start.14
  100.2 2.2 copy-start.15
  102.4 3.4 copy-start.2
  102.4 3.6 copy-start.18
  113.0 2.7 copy-start.10
  114.6 4.3 copy-start.1
  114.7 4.3 copy-start.3
  271.6 5.2 copy-start.7
  271.6 6.5 copy-start.25
  291.4 12.0 %copy-start.26 = (bf16[1024,2048]{1,0:T(8,128)(2,1)S(1)}, bf16[1024,2048]{1,0:T(8,128)(2,1)}, u32[]{:S(2)}) copy-start(bf16[1024,2048]{1,0:T(8,128)(2,1)} %get-tuple-element.27) | copy-start | bytes 12582916
  303.3 14.2 %copy-start.13 = (bf16[1024,1024]{1,0:T(8,128)(2,1)}, bf16[1024,1024]{1,0:T(8,128)(2,1)S(1)}, u32[]{:S(2)}) copy-start(bf16[1024,1024]{1,0:T(8,128)(2,1)S(1)} %get-tuple-element.44.act_h) | copy-start | bytes 6291460
  315.1 3.7 copy-start.24
  690.0 4.4 copy-start.16
  690.0 6.0 copy-start.11
  696.0 3.7 copy-start.8
  704.4 11.7 %copy-start = (bf16[1,128,2048]{2,1,0:T(8,128)(2,1)S(1)}, bf16[1,128,2048]{2,1,0:T(8,128)(2,1)}, u32[]{:S(2)}) copy-start(bf16[1,128,2048]{2,1,0:T(8,128)(2,1)} %param.7) | copy-start | bytes 1572868
  704.4 11.7 %copy-start.9 = (f32[128,2048]{1,0:T(8,128)S(1)}, f32[128,2048]{1,0:T(8,128)}, u32[]{:S(2)}) copy-start(f32[128,2048]{1,0:T(8,128)} %get-tuple-element.35) | copy-start | bytes 3145732
  704.4 11.7 %copy-start.17 = (f32[128,2048]{1,0:T(8,128)S(1)}, f32[128,2048]{1,0:T(8,128)}, u32[]{:S(2)}) copy-start(f32[128,2048]{1,0:T(8,128)} %get-tuple-element.34) | copy-start | bytes 3145732
  704.4 11.7 %copy-start.20 = (f32[128]{0:T(128)S(1)}, f32[128]{0:T(128)}, u32[]{:S(2)}) copy-start(f32[128]{0:T(128)} %copy-done.19) | copy-start | bytes 1540
  704.4 11.7 %copy-start.22 = (f32[128]{0:T(128)S(1)}, f32[128]{0:T(128)}, u32[]{:S(2)}) copy-start(f32[128]{0:T(128)} %copy-done.21) | copy-start | bytes 1540
Sparse Core Ops, SparseCore 0:
  74.6 48.4 all-gather.1

commit v4 on v3

--- a/solution.py
+++ b/solution.py
@@ -34,21 +34,6 @@
     freqs = 10000.0 ** (-jnp.arange(half, dtype=F32) * 2.0 / head_dim)
     angles = positions.astype(F32)[:, None] * freqs[None, :]
     return (jnp.cos(angles), jnp.sin(angles))
-
-
-def rotate(values, cosine, sine):
-    half = values.shape[-1] // 2
-    first = values[..., :half]
-    second = values[..., half:]
-    cosine = cosine[:, None, :]
-    sine = sine[:, None, :]
-    return jnp.concatenate(
-        [first * cosine - second * sine, second * cosine + first * sine], axis=-1
-    )
-
-
-def rotate_back(grads, cosine, sine):
-    return rotate(grads, cosine, -sine)
 
 
 def times_transpose(left, weight):
@@ -537,39 +522,11 @@
 VMEM = pltpu.VMEM
 
 
-def begin_kernel(sizes, n1, w_qkv, n1_full, cols, stage, sems):
-    kit = Kit(sems, sizes)
-    kit.barrier()
-    move = reshard(kit, w_qkv, cols, stage, 3)
-    next(move)
-    rows = kit.gather_line(n1, n1_full, n1.shape[0])
-    next(rows)
-    next(move)
-    spread = kit.gather_rep(column_blocks(cols))
-    next(spread)
-    finish_in_turn([rows, spread, move])
-
-
 def finish_in_turn(tasks):
     tasks = list(tasks)
     done = object()
     while tasks:
         tasks = [t for t in tasks if next(t, done) is not done]
-
-
-def begin(sizes, n1, w_qkv):
-    n, reps = sizes
-    rows, width = n1.shape
-    depth = w_qkv.shape[0]
-    part, own = depth // reps, w_qkv.shape[1] // n
-    full, cols = call(
-        functools.partial(begin_kernel, sizes),
-        [(n1, VMEM), (w_qkv, ANY)],
-        [((n * rows, width), BF16, ANY), ((n, reps, part, own), BF16, ANY)],
-        [VMEM((part, own), BF16)],
-        20 * n, 1, "begin",
-    )
-    return full, cols.reshape(n * depth, own)
 
 
 def norm_rows(dst, src):
@@ -582,53 +539,8 @@
     each(dst, body)
 
 
-def middle_kernel(sizes, partial, x, w_in, hidden, n2_full, cols, near, land, n2, stage, sems):
-    kit = Kit(sems, sizes)
-    kit.barrier()
-    move = reshard(kit, w_in, cols, stage, 2)
-    next(move)
-    total = kit.scatter_line(partial, hidden, x.shape[0], near, land)
-    next(total)
-    next(total)
-    next(move)
-    spread = kit.gather_rep(column_blocks(cols))
-    next(spread)
-    for _ in range(kit.chips - 1):
-        next(total)
-    next(total)
-
-    def body(at):
-        hidden[at] = hidden[at] + x[at].astype(F32)
-
-    each(hidden, body)
-    norm_rows(n2, hidden)
-    rows = kit.gather_line(n2, n2_full, n2.shape[0])
-    next(rows)
-    finish_in_turn([spread, rows, move, total])
-
-
 def line_lands(n, rows, width):
     return [VMEM((n // 2, rows, width), BF16), VMEM((n // 2 + 1, rows, width), BF16)]
-
-
-def middle(sizes, partial, x, w_in):
-    n, reps = sizes
-    rows, width = x.shape
-    depth = w_in.shape[0]
-    part, own = depth // reps, w_in.shape[1] // n
-    lands = line_lands(n, rows, width)
-    hidden, full, cols = call(
-        functools.partial(middle_kernel, sizes),
-        [(partial, VMEM), (x, VMEM), (w_in, ANY)],
-        [
-            ((rows, width), F32, VMEM),
-            ((n * rows, width), BF16, ANY),
-            ((n, reps, part, own), BF16, ANY),
-        ],
-        lands + [VMEM((rows, width), BF16), VMEM((part, own), BF16)],
-        24 * n, 2, "middle",
-    )
-    return hidden, full, cols.reshape(n * depth, own)
 
 
 def lands_of(shape, reps):
@@ -689,6 +601,143 @@
 def wait_all(copies):
     for cp in copies:
         cp.wait()
+
+
+def project_qkv(n1, cols, cosine, sine, qkv):
+    slot, total = qkv.shape
+    own = total // 3
+    size = 256
+
+    def step(i, carry):
+        at = pl.ds(pl.multiple_of(i * size, size), size)
+        value = dot(n1[at, :], cols[...])
+        for low in range(0, 2 * own, HEAD_DIM):
+            part = value[:, low : low + HEAD_DIM]
+            turned = part * cosine[at, :] - pltpu.roll(part, HEAD_DIM // 2, 1) * sine[at, :]
+            qkv[at, low : low + HEAD_DIM] = turned.astype(BF16)
+        qkv[at, 2 * own :] = value[:, 2 * own :].astype(BF16)
+        return carry
+
+    lax.fori_loop(0, slot // size, step, 0)
+
+
+def attend(qkv, length, att, att_low, lse):
+    slot, own = att.shape
+    heads = own // HEAD_DIM
+    size = min(256, slot)
+    scale = HEAD_DIM ** (-0.5)
+    for i in range(slot // size):
+        at = slice(i * size, (i + 1) * size)
+        width = (i + 1) * size
+        rows = i * size + lax.broadcasted_iota(jnp.int32, (size, width), 0)
+        keys = lax.broadcasted_iota(jnp.int32, (size, width), 1)
+        allowed = (keys <= rows) & (keys < length)
+        for head in range(heads):
+            low = head * HEAD_DIM
+            q = qkv[at, low : low + HEAD_DIM]
+            k = qkv[:width, own + low : own + low + HEAD_DIM]
+            v = qkv[:width, 2 * own + low : 2 * own + low + HEAD_DIM]
+            scores = jnp.where(allowed, times_transpose(q, k) * scale, neg_big)
+            top = jnp.max(scores, axis=-1, keepdims=True)
+            level = top + jnp.log(jnp.sum(jnp.exp(scores - top), axis=-1, keepdims=True))
+            probs = jnp.exp(scores - level).astype(BF16)
+            value = dot(probs, v)
+            att[at, low : low + HEAD_DIM] = value
+            att_low[at, low : low + HEAD_DIM] = value.astype(BF16)
+            lse[at, head:] = jnp.broadcast_to(level, (size, 128 - head))
+
+
+def front_kernel(sizes, *refs):
+    (length, x, dy, w_qkv, w_in, w_out_h, cos_h, sin_h) = refs[:8]
+    (hidden, qkv, att, att_low, lse, n1_full, n2_full, dy_full, qkv_cols, in_cols) = refs[8:18]
+    (n_low, n1, cols, w_out, cosine, sine, partial, near, land, stage, stage_in, sems) = refs[18:]
+    kit = Kit(sems, sizes)
+    rows = x.shape[0]
+    loads = load_all(kit, [(w_out_h, w_out), (cos_h, cosine), (sin_h, sine)])
+
+    def widen(at):
+        hidden[at] = x[at].astype(F32)
+
+    each(hidden, widen)
+    norm_rows(n_low.at[0], hidden)
+    kit.barrier()
+    move = reshard(kit, w_qkv, qkv_cols, stage, 3)
+    next(move)
+    line = kit.gather_line(n_low.at[0], n1_full, rows)
+    next(line)
+    next(move)
+    spread = kit.gather_rep(column_blocks(qkv_cols))
+    next(spread)
+    finish_in_turn([line, spread, move])
+    move_in = reshard(kit, w_in, in_cols, stage_in, 2)
+    next(move_in)
+    n, reps, part, own = qkv_cols.shape
+    more = [(n1_full, n1)] + [
+        (qkv_cols.at[d, r], cols.at[pl.ds((d * reps + r) * part, part)]) for d in range(n) for r in range(reps)
+    ]
+    wait_all(loads + load_all(kit, more))
+    project_qkv(n1, cols, cosine, sine, qkv)
+    attend(qkv, length[0], att, att_low, lse)
+
+    def first(d):
+        times_tiles(att_low, pl.ds(d * 2 * rows, 2 * rows), w_out, partial, False, 256)
+
+    total = kit.scatter_line(partial, hidden, rows, near, land, first)
+    next(total)
+    next(total)
+    next(move_in)
+    spread_in = kit.gather_rep(column_blocks(in_cols))
+    next(spread_in)
+    for _ in range(kit.chips - 2):
+        next(total)
+    next(spread_in)
+    next(total)
+    next(total)
+
+    def body(at):
+        hidden[at] = hidden[at] + x[at].astype(F32)
+
+    each(hidden, body)
+    norm_rows(n_low.at[1], hidden)
+    gather = kit.gather_line(n_low.at[1], n2_full, rows)
+    next(gather)
+    other = kit.gather_line(dy, dy_full, rows)
+    next(other)
+    finish_in_turn([gather, other, spread_in, move_in, total])
+
+
+def front(sizes, length, x, dy, w_qkv, w_in, w_out, cosine, sine):
+    n, reps = sizes
+    rows, width = x.shape
+    slot = n * rows
+    depth = w_qkv.shape[0]
+    part, own_qkv, own_in = depth // reps, w_qkv.shape[1] // n, w_in.shape[1] // n
+    own = w_out.shape[0]
+    big = lambda *shape: VMEM(shape, BF16)
+    wide = lambda *shape: VMEM(shape, F32)
+    outs = call(
+        functools.partial(front_kernel, sizes),
+        [(length, pltpu.SMEM), (x, VMEM), (dy, VMEM)]
+        + [(a, ANY) for a in (w_qkv, w_in, w_out, cosine, sine)],
+        [
+            ((rows, width), F32, VMEM),
+            ((slot, 3 * own), BF16, VMEM),
+            ((slot, own), F32, VMEM),
+            ((slot, own), BF16, VMEM),
+            ((slot, 128), F32, VMEM),
+            ((slot, width), BF16, ANY),
+            ((slot, width), BF16, ANY),
+            ((slot, width), BF16, ANY),
+            ((n, reps, part, own_qkv), BF16, ANY),
+            ((n, reps, part, own_in), BF16, ANY),
+        ],
+        [big(2, rows, width), big(slot, width), big(n * depth, own_qkv), big(own, width)]
+        + [wide(slot, 128), wide(slot, 128), big(slot, width)]
+        + line_lands(n, rows, width)
+        + [big(part, own_qkv), big(part, own_in)],
+        64 * n, 1, "front",
+    )
+    return list(outs[:8]) + [o.reshape(n * depth, -1) for o in outs[8:]]
 
 
 def back_kernel(sizes, dgu_h, cols_h, act_h, down_h, hidden, dy, g_in, g_down, resid, out, full, s_in, s_down, dgu, cols, act, down, dn2, near, land, low, *rest):
@@ -762,7 +811,7 @@
     )
 
 
-def attend_back(q, k, v, datt, att, lse, length, acc_q, acc_k, acc_v):
+def attend_back(q, k, v, datt, att, lse, length, acc_q, acc_k, acc_v, between):
     slot, own = q.shape
     heads = own // HEAD_DIM
     size = min(256, slot)
@@ -799,6 +848,7 @@
             return lax.fori_loop(0, i + 1, key_block, carry)
 
         lax.fori_loop(0, slot // size, query_block, 0)
+        between(head)
 
 
 def turn_back(acc, cosine, sine, out, start):
@@ -862,8 +912,11 @@
         return carry
 
     lax.fori_loop(0, kit.chips, project, 0)
-    attend_back(q, k, v, datt, att, lse, length[0], acc_q, acc_k, acc_v)
-    next(spread_down)
+    def between(head):
+        if head == 0:
+            next(spread_down)
+
+    attend_back(q, k, v, datt, att, lse, length[0], acc_q, acc_k, acc_v, between)
     wait_all(later)
     turn_back(acc_q, cosine, sine, dqkv, 0)
     turn_back(acc_k, cosine, sine, dqkv, own)
@@ -883,6 +936,10 @@
         times_tiles(dqkv, pl.ds(d * 2 * rows, 2 * rows), cols, dn1, True, 256)
 
     total = kit.scatter_line(dn1, total_out, rows, near, land, first)
+    next(total)
+    next(move_in)
+    spread_in = kit.gather_rep(column_blocks(o_in))
+    next(spread_in)
     next(total)
     rows_tiles(att_low, dres, g_out, 128)
     t_out = kit.scatter_rep(
@@ -892,30 +949,29 @@
     )
     next(t_out)
     next(total)
-    next(move_in)
-    spread_in = kit.gather_rep(column_blocks(o_in))
-    next(spread_in)
-    next(total)
-    for _ in range(bits):
+    next(t_qkv)
+    for _ in range(kit.chips - 2):
+        next(total)
+    for _ in range(bits - 1):
         next(t_qkv)
     move_qkv = unshard(kit, s_qkv, o_qkv, 3)
     next(move_qkv)
+    next(spread_in)
     for _ in range(bits):
         next(t_out)
     own_out = pltpu.make_async_copy(s_out, o_out.at[kit.rep], kit.sem())
     own_out.start()
-    for _ in range(kit.chips - 1):
-        next(total)
     other = kit.scatter_line(part_h, branch, rows, near_b, land_b, stage=stage)
+    next(other)
+    next(total)
     next(other)
     own_out.wait()
     spread_out = kit.gather_rep(column_blocks(o_out))
     next(spread_out)
-    next(other)
     next(move_qkv)
     spread_qkv = kit.gather_rep(column_blocks(o_qkv))
     next(spread_qkv)
-    finish_in_turn([other, spread_in, spread_qkv, spread_out, total, spread_down, move_in, move_qkv, t_qkv, t_out])
+    finish_in_turn([other, spread_qkv, spread_out, spread_in, total, spread_down, move_in, move_qkv, t_qkv, t_out])
 
 
 def end(sizes, length, dres, w_out, qkv, att, att_low, lse, cosine, sine, cols, n1, part, s_in, s_down):
@@ -952,23 +1008,12 @@
     return [total, branch] + [o.reshape(-1, o.shape[-1]).astype(F32) for o in (o_in, o_down, o_qkv, o_out)]
 
 
-def after(value, *tokens):
-    return lax.optimization_barrier((value,) + tokens)[0]
-
-
-def gather_rows(block):
-    return lax.all_gather(block, "fsdp", axis=0, tiled=True)
-
-
 def on_device(tokens, lengths, cotangent, w_qkv, w_out, w_in, w_down):
     rows = tokens.shape[1]
     width = tokens.shape[2]
     n = lax.axis_size("fsdp")
     slot_len = rows * n
     head_dim = HEAD_DIM
-    own_width = width // n
-    heads = own_width // head_dim
-    scale = head_dim ** (-0.5)
     length = lengths[0]
     own_positions = lax.axis_index("fsdp") * rows + jnp.arange(rows, dtype=jnp.int32)
     valid = (own_positions < length).astype(F32)[:, None]
@@ -976,34 +1021,13 @@
     cosine, sine = rotary_tables(positions, head_dim)
 
     sizes = (n, lax.axis_size("rep"))
-    x_rows = tokens[0].astype(F32)
-    normed1, inv1 = normalize(x_rows)
-    n1_full, qkv_cols = begin(sizes, normed1.astype(BF16), w_qkv)
     dy_rows = valid * cotangent[0].astype(F32)
     dy_low = dy_rows.astype(BF16)
-    dy_full = gather_rows(after(dy_low, n1_full))
-
-    qkv = dot(n1_full, qkv_cols)
-    query = rotate(
-        qkv[:, :own_width].reshape(slot_len, heads, head_dim), cosine, sine
-    ).astype(BF16)
-    keys = rotate(
-        qkv[:, own_width : 2 * own_width].reshape(slot_len, heads, head_dim), cosine, sine
-    ).astype(BF16)
-    values = qkv[:, 2 * own_width :].reshape(slot_len, heads, head_dim).astype(BF16)
-    allowed = (positions[None, :] <= positions[:, None]) & (positions[None, :] < length)
-
-    raw = jnp.einsum("qhd,khd->hqk", query, keys, preferred_element_type=F32) * scale
-    scores = jnp.where(allowed[None], raw, neg_big)
-    top = jnp.max(scores, axis=-1, keepdims=True)
-    log_total = top + jnp.log(jnp.sum(jnp.exp(scores - top), axis=-1, keepdims=True))
-    probs = jnp.exp(scores - log_total)
-    probs_low = probs.astype(BF16)
-    attended = jnp.einsum("hqk,khd->qhd", probs_low, values, preferred_element_type=F32)
-    att_low = attended.reshape(slot_len, own_width).astype(BF16)
-
-    out_partial = dot(att_low, w_out).astype(BF16)
-    hidden_in, n2_full, in_cols = middle(sizes, out_partial, tokens[0], w_in)
+    turn_cos = jnp.concatenate([cosine, cosine], axis=1)
+    turn_sin = jnp.concatenate([sine, -sine], axis=1)
+    hidden_in, qkv_low, attended, att_low, level, n1_full, n2_full, dy_full, qkv_cols, in_cols = front(
+        sizes, lengths, tokens[0], dy_low, w_qkv, w_in, w_out, turn_cos, turn_sin
+    )
     gate_up = dot(n2_full, in_cols)
     units = gate_up.shape[1] // 2
     gate = gate_up[:, :units]
@@ -1021,21 +1045,17 @@
         sizes, dgu_low, in_cols, act_low, w_down, hidden_in, dy_low, grad_in, grad_down
     )
 
-    qkv_low = jnp.concatenate(
-        [m.reshape(slot_len, own_width) for m in (query, keys, values)], axis=1
-    )
-    level = jnp.pad(log_total[..., 0].T, ((0, 0), (0, 128 - heads)))
     d_norm1, branch, all_in, all_down, all_qkv, all_out = end(
         sizes,
         lengths,
         dres_full,
         w_out,
         qkv_low,
-        attended.reshape(slot_len, own_width),
+        attended,
         att_low,
         level,
-        jnp.concatenate([cosine, cosine], axis=1),
-        jnp.concatenate([sine, -sine], axis=1),
+        turn_cos,
+        turn_sin,
         qkv_cols,
         n1_full,
         branch_partial,
@@ -1043,6 +1063,7 @@
         sum_down,
     )
     output = (valid * (hidden_in + branch)).astype(BF16)
+    normed1, inv1 = normalize(tokens[0].astype(F32))
     grad_tokens = (d_resid + norm_back(normed1, inv1, d_norm1)).astype(BF16)
     return (output[None], grad_tokens[None], all_qkv, all_out, all_in, all_down)
 

time: 733 us -> 659 us (0.90)
  local copies, waits for them, and re-layouts: 21.9 us -> 0.06 us
  matrix products: 61.5 us -> 41.4 us
  other arithmetic: 49.3 us -> 31.2 us
  between operations: 15.5 us -> 1.91 us
    unnamed x59 -> x30, local copies, waits for them, and re-layouts: 12 us -> 0.06 us
    dot_general x2 -> x0, matrix products: 8.78 us -> none  [the longest x1 6.98 us: on_device(): jnp.einsum('hqk,khd->qhd', probs_low, values, preferred_element_type=F32)]
    dot_general x3 -> x1, matrix products: 22.8 us -> 14.6 us  [dot(): return jnp.dot(left, right, preferred_element_type=F32)]
    pallas_call x4 -> x3, Pallas kernels: 576 us -> 577 us  [call(): pl.pallas_call(body, out_shape=[jax.ShapeDtypeStruct(s, d) for s, d, _ in...]
  transfers between devices with their start and end apart: 1 -> 0, of which waited for: 0 -> 0; matrix products, arithmetic and copies ran while one was open for 8% -> 0% of each run, Pallas kernels for 21% -> 0%
where the time goes in v4:
time: 659 us; the launch traced here: 652 us
  Pallas kernels  577 us (88%)
  matrix products  41.4 us (6%)
  other arithmetic  31.2 us (5%)
    pallas_call x3, Pallas kernels, call(): pl.pallas_call(body, out_shape=[jax.ShapeDtypeStruct(s, d) for s, d, _ in...  577 us
    convert_element_type x4, other arithmetic, end(): o.reshape(-1, o.shape[-1]).astype(F32)  21.7 us
    dot_general x2, matrix products, over_rows(): lax.dot_general(left, right, (((0,), (0,)), ((), ())), preferred_element_...  18 us
    dot_general x1, matrix products, dot(): return jnp.dot(left, right, preferred_element_type=F32)  14.6 us

profile of v4, /device:TPU:8, one launch (start us, length us, event | category | flops | bytes accessed | tf_op | source)
XLA Modules:
  0.0 651.8 jit_solution(3107157785653703378)
XLA Ops:
  0.6 0.0 copy-start.10
  0.7 1.9 multiply_sine_fusion
  2.6 1.3 pad_maximum_fusion.1
  4.6 0.0 copy-done.10
  4.6 0.0 copy-start.11
  4.6 0.9 fusion.11.refs_2_.dy
  5.5 0.0 copy-done.11
  5.5 229.0 %front.1 = (f32[128,2048]{1,0:T(8,128)}, bf16[1024,768]{1,0:T(8,128)(2,1)}, f32[1024,256]{1,0:T(8,128)}, bf16[1024,256]{1,0:T(8,128)(2,1)}, f32[1024,128]{1,0:T(...) custom-call(s32[1]{0:T(128)} %copy.16.refs_0_, ...), custom_call_target="tpu_custom_call" | custom-call | tf_op jit(solution)/shard_map/front/pallas_call | solution.py:508
  234.5 0.0 copy-start.4
  234.6 0.0 copy-start.14
  234.6 14.6 %fusion.16 = f32[1024,2048]{1,0:T(8,128)} fusion(bf16[1024,2048]{1,0:T(8,128)(2,1)} %get-tuple-element.29, bf16[2048,2048]{1,0:T(8,128)(2,1)} %bitcast.38), kind=kOutput, calls=%fused_computation.42 | convolution fusion | flops 8589934592 | bytes 20971520 | tf_op jit(solution)/shard_map/dot_general | solution.py:52
  249.2 0.0 copy-done.4
  249.2 0.0 copy-done.14
  249.2 8.7 %multiply_convert_fusion.2 = (bf16[1024,1024]{1,0:T(8,128)(2,1)S(1)}, bf16[1024,1024]{1,0:T(8,128)(2,1)S(1)}, bf16[1024,1024]{1,0:T(8,128)(2,1)S(1)}) fusion(f32[1024,2048]{1,0:T(8,128)} %fusion.16, bf16[1024,2048]{1,0:T(8,128)(2,1)S(1)} %copy-done.14, bf16[1024,2048]{1,0:T(8,128)(2,1)S(1)} %copy-done.4), kind=kOutput, calls=%fused_computation.6 | convolution fusion | flops 4310695936 | bytes 23068672 | tf_op jit(solution)/shard_map/dot_general | solution.py:40
  257.9 0.0 copy-start.6
  257.9 0.0 copy-start.13
  257.9 6.2 convolution_convert_fusion.1
  264.2 0.0 copy-done.6
  264.2 0.0 copy-done.13
  264.2 11.8 %convolution_convert_fusion = bf16[2048,2048]{1,0:T(8,128)(2,1)} fusion(bf16[1024,2048]{1,0:T(8,128)(2,1)S(1)} %copy-done.13, bf16[1024,1024]{1,0:T(8,128)(2,1)S(1)} %get-tuple-element.51, bf16[1024,1024]{1,0:T(8,128)(2,1)S(1)} %get-tuple-element.50), kind=kOutput, calls=%fused_computation.1 | convolution fusion | flops 8602517504 | bytes 16777216 | tf_op jit(solution)/shard_map/dot_general | solution.py:46
  276.0 2.3 pad_maximum_fusion.dgu_h
  278.3 130.7 %back.1 = (f32[128,2048]{1,0:T(8,128)}, bf16[1024,2048]{1,0:T(8,128)(2,1)}, bf16[1024,2048]{1,0:T(8,128)(2,1)}, bf16[8,64,2048]{2,1,0:T(8,128)(2,1)}, bf16[256,2048]{1,0:T(8,128)(2,1)}) custom-call(bf16[1024,2048]{1,0:T(8,128)(2,1)} %pad_maximum_fusion.dgu_h, bf16[2048,2048]{1,0:T(8,128)(2,1)} %bitcast.39, bf16[1024,1024]{1,0:T(8,128)(2,1)} %copy-done.6, ...), custom_call_target="tpu_custom_call" | custom-call | tf_op jit(solution)/shard_map/back/pallas_call | solution.py:508
  409.0 217.6 %end.1 = (f32[128,2048]{1,0:T(8,128)}, f32[128,2048]{1,0:T(8,128)}, bf16[4,64,16384]{2,1,0:T(8,128)(2,1)}, bf16[4,256,2048]{2,1,0:T(8,128)(2,1)}, bf16[4,64,6144...) custom-call(s32[1]{0:T(128)} %copy.16.refs_0_, bf16[1024,2048]{1,0:T(8,128)(2,1)} %get-tuple-element.31.refs_1_, ...), custom_call_target="tpu_custom_call" | custom-call | tf_op jit(solution)/shard_map/end/pallas_call | solution.py:508
  626.6 0.0 copy-start.1
  626.6 11.7 %bitcast_convert_fusion = f32[256,16384]{1,0:T(8,128)} fusion(bf16[4,64,16384]{2,1,0:T(8,128)(2,1)} %get-tuple-element.46), kind=kLoop, calls=%fused_computation | loop fusion | flops 4194304 | bytes 25165824 | tf_op jit(solution)/shard_map/convert_element_type | solution.py:1008
  638.3 0.0 copy-done.1
  638.3 0.0 copy-start.5
  638.3 4.7 bitcast_convert_fusion.1
  643.1 0.0 copy-done.5
  643.1 0.0 copy-start.7
  643.1 0.0 copy-start
  643.1 3.7 bitcast_convert_fusion.2
  646.7 0.0 copy-start.3
  646.7 0.0 copy-start.9
  646.7 0.0 copy-done.7
  646.7 0.0 copy-start.2
  646.7 0.0 copy-start.8
  646.8 0.0 copy-start.12
  646.8 1.6 bitcast_convert_fusion.3
  648.4 0.0 copy-done
  648.4 0.2 convert_reduce_fusion
  648.6 0.3 fusion.10
  648.9 0.0 copy-done.3
  648.9 0.3 fusion.15
  649.2 0.0 copy-done.9
  649.2 1.2 fusion.13
  650.5 0.0 copy-done.2
  650.5 0.0 copy-done.8
  650.5 0.0 copy-done.12
  650.5 0.9 fusion.12
  (7 shorter events, 0.0 us)
Async XLA Ops:
  0.6 3.9 copy-start.10
  4.6 1.0 copy-start.11
  234.5 14.6 %copy-start.4 = (bf16[1024,2048]{1,0:T(8,128)(2,1)S(1)}, bf16[1024,2048]{1,0:T(8,128)(2,1)}, u32[]{:S(2)}) copy-start(bf16[1024,2048]{1,0:T(8,128)(2,1)} %down_h.1) | copy-start | bytes 12582916
  234.6 14.6 %copy-start.14 = (bf16[1024,2048]{1,0:T(8,128)(2,1)S(1)}, bf16[1024,2048]{1,0:T(8,128)(2,1)}, u32[]{:S(2)}) copy-start(bf16[1024,2048]{1,0:T(8,128)(2,1)} %get-tuple-element.28) | copy-start | bytes 12582916
  257.9 6.2 copy-start.6
  257.9 6.2 copy-start.13
  626.6 11.7 %copy-start.1 = (bf16[4,256,2048]{2,1,0:T(8,128)(2,1)S(1)}, bf16[4,256,2048]{2,1,0:T(8,128)(2,1)}, u32[]{:S(2)}) copy-start(bf16[4,256,2048]{2,1,0:T(8,128)(2,1)} %get-tuple-element.47) | copy-start | bytes 12582916
  638.3 4.8 copy-start.5
  643.1 3.7 copy-start.7
  643.1 5.3 copy-start
  646.7 2.1 copy-start.3
  646.7 2.5 copy-start.9
  646.7 3.7 copy-start.2
  646.7 3.7 copy-start.8
  646.8 3.7 copy-start.12

commit v5 on v4

--- a/solution.py
+++ b/solution.py
@@ -352,13 +352,16 @@
 
 def each(ref, body):
     lead = ref.shape[:-2]
-    count = ref.shape[-2] // 16
+    height = 16
+    while height * ref.shape[-1] < 16 * 2048 and ref.shape[-2] % (2 * height) == 0:
+        height *= 2
+    count = ref.shape[-2] // height
     total = count
     for size in lead:
         total *= size
 
     def step(t, carry):
-        rows = pl.ds(pl.multiple_of((t % count) * 16, 16), 16)
+        rows = pl.ds(pl.multiple_of((t % count) * height, height), height)
         rest = t // count
         index = []
         for size in reversed(lead):
@@ -473,18 +476,19 @@
     finish(move)
 
 
-def unshard(kit, sums, out, groups):
+def unshard(kit, sums, out, groups, only=None):
     n, part, total = sums.shape
     width = total // groups
+    chosen = range(groups) if only is None else (only,)
 
     def target(g, d):
         return out.at[kit.rep, :, column_slice(g * (width * n) + d * width, width)]
 
     def pieces(d):
-        return [(sums.at[d, :, pl.ds(g * width, width)], target(g, kit.me)) for g in range(groups)]
+        return [(sums.at[d, :, pl.ds(g * width, width)], target(g, kit.me)) for g in chosen]
 
     def arrivals(d):
-        return [(sums.at[d, :, pl.ds(g * width, width)], target(g, d)) for g in range(groups)]
+        return [(sums.at[d, :, pl.ds(g * width, width)], target(g, d)) for g in chosen]
 
     own = [
         pltpu.make_async_copy(src, dst, kit.sem()) for src, dst in pieces(kit.me)
@@ -585,10 +589,6 @@
         return carry
 
     lax.fori_loop(0, count, step, 0)
-
-
-def own_stages(shape):
-    return [VMEM(shape[:-3] + (shape[-2], size), BF16) for _, size in cut(shape[-1])]
 
 
 def load_all(kit, pairs):
@@ -648,9 +648,9 @@
 
 
 def front_kernel(sizes, *refs):
-    (length, x, dy, w_qkv, w_in, w_out_h, cos_h, sin_h) = refs[:8]
-    (hidden, qkv, att, att_low, lse, n1_full, n2_full, dy_full, qkv_cols, in_cols) = refs[8:18]
-    (n_low, n1, cols, w_out, cosine, sine, partial, near, land, stage, stage_in, sems) = refs[18:]
+    (length, x, w_qkv, w_in, w_out_h, cos_h, sin_h) = refs[:7]
+    (hidden, qkv, att, att_low, lse, n1_full, n2_full, qkv_cols, in_cols) = refs[7:16]
+    (n_low, n1, cols, w_out, cosine, sine, partial, near, land, stage, stage_in, sems) = refs[16:]
     kit = Kit(sems, sizes)
     rows = x.shape[0]
     loads = load_all(kit, [(w_out_h, w_out), (cos_h, cosine), (sin_h, sine)])
@@ -701,12 +701,10 @@
     norm_rows(n_low.at[1], hidden)
     gather = kit.gather_line(n_low.at[1], n2_full, rows)
     next(gather)
-    other = kit.gather_line(dy, dy_full, rows)
-    next(other)
-    finish_in_turn([gather, other, spread_in, move_in, total])
-
-
-def front(sizes, length, x, dy, w_qkv, w_in, w_out, cosine, sine):
+    finish_in_turn([gather, spread_in, move_in, total])
+
+
+def front(sizes, length, x, w_qkv, w_in, w_out, cosine, sine):
     n, reps = sizes
     rows, width = x.shape
     slot = n * rows
@@ -717,7 +715,7 @@
     wide = lambda *shape: VMEM(shape, F32)
     outs = call(
         functools.partial(front_kernel, sizes),
-        [(length, pltpu.SMEM), (x, VMEM), (dy, VMEM)]
+        [(length, pltpu.SMEM), (x, VMEM)]
         + [(a, ANY) for a in (w_qkv, w_in, w_out, cosine, sine)],
         [
             ((rows, width), F32, VMEM),
@@ -725,7 +723,6 @@
             ((slot, own), F32, VMEM),
             ((slot, own), BF16, VMEM),
             ((slot, 128), F32, VMEM),
-            ((slot, width), BF16, ANY),
             ((slot, width), BF16, ANY),
             ((slot, width), BF16, ANY),
             ((n, reps, part, own_qkv), BF16, ANY),
@@ -737,36 +734,107 @@
         + [big(part, own_qkv), big(part, own_in)],
         64 * n, 1, "front",
     )
-    return list(outs[:8]) + [o.reshape(n * depth, -1) for o in outs[8:]]
-
-
-def back_kernel(sizes, dgu_h, cols_h, act_h, down_h, hidden, dy, g_in, g_down, resid, out, full, s_in, s_down, dgu, cols, act, down, dn2, near, land, low, *rest):
-    sems = rest[-1]
+    return list(outs[:7]) + [o.reshape(n * depth, -1) for o in outs[7:]]
+
+
+def gated(n2, cols, at, act, slopes):
+    units = act.shape[1]
+    tile = 256
+
+    def step(t, carry):
+        low = pl.ds(pl.multiple_of(t * tile, tile), tile)
+        high = pl.ds(pl.multiple_of(units + t * tile, tile), tile)
+        gate = dot(n2[at, :], cols[:, low])
+        upper = dot(n2[at, :], cols[:, high])
+        sigma = 1.0 / (1.0 + jnp.exp(-gate))
+        silu_gate = gate * sigma
+        act[at, low] = (silu_gate * upper).astype(BF16)
+        slopes[at, low] = (upper * sigma * (1.0 + gate * (1.0 - sigma))).astype(BF16)
+        slopes[at, high] = silu_gate.astype(BF16)
+        return carry
+
+    lax.fori_loop(0, units // tile, step, 0)
+
+
+def gated_back(dy, down, at, dgu):
+    units = down.shape[0]
+    tile = 256
+
+    def step(t, carry):
+        low = pl.ds(pl.multiple_of(t * tile, tile), tile)
+        high = pl.ds(pl.multiple_of(units + t * tile, tile), tile)
+        value = times_transpose(dy[at, :], down[low, :])
+        dgu[at, low] = (value * dgu[at, low].astype(F32)).astype(BF16)
+        dgu[at, high] = (value * dgu[at, high].astype(F32)).astype(BF16)
+        return carry
+
+    lax.fori_loop(0, units // tile, step, 0)
+
+
+def back_kernel(sizes, *refs):
+    (n2_h, cols_h, down_h, hidden, dy) = refs[:5]
+    (resid, branch_h, dy_full, full, s_in, s_down) = refs[5:11]
+    (n2, cols, down, dy_rows, act, dgu, g_in, g_down, near, land, low) = refs[11:22]
+    rest = refs[22:]
+    n, reps = sizes
     rows = dy.shape[0]
-    bits = sizes[1].bit_length() - 1
-    kit = Kit(sems, sizes)
-    loads = load_all(kit, [(dgu_h, dgu), (cols_h, cols)])
-    later = load_all(kit, [(act_h, act), (down_h, down)])
+    bits = reps.bit_length() - 1
+    kit = Kit(rest[-1], sizes)
+    loads = load_all(kit, [(n2_h, n2), (cols_h, cols)])
+    later = load_all(kit, [(down_h, down)])
+
+    def chunk(d):
+        return pl.ds(d * 2 * rows, 2 * rows)
+
     kit.barrier()
-    t_in = kit.scatter_rep(
-        column_blocks(g_in), land_in(rest[: 2 * bits]), put_half(s_in), rest[4 * bits : 4 * bits + 2]
-    )
-    next(t_in)
+    line_dy = kit.gather_line(dy, dy_full, rows)
+    next(line_dy)
+    wait_all(loads)
+    for d in range(kit.chips):
+        gated(n2, cols, chunk(d), act, dgu)
+        if d > 0:
+            next(line_dy)
+    finish(line_dy)
+    wait_all(later + load_all(kit, [(dy_full, dy_rows)]))
+    rows_tiles(act, dy_rows, g_down, 256)
     t_down = kit.scatter_rep(
-        column_blocks(g_down), land_in(rest[2 * bits : 4 * bits]), put_half(s_down), rest[4 * bits + 2 : 4 * bits + 4]
+        column_blocks(g_down.reshape(reps, g_down.shape[0] // reps, g_down.shape[1])),
+        land_in(rest[4 * bits : 6 * bits]),
+        put_half(s_down),
     )
     next(t_down)
 
     def first(d):
-        times_tiles(dgu, pl.ds(d * 2 * rows, 2 * rows), cols, dn2, True, 256)
-
-    wait_all(loads)
-    total = kit.scatter_line(dn2, resid, rows, near, land, first)
-    next(total)
-    wait_all(later)
+        gated_back(dy_rows, down, chunk(d), dgu)
+        times_tiles(dgu, chunk(d), cols, dy_rows, True, 256)
+
+    total = kit.scatter_line(dy_rows, resid, rows, near, land, first)
+    next(total)
+    next(total)
+    units = act.shape[1]
+    blocks = g_in.reshape(n, reps, g_in.shape[0] // (n * reps), 2 * units)
+    parts_in = []
+    for g in range(2):
+        window = pl.ds(g * units, units)
+        rows_tiles(n2, dgu, g_in, 256, window)
+        if g == 0:
+            next(t_down)
+        part = kit.scatter_rep(
+            column_blocks(blocks.at[:, :, :, window]),
+            land_in(rest[2 * g * bits : 2 * (g + 1) * bits]),
+            put_half(s_in.at[:, :, window]),
+        )
+        next(part)
+        parts_in.append(part)
+        if g == 0:
+            next(total)
+    next(total)
     for d in range(kit.chips):
+        times_tiles(act, chunk(d), down, n2, False, 256)
+    for _ in range(kit.chips - 3):
         next(total)
-        times_tiles(act, pl.ds(d * 2 * rows, 2 * rows), down, out, False, 256)
+    store = pltpu.make_async_copy(n2, branch_h, kit.sem())
+    store.start()
     next(total)
 
     def body(at):
@@ -780,34 +848,35 @@
     each(resid, body)
     line = kit.gather_line(low, full, rows)
     next(line)
-    finish_in_turn([line, t_in, t_down, total])
-
-
-def back(sizes, dgu, in_cols, act, w_down, hidden, dy, g_in, g_down):
+    finish_in_turn([parts_in[0], line, parts_in[1], t_down, total])
+    store.wait()
+
+
+def back(sizes, n2_full, in_cols, w_down, hidden, dy):
     n, reps = sizes
     rows, width = dy.shape
-    g_in = g_in.reshape(n, reps, g_in.shape[0] // (n * reps), g_in.shape[1])
-    g_down = g_down.reshape(reps, g_down.shape[0] // reps, g_down.shape[1])
-    own = [(a, ANY) for a in (dgu, in_cols, act, w_down)]
+    units = w_down.shape[0]
+    g_in = (n, reps, width // (n * reps), 2 * units)
+    g_down = (reps, units // reps, width)
+    big = lambda *shape: VMEM(shape, BF16)
     return call(
         functools.partial(back_kernel, sizes),
-        own + [(hidden, VMEM), (dy, VMEM), (g_in, ANY), (g_down, ANY)],
+        [(n2_full, ANY), (in_cols, ANY), (w_down, ANY), (hidden, VMEM), (dy, VMEM)],
         [
             ((rows, width), F32, VMEM),
-            ((n * rows, width), BF16, VMEM),
             ((n * rows, width), BF16, ANY),
-            ((n,) + g_in.shape[2:], BF16, VMEM),
-            (g_down.shape[1:], BF16, VMEM),
+            ((n * rows, width), BF16, ANY),
+            ((n * rows, width), BF16, ANY),
+            ((n,) + g_in[2:], BF16, VMEM),
+            (g_down[1:], BF16, VMEM),
         ],
-        [VMEM(a.shape, a.dtype) for a, _ in own]
-        + [VMEM((n * rows, width), BF16)]
+        [big(n * rows, width), big(width, 2 * units), big(units, width), big(n * rows, width)]
+        + [big(n * rows, units), big(n * rows, 2 * units), big(width, 2 * units), big(units, width)]
         + line_lands(n, rows, width)
-        + [VMEM((rows, width), BF16)]
-        + lands_of(g_in.shape, reps)
-        + lands_of(g_down.shape, reps)
-        + own_stages(g_in.shape)
-        + own_stages(g_down.shape),
-        20 * n, 3, "back",
+        + [big(rows, width)]
+        + lands_of(g_in[:3] + (units,), reps) * 2
+        + lands_of(g_down, reps),
+        28 * n, 3, "back",
     )
 
 
@@ -819,7 +888,7 @@
 
     def zero(at):
         for acc in (acc_q, acc_k, acc_v):
-            acc[at] = jnp.zeros((16, own), F32)
+            acc[at] = jnp.zeros_like(acc[at])
 
     each(acc_q, zero)
     for head in range(heads):
@@ -868,10 +937,10 @@
     lax.fori_loop(0, slot // size, step, 0)
 
 
-def rows_tiles(left, right, out, tile):
+def rows_tiles(left, right, out, tile, window=slice(None)):
     def step(t, carry):
         cols = pl.ds(pl.multiple_of(t * tile, tile), tile)
-        out[cols, :] = over_rows(left[:, cols], right[...]).astype(BF16)
+        out[cols, window] = over_rows(left[:, cols], right[:, window]).astype(BF16)
         return carry
 
     lax.fori_loop(0, left.shape[1] // tile, step, 0)
@@ -899,8 +968,9 @@
     own_down = pltpu.make_async_copy(s_down, o_down.at[kit.rep], kit.sem())
     own_down.start()
     kit.barrier()
-    move_in = unshard(kit, s_in, o_in, 2)
-    next(move_in)
+    moves_in = [unshard(kit, s_in, o_in, 2, g) for g in range(2)]
+    for move in moves_in:
+        next(move)
     own_down.wait()
     spread_down = kit.gather_rep(column_blocks(o_down))
     next(spread_down)
@@ -937,9 +1007,6 @@
 
     total = kit.scatter_line(dn1, total_out, rows, near, land, first)
     next(total)
-    next(move_in)
-    spread_in = kit.gather_rep(column_blocks(o_in))
-    next(spread_in)
     next(total)
     rows_tiles(att_low, dres, g_out, 128)
     t_out = kit.scatter_rep(
@@ -948,15 +1015,24 @@
         put_half(s_out),
     )
     next(t_out)
+    units = o_in.shape[2] // 2
+    spreads = []
+    for g in range(2):
+        next(moves_in[g])
+        spread = kit.gather_rep(column_blocks(o_in.at[:, :, pl.ds(g * units, units)]))
+        next(spread)
+        spreads.append(spread)
     next(total)
     next(t_qkv)
-    for _ in range(kit.chips - 2):
-        next(total)
+    next(total)
+    next(spreads[0])
     for _ in range(bits - 1):
         next(t_qkv)
     move_qkv = unshard(kit, s_qkv, o_qkv, 3)
     next(move_qkv)
-    next(spread_in)
+    for _ in range(kit.chips - 3):
+        next(total)
+    next(spreads[1])
     for _ in range(bits):
         next(t_out)
     own_out = pltpu.make_async_copy(s_out, o_out.at[kit.rep], kit.sem())
@@ -971,7 +1047,12 @@
     next(move_qkv)
     spread_qkv = kit.gather_rep(column_blocks(o_qkv))
     next(spread_qkv)
-    finish_in_turn([other, spread_qkv, spread_out, spread_in, total, spread_down, move_in, move_qkv, t_qkv, t_out])
+    for _ in range(kit.chips):
+        next(other)
+    finish_in_turn(
+        [spread_qkv, spread_out, other, total, spread_down]
+        + spreads + moves_in + [move_qkv, t_qkv, t_out]
+    )
 
 
 def end(sizes, length, dres, w_out, qkv, att, att_low, lse, cosine, sine, cols, n1, part, s_in, s_down):
@@ -1025,26 +1106,12 @@
     dy_low = dy_rows.astype(BF16)
     turn_cos = jnp.concatenate([cosine, cosine], axis=1)
     turn_sin = jnp.concatenate([sine, -sine], axis=1)
-    hidden_in, qkv_low, attended, att_low, level, n1_full, n2_full, dy_full, qkv_cols, in_cols = front(
-        sizes, lengths, tokens[0], dy_low, w_qkv, w_in, w_out, turn_cos, turn_sin
-    )
-    gate_up = dot(n2_full, in_cols)
-    units = gate_up.shape[1] // 2
-    gate = gate_up[:, :units]
-    upper = gate_up[:, units:]
-    sigma = jax.nn.sigmoid(gate)
-    silu_gate = gate * sigma
-    act_low = (silu_gate * upper).astype(BF16)
-    d_hidden = times_transpose(dy_full, w_down)
-    d_gate = d_hidden * upper * sigma * (1.0 + gate * (1.0 - sigma))
-    d_up = d_hidden * silu_gate
-    dgu_low = jnp.concatenate([d_gate, d_up], axis=1).astype(BF16)
-    grad_down = over_rows(act_low, dy_full).astype(BF16)
-    grad_in = over_rows(n2_full, dgu_low).astype(BF16)
-    d_resid, branch_partial, dres_full, sum_in, sum_down = back(
-        sizes, dgu_low, in_cols, act_low, w_down, hidden_in, dy_low, grad_in, grad_down
-    )
-
+    hidden_in, qkv_low, attended, att_low, level, n1_full, n2_full, qkv_cols, in_cols = front(
+        sizes, lengths, tokens[0], w_qkv, w_in, w_out, turn_cos, turn_sin
+    )
+    d_resid, branch_partial, _, dres_full, sum_in, sum_down = back(
+        sizes, n2_full, in_cols, w_down, hidden_in, dy_low
+    )
     d_norm1, branch, all_in, all_down, all_qkv, all_out = end(
         sizes,
         lengths,

time: 659 us -> 638 us (0.968)
  matrix products: 41.4 us -> 0 us
  Pallas kernels: 577 us -> 603 us
    dot_general x4 -> x0, matrix products: 41.4 us -> none  [the longest x2 18 us: over_rows(): lax.dot_general(left, right, (((0,), (0,)), ((), ())), preferred_element_...]
    pallas_call x3, Pallas kernels: 577 us -> 603 us  [call(): pl.pallas_call(body, out_shape=[jax.ShapeDtypeStruct(s, d) for s, d, _ in...]
where the time goes in v5:
time: 638 us; the launch traced here: 635 us
  Pallas kernels  603 us (95%)
  other arithmetic  29.9 us (5%)
    pallas_call x3, Pallas kernels, call(): pl.pallas_call(body, out_shape=[jax.ShapeDtypeStruct(s, d) for s, d, _ in...  603 us
    convert_element_type x4, other arithmetic, end(): o.reshape(-1, o.shape[-1]).astype(F32)  21.7 us

profile of v5, /device:TPU:8, one launch (start us, length us, event | category | flops | bytes accessed | tf_op | source)
XLA Modules:
  0.0 635.3 jit_solution(10463269709872933029)
XLA Ops:
  0.7 1.9 multiply_sine_fusion
  2.6 1.3 pad_maximum_fusion
  4.5 203.5 %front.1 = (f32[128,2048]{1,0:T(8,128)}, bf16[1024,768]{1,0:T(8,128)(2,1)}, f32[1024,256]{1,0:T(8,128)}, bf16[1024,256]{1,0:T(8,128)(2,1)}, f32[1024,128]{1,0:T(...) custom-call(s32[1]{0:T(128)} %copy.13.refs_0_, ...), custom_call_target="tpu_custom_call" | custom-call | tf_op jit(solution)/shard_map/front/pallas_call | solution.py:512
  208.1 0.0 copy-start.8
  208.1 0.5 copy-done.8
  208.6 2.0 fusion.10.refs_4_
  210.6 172.3 %back.1 = (f32[128,2048]{1,0:T(8,128)}, bf16[1024,2048]{1,0:T(8,128)(2,1)}, bf16[1024,2048]{1,0:T(8,128)(2,1)}, bf16[1024,2048]{1,0:T(8,128)(2,1)}, bf16[8,64,20...) custom-call(bf16[1024,2048]{1,0:T(8,128)(2,1)} %get-tuple-element.27.refs_0_, bf16[2048,2048]{1,0:T(8,128)(2,1)} %bitcast.29, ...), custom_call_target="tpu_custom_call" | custom-call | tf_op jit(solution)/shard_map/back/pallas_call | solution.py:512
  382.9 227.5 %end.1 = (f32[128,2048]{1,0:T(8,128)}, f32[128,2048]{1,0:T(8,128)}, bf16[4,64,16384]{2,1,0:T(8,128)(2,1)}, bf16[4,256,2048]{2,1,0:T(8,128)(2,1)}, bf16[4,64,6144...) custom-call(s32[1]{0:T(128)} %copy.13.refs_0_, bf16[1024,2048]{1,0:T(8,128)(2,1)} %get-tuple-element.29.refs_1_, ...), custom_call_target="tpu_custom_call" | custom-call | tf_op jit(solution)/shard_map/end/pallas_call | solution.py:512
  610.4 0.0 copy-start.1
  610.5 11.7 %bitcast_convert_fusion = f32[256,16384]{1,0:T(8,128)} fusion(bf16[4,64,16384]{2,1,0:T(8,128)(2,1)} %get-tuple-element.44), kind=kLoop, calls=%fused_computation | loop fusion | flops 4194304 | bytes 25165824 | tf_op jit(solution)/shard_map/convert_element_type | solution.py:1089
  622.1 0.0 copy-done.1
  622.2 0.0 copy-start.4
  622.2 4.7 bitcast_convert_fusion.1
  626.9 0.0 copy-done.4
  626.9 0.0 copy-start.5
  626.9 0.0 copy-start
  626.9 3.7 bitcast_convert_fusion.2
  630.6 0.0 copy-start.3
  630.6 0.0 copy-start.7
  630.6 0.0 copy-done.5
  630.6 0.0 copy-start.2
  630.6 0.0 copy-start.6
  630.6 0.0 copy-start.9
  630.6 1.6 bitcast_convert_fusion.3
  632.2 0.0 copy-done
  632.2 0.2 convert_reduce_fusion
  632.4 0.3 fusion.9
  632.7 0.0 copy-done.3
  632.7 0.3 fusion.14
  633.1 0.0 copy-done.7
  633.1 1.3 fusion.12
  634.3 0.0 copy-done.2
  634.3 0.0 copy-done.6
  634.3 0.0 copy-done.9
  634.3 0.9 fusion.11
  (7 shorter events, 0.0 us)
Async XLA Ops:
  208.1 0.5 copy-start.8
  610.4 11.7 %copy-start.1 = (bf16[4,256,2048]{2,1,0:T(8,128)(2,1)S(1)}, bf16[4,256,2048]{2,1,0:T(8,128)(2,1)}, u32[]{:S(2)}) copy-start(bf16[4,256,2048]{2,1,0:T(8,128)(2,1)} %get-tuple-element.45) | copy-start | bytes 12582916
  622.2 4.8 copy-start.4
  626.9 3.7 copy-start.5
  626.9 5.3 copy-start
  630.6 2.1 copy-start.3
  630.6 2.5 copy-start.7
  630.6 3.8 copy-start.2
  630.6 3.8 copy-start.6
  630.6 3.7 copy-start.9

commit v6 on v5

--- a/solution.py
+++ b/solution.py
@@ -1015,6 +1015,9 @@
         put_half(s_out),
     )
     next(t_out)
+    next(total)
+    next(t_qkv)
+    next(t_out)
     units = o_in.shape[2] // 2
     spreads = []
     for g in range(2):
@@ -1023,30 +1026,28 @@
         next(spread)
         spreads.append(spread)
     next(total)
-    next(t_qkv)
-    next(total)
-    next(spreads[0])
     for _ in range(bits - 1):
         next(t_qkv)
     move_qkv = unshard(kit, s_qkv, o_qkv, 3)
     next(move_qkv)
-    for _ in range(kit.chips - 3):
-        next(total)
-    next(spreads[1])
-    for _ in range(bits):
+    for _ in range(bits - 1):
         next(t_out)
     own_out = pltpu.make_async_copy(s_out, o_out.at[kit.rep], kit.sem())
     own_out.start()
+    for _ in range(kit.chips - 3):
+        next(total)
     other = kit.scatter_line(part_h, branch, rows, near_b, land_b, stage=stage)
     next(other)
     next(total)
+    next(spreads[0])
     next(other)
     own_out.wait()
-    spread_out = kit.gather_rep(column_blocks(o_out))
-    next(spread_out)
     next(move_qkv)
     spread_qkv = kit.gather_rep(column_blocks(o_qkv))
     next(spread_qkv)
+    spread_out = kit.gather_rep(column_blocks(o_out))
+    next(spread_out)
+    next(spreads[1])
     for _ in range(kit.chips):
         next(other)
     finish_in_turn(

time: 638 us -> 603 us (0.945)
  Pallas kernels: 603 us -> 571 us
    pallas_call x3, Pallas kernels: 603 us -> 571 us  [call(): pl.pallas_call(body, out_shape=[jax.ShapeDtypeStruct(s, d) for s, d, _ in...]
where the time goes in v6:
time: 603 us
  Pallas kernels  571 us (95%)
  other arithmetic  29.9 us (5%)
    pallas_call x3, Pallas kernels, call(): pl.pallas_call(body, out_shape=[jax.ShapeDtypeStruct(s, d) for s, d, _ in...  571 us
    convert_element_type x4, other arithmetic, end(): o.reshape(-1, o.shape[-1]).astype(F32)  21.7 us

profile of v6, /device:TPU:8, one launch (start us, length us, event | category | flops | bytes accessed | tf_op | source)
XLA Modules:
  0.0 602.6 jit_solution(10761857298948505208)
XLA Ops:
  0.7 1.9 multiply_sine_fusion
  2.6 1.3 pad_maximum_fusion
  4.5 203.5 %front.1 = (f32[128,2048]{1,0:T(8,128)}, bf16[1024,768]{1,0:T(8,128)(2,1)}, f32[1024,256]{1,0:T(8,128)}, bf16[1024,256]{1,0:T(8,128)(2,1)}, f32[1024,128]{1,0:T(...) custom-call(s32[1]{0:T(128)} %copy.13.refs_0_, ...), custom_call_target="tpu_custom_call" | custom-call | tf_op jit(solution)/shard_map/front/pallas_call | solution.py:512
  208.1 0.0 copy-start.8
  208.1 0.5 copy-done.8
  208.6 2.0 fusion.10.refs_4_
  210.6 172.3 %back.1 = (f32[128,2048]{1,0:T(8,128)}, bf16[1024,2048]{1,0:T(8,128)(2,1)}, bf16[1024,2048]{1,0:T(8,128)(2,1)}, bf16[1024,2048]{1,0:T(8,128)(2,1)}, bf16[8,64,20...) custom-call(bf16[1024,2048]{1,0:T(8,128)(2,1)} %get-tuple-element.27.refs_0_, bf16[2048,2048]{1,0:T(8,128)(2,1)} %bitcast.29, ...), custom_call_target="tpu_custom_call" | custom-call | tf_op jit(solution)/shard_map/back/pallas_call | solution.py:512
  382.9 194.9 %end.1 = (f32[128,2048]{1,0:T(8,128)}, f32[128,2048]{1,0:T(8,128)}, bf16[4,64,16384]{2,1,0:T(8,128)(2,1)}, bf16[4,256,2048]{2,1,0:T(8,128)(2,1)}, bf16[4,64,6144...) custom-call(s32[1]{0:T(128)} %copy.13.refs_0_, bf16[1024,2048]{1,0:T(8,128)(2,1)} %get-tuple-element.29.refs_1_, ...), custom_call_target="tpu_custom_call" | custom-call | tf_op jit(solution)/shard_map/end/pallas_call | solution.py:512
  577.8 0.0 copy-start.1
  577.8 11.7 %bitcast_convert_fusion = f32[256,16384]{1,0:T(8,128)} fusion(bf16[4,64,16384]{2,1,0:T(8,128)(2,1)} %get-tuple-element.44), kind=kLoop, calls=%fused_computation | loop fusion | flops 4194304 | bytes 25165824 | tf_op jit(solution)/shard_map/convert_element_type | solution.py:1090
  589.5 0.0 copy-done.1
  589.5 0.0 copy-start.4
  589.5 4.7 bitcast_convert_fusion.1
  594.2 0.0 copy-done.4
  594.2 0.0 copy-start.5
  594.2 0.0 copy-start
  594.2 3.7 bitcast_convert_fusion.2
  597.9 0.0 copy-start.3
  597.9 0.0 copy-start.7
  597.9 0.0 copy-done.5
  597.9 0.0 copy-start.2
  597.9 0.0 copy-start.6
  597.9 0.0 copy-start.9
  597.9 1.6 bitcast_convert_fusion.3
  599.6 0.0 copy-done
  599.6 0.2 convert_reduce_fusion
  599.7 0.3 fusion.9
  600.0 0.0 copy-done.3
  600.0 0.3 fusion.14
  600.4 0.0 copy-done.7
  600.4 1.3 fusion.12
  601.7 0.0 copy-done.2
  601.7 0.0 copy-done.6
  601.7 0.0 copy-done.9
  601.7 0.9 fusion.11
  (7 shorter events, 0.0 us)
Async XLA Ops:
  208.1 0.5 copy-start.8
  577.8 11.7 %copy-start.1 = (bf16[4,256,2048]{2,1,0:T(8,128)(2,1)S(1)}, bf16[4,256,2048]{2,1,0:T(8,128)(2,1)}, u32[]{:S(2)}) copy-start(bf16[4,256,2048]{2,1,0:T(8,128)(2,1)} %get-tuple-element.45) | copy-start | bytes 12582916
  589.5 4.8 copy-start.4
  594.2 3.7 copy-start.5
  594.2 5.3 copy-start
  597.9 2.1 copy-start.3
  597.9 2.5 copy-start.7
  597.9 3.8 copy-start.2
  597.9 3.8 copy-start.6
  597.9 3.7 copy-start.9

commit v7 on v6

--- a/solution.py
+++ b/solution.py
@@ -701,6 +701,8 @@
     norm_rows(n_low.at[1], hidden)
     gather = kit.gather_line(n_low.at[1], n2_full, rows)
     next(gather)
+    for _ in range(kit.chips - 1):
+        next(gather)
     finish_in_turn([gather, spread_in, move_in, total])
 
 
@@ -816,9 +818,9 @@
     parts_in = []
     for g in range(2):
         window = pl.ds(g * units, units)
-        rows_tiles(n2, dgu, g_in, 256, window)
         if g == 0:
             next(t_down)
+        rows_tiles(n2, dgu, g_in, 256, window)
         part = kit.scatter_rep(
             column_blocks(blocks.at[:, :, :, window]),
             land_in(rest[2 * g * bits : 2 * (g + 1) * bits]),
@@ -848,7 +850,13 @@
     each(resid, body)
     line = kit.gather_line(low, full, rows)
     next(line)
-    finish_in_turn([parts_in[0], line, parts_in[1], t_down, total])
+    next(parts_in[0])
+    next(line)
+    next(line)
+    next(parts_in[1])
+    for _ in range(kit.chips - 3):
+        next(line)
+    finish_in_turn([parts_in[0], t_down, line, parts_in[1], total])
     store.wait()
 
 

time: 603 us -> 596 us (0.988)
  Pallas kernels: 571 us -> 563 us
    pallas_call x3, Pallas kernels: 571 us -> 563 us  [call(): pl.pallas_call(body, out_shape=[jax.ShapeDtypeStruct(s, d) for s, d, _ in...]
where the time goes in v7:
time: 596 us; the launch traced here: 595 us
  Pallas kernels  563 us (94%)
  other arithmetic  29.9 us (5%)
    pallas_call x3, Pallas kernels, call(): pl.pallas_call(body, out_shape=[jax.ShapeDtypeStruct(s, d) for s, d, _ in...  563 us
    convert_element_type x4, other arithmetic, end(): o.reshape(-1, o.shape[-1]).astype(F32)  21.7 us

profile of v7, /device:TPU:8, one launch (start us, length us, event | category | flops | bytes accessed | tf_op | source)
XLA Modules:
  0.0 595.3 jit_solution(18256431486946236409)
XLA Ops:
  0.7 1.9 multiply_sine_fusion
  2.6 1.3 pad_maximum_fusion
  4.5 195.6 %front.1 = (f32[128,2048]{1,0:T(8,128)}, bf16[1024,768]{1,0:T(8,128)(2,1)}, f32[1024,256]{1,0:T(8,128)}, bf16[1024,256]{1,0:T(8,128)(2,1)}, f32[1024,128]{1,0:T(...) custom-call(s32[1]{0:T(128)} %copy.13.refs_0_, ...), custom_call_target="tpu_custom_call" | custom-call | tf_op jit(solution)/shard_map/front/pallas_call | solution.py:512
  200.1 0.0 copy-start.8
  200.1 0.5 copy-done.8
  200.6 2.0 fusion.10.refs_4_
  202.6 174.5 %back.1 = (f32[128,2048]{1,0:T(8,128)}, bf16[1024,2048]{1,0:T(8,128)(2,1)}, bf16[1024,2048]{1,0:T(8,128)(2,1)}, bf16[1024,2048]{1,0:T(8,128)(2,1)}, bf16[8,64,20...) custom-call(bf16[1024,2048]{1,0:T(8,128)(2,1)} %get-tuple-element.27.refs_0_, bf16[2048,2048]{1,0:T(8,128)(2,1)} %bitcast.29, ...), custom_call_target="tpu_custom_call" | custom-call | tf_op jit(solution)/shard_map/back/pallas_call | solution.py:512
  377.1 193.4 %end.1 = (f32[128,2048]{1,0:T(8,128)}, f32[128,2048]{1,0:T(8,128)}, bf16[4,64,16384]{2,1,0:T(8,128)(2,1)}, bf16[4,256,2048]{2,1,0:T(8,128)(2,1)}, bf16[4,64,6144...) custom-call(s32[1]{0:T(128)} %copy.13.refs_0_, bf16[1024,2048]{1,0:T(8,128)(2,1)} %get-tuple-element.29.refs_1_, ...), custom_call_target="tpu_custom_call" | custom-call | tf_op jit(solution)/shard_map/end/pallas_call | solution.py:512
  570.5 0.0 copy-start.1
  570.5 11.7 %bitcast_convert_fusion = f32[256,16384]{1,0:T(8,128)} fusion(bf16[4,64,16384]{2,1,0:T(8,128)(2,1)} %get-tuple-element.44), kind=kLoop, calls=%fused_computation | loop fusion | flops 4194304 | bytes 25165824 | tf_op jit(solution)/shard_map/convert_element_type | solution.py:1098
  582.2 0.0 copy-done.1
  582.2 0.0 copy-start.4
  582.2 4.7 bitcast_convert_fusion.1
  586.9 0.0 copy-done.4
  586.9 0.0 copy-start.5
  586.9 0.0 copy-start
  586.9 3.7 bitcast_convert_fusion.2
  590.6 0.0 copy-start.3
  590.6 0.0 copy-start.7
  590.6 0.0 copy-done.5
  590.6 0.0 copy-start.2
  590.6 0.0 copy-start.6
  590.6 0.0 copy-start.9
  590.6 1.6 bitcast_convert_fusion.3
  592.3 0.0 copy-done
  592.3 0.2 convert_reduce_fusion
  592.4 0.3 fusion.9
  592.7 0.0 copy-done.3
  592.7 0.3 fusion.14
  593.1 0.0 copy-done.7
  593.1 1.3 fusion.12
  594.4 0.0 copy-done.2
  594.4 0.0 copy-done.6
  594.4 0.0 copy-done.9
  594.4 0.9 fusion.11
  (7 shorter events, 0.0 us)
Async XLA Ops:
  200.1 0.5 copy-start.8
  570.5 11.7 %copy-start.1 = (bf16[4,256,2048]{2,1,0:T(8,128)(2,1)S(1)}, bf16[4,256,2048]{2,1,0:T(8,128)(2,1)}, u32[]{:S(2)}) copy-start(bf16[4,256,2048]{2,1,0:T(8,128)(2,1)} %get-tuple-element.45) | copy-start | bytes 12582916
  582.2 4.8 copy-start.4
  586.9 3.7 copy-start.5
  586.9 5.3 copy-start
  590.6 2.1 copy-start.3
  590.6 2.5 copy-start.7
  590.6 3.8 copy-start.2
  590.6 3.8 copy-start.6
  590.6 3.7 copy-start.9

commit v8 on v7

--- a/solution.py
+++ b/solution.py
@@ -648,9 +648,9 @@
 
 
 def front_kernel(sizes, *refs):
-    (length, x, w_qkv, w_in, w_out_h, cos_h, sin_h) = refs[:7]
-    (hidden, qkv, att, att_low, lse, n1_full, n2_full, qkv_cols, in_cols) = refs[7:16]
-    (n_low, n1, cols, w_out, cosine, sine, partial, near, land, stage, stage_in, sems) = refs[16:]
+    (length, x, cot, w_qkv, w_in, w_out_h, cos_h, sin_h) = refs[:8]
+    (hidden, qkv, att, att_low, lse, dy, n1_full, n2_full, qkv_cols, in_cols) = refs[8:18]
+    (n_low, n1, cols, w_out, cosine, sine, partial, near, land, stage, stage_in, sems) = refs[18:]
     kit = Kit(sems, sizes)
     rows = x.shape[0]
     loads = load_all(kit, [(w_out_h, w_out), (cos_h, cosine), (sin_h, sine)])
@@ -668,6 +668,13 @@
     next(move)
     spread = kit.gather_rep(column_blocks(qkv_cols))
     next(spread)
+
+    def mask(at):
+        start, size = at[0].start, at[0].size
+        place = kit.me * rows + start + lax.broadcasted_iota(jnp.int32, (size, cot.shape[1]), 0)
+        dy[at] = jnp.where(place < length[0], cot[at].astype(F32), 0.0).astype(BF16)
+
+    each(dy, mask)
     finish_in_turn([line, spread, move])
     move_in = reshard(kit, w_in, in_cols, stage_in, 2)
     next(move_in)
@@ -706,7 +713,7 @@
     finish_in_turn([gather, spread_in, move_in, total])
 
 
-def front(sizes, length, x, w_qkv, w_in, w_out, cosine, sine):
+def front(sizes, length, x, cot, w_qkv, w_in, w_out, cosine, sine):
     n, reps = sizes
     rows, width = x.shape
     slot = n * rows
@@ -717,7 +724,7 @@
     wide = lambda *shape: VMEM(shape, F32)
     outs = call(
         functools.partial(front_kernel, sizes),
-        [(length, pltpu.SMEM), (x, VMEM)]
+        [(length, pltpu.SMEM), (x, VMEM), (cot, VMEM)]
         + [(a, ANY) for a in (w_qkv, w_in, w_out, cosine, sine)],
         [
             ((rows, width), F32, VMEM),
@@ -725,6 +732,7 @@
             ((slot, own), F32, VMEM),
             ((slot, own), BF16, VMEM),
             ((slot, 128), F32, VMEM),
+            ((rows, width), BF16, VMEM),
             ((slot, width), BF16, ANY),
             ((slot, width), BF16, ANY),
             ((n, reps, part, own_qkv), BF16, ANY),
@@ -736,7 +744,7 @@
         + [big(part, own_qkv), big(part, own_in)],
         64 * n, 1, "front",
     )
-    return list(outs[:7]) + [o.reshape(n * depth, -1) for o in outs[7:]]
+    return list(outs[:8]) + [o.reshape(n * depth, -1) for o in outs[8:]]
 
 
 def gated(n2, cols, at, act, slopes):
@@ -1111,12 +1119,10 @@
     cosine, sine = rotary_tables(positions, head_dim)
 
     sizes = (n, lax.axis_size("rep"))
-    dy_rows = valid * cotangent[0].astype(F32)
-    dy_low = dy_rows.astype(BF16)
     turn_cos = jnp.concatenate([cosine, cosine], axis=1)
     turn_sin = jnp.concatenate([sine, -sine], axis=1)
-    hidden_in, qkv_low, attended, att_low, level, n1_full, n2_full, qkv_cols, in_cols = front(
-        sizes, lengths, tokens[0], w_qkv, w_in, w_out, turn_cos, turn_sin
+    hidden_in, qkv_low, attended, att_low, level, dy_low, n1_full, n2_full, qkv_cols, in_cols = front(
+        sizes, lengths, tokens[0], cotangent[0], w_qkv, w_in, w_out, turn_cos, turn_sin
     )
     d_resid, branch_partial, _, dres_full, sum_in, sum_down = back(
         sizes, n2_full, in_cols, w_down, hidden_in, dy_low

time: 596 us -> 594 us (level)
  no operation moved by 1% of the time
where the time goes in v8:
time: 594 us; the launch traced here: 593 us
  Pallas kernels  564 us (95%)
  other arithmetic  27.9 us (5%)
    pallas_call x3, Pallas kernels, call(): pl.pallas_call(body, out_shape=[jax.ShapeDtypeStruct(s, d) for s, d, _ in...  564 us
    convert_element_type x4, other arithmetic, end(): o.reshape(-1, o.shape[-1]).astype(F32)  21.7 us

profile of v8, /device:TPU:8, one launch (start us, length us, event | category | flops | bytes accessed | tf_op | source)
XLA Modules:
  0.0 593.2 jit_solution(17322397132715621083)
XLA Ops:
  0.7 1.9 multiply_sine_fusion
  2.6 1.3 pad_maximum_fusion
  4.5 195.9 %front.1 = (f32[128,2048]{1,0:T(8,128)}, bf16[1024,768]{1,0:T(8,128)(2,1)}, f32[1024,256]{1,0:T(8,128)}, bf16[1024,256]{1,0:T(8,128)(2,1)}, f32[1024,128]{1,0:T(...) custom-call(s32[1]{0:T(128)} %copy.13.refs_0_, ...), custom_call_target="tpu_custom_call" | custom-call | tf_op jit(solution)/shard_map/front/pallas_call | solution.py:512
  200.5 174.5 %back.1 = (f32[128,2048]{1,0:T(8,128)}, bf16[1024,2048]{1,0:T(8,128)(2,1)}, bf16[1024,2048]{1,0:T(8,128)(2,1)}, bf16[1024,2048]{1,0:T(8,128)(2,1)}, bf16[8,64,20...) custom-call(bf16[1024,2048]{1,0:T(8,128)(2,1)} %get-tuple-element.28.refs_0_, bf16[2048,2048]{1,0:T(8,128)(2,1)} %bitcast.27, ...), custom_call_target="tpu_custom_call" | custom-call | tf_op jit(solution)/shard_map/back/pallas_call | solution.py:512
  375.0 193.4 %end.1 = (f32[128,2048]{1,0:T(8,128)}, f32[128,2048]{1,0:T(8,128)}, bf16[4,64,16384]{2,1,0:T(8,128)(2,1)}, bf16[4,256,2048]{2,1,0:T(8,128)(2,1)}, bf16[4,64,6144...) custom-call(s32[1]{0:T(128)} %copy.13.refs_0_, bf16[1024,2048]{1,0:T(8,128)(2,1)} %get-tuple-element.31.refs_1_, ...), custom_call_target="tpu_custom_call" | custom-call | tf_op jit(solution)/shard_map/end/pallas_call | solution.py:512
  568.4 0.0 copy-start.1
  568.4 11.7 %bitcast_convert_fusion = f32[256,16384]{1,0:T(8,128)} fusion(bf16[4,64,16384]{2,1,0:T(8,128)(2,1)} %get-tuple-element.46), kind=kLoop, calls=%fused_computation | loop fusion | flops 4194304 | bytes 25165824 | tf_op jit(solution)/shard_map/convert_element_type | solution.py:1106
  580.0 0.0 copy-done.1
  580.1 0.0 copy-start.4
  580.1 4.7 bitcast_convert_fusion.1
  584.8 0.0 copy-done.4
  584.8 0.0 copy-start.5
  584.8 0.0 copy-start
  584.8 3.7 bitcast_convert_fusion.2
  588.5 0.0 copy-start.3
  588.5 0.0 copy-start.7
  588.5 0.0 copy-done.5
  588.5 0.0 copy-start.2
  588.5 0.0 copy-start.6
  588.5 1.6 bitcast_convert_fusion.3
  590.1 0.0 copy-done
  590.1 0.2 convert_reduce_fusion
  590.3 0.3 fusion.9
  590.6 0.0 copy-done.3
  590.6 0.3 fusion.13
  591.0 0.0 copy-done.7
  591.0 1.3 fusion.11
  592.2 0.0 copy-done.2
  592.2 0.0 copy-done.6
  592.2 0.9 fusion.10
  (7 shorter events, 0.0 us)
Async XLA Ops:
  568.4 11.7 %copy-start.1 = (bf16[4,256,2048]{2,1,0:T(8,128)(2,1)S(1)}, bf16[4,256,2048]{2,1,0:T(8,128)(2,1)}, u32[]{:S(2)}) copy-start(bf16[4,256,2048]{2,1,0:T(8,128)(2,1)} %get-tuple-element.47) | copy-start | bytes 12582916
  580.1 4.8 copy-start.4
  584.8 3.7 copy-start.5
  584.8 5.3 copy-start
  588.5 2.1 copy-start.3
  588.5 2.5 copy-start.7
  588.5 3.8 copy-start.2
  588.5 3.8 copy-start.6
